TPU v7x, 128 devices: a whole 4x4x4 slice. The times are simulated.
128 devices in a mesh: rows: 8 (over x, core), cols: 16 (over y, z).
Axes of the slice: x: 4, y: 4, z: 4, core: 2. Of those that a mesh axis runs over, the one named last changes fastest.
Arguments:
- cells: int32 [1024], replicated, may hold values from 0 to 65535, as said below
- gram_slots: float32 [6, 4096, 2048], P(None, 'rows', 'cols'), may hold values from -6 to 6
- diag_inverse: float32 [2, 4096, 4096], P(None, 'rows', 'cols'), may hold values from -1 to 2.1, as said below
- lower_block: float32 [4096, 4096], P('rows', 'cols'), may hold values from -0.09375 to 0.09375
- trail_factor: float32 [4, 2, 4096, 4096], P(None, None, 'rows', 'cols'), may hold values from -0.0625 to 0.0625
Outputs:
- y_panels: float32 [2, 4096, 1024], P(None, 'rows')
- g_trail: float32 [4, 4096, 1024], P(None, 'rows', 'cols')
Inputs may be any that keep to these rules, and one draw needn't show every extreme that they name: Within each aligned run of 64 list positions no column block owns more than 8 cells; one column block owns exactly 8 in every run, and so 128 listed cells in all, and no column block owns more than 128. `diag_inverse`: each matrix is lower triangular with a positive diagonal.
All inputs are finite; a program needn't handle non-finite values.
Results may differ from a plain program's by a relative error of at most 0.00011.
Values sent between devices are 32-bit elements; how exact they have to be, the bound alone decides.
No kernel may reach another device: no remote copies, remote signals or barrier semaphores. Data moves between devices by JAX's collectives and lax.ppermute only.
A program may use at most 128 MiB of HBM per device.

v0:
```python
import functools

import jax
import jax.numpy as jnp
from jax import lax
from jax.experimental import pallas as pl
from jax.experimental.pallas import tpu as pltpu
from jax.sharding import Mesh
from jax.sharding import PartitionSpec as P

NCELL = 65536
ROWS = ("x", "core")
COLS = ("y", "z")
HIGHEST = lax.Precision.HIGHEST
F32 = jnp.float32
BF16 = jnp.bfloat16
SMEM = pl.BlockSpec(memory_space=pltpu.SMEM)


def dot(a, b, dims, precision):
    return lax.dot_general(a, b, (dims, ((), ())), precision=precision, preferred_element_type=F32)


def shift(value, axis, by):
    size = lax.axis_size(axis)
    return lax.ppermute(value, axis, [(i, (i + by) % size) for i in range(size)])


def exchange(value, axes):
    return lax.all_to_all(value, axes, 0, 0, tiled=True)


def spread(value, axes):
    return exchange(jnp.broadcast_to(value[None], (lax.axis_size(axes), *value.shape)), axes)


def split(value):
    high = value.astype(BF16)
    return high, (value - high.astype(F32)).astype(BF16)


def mul(a, b):
    f = lambda u, v: jnp.dot(u, v, preferred_element_type=F32)
    return f(a[0], b[0]) + (f(a[0], b[1]) + f(a[1], b[0]))


def band_rows(ref, lead, at, by, n_z):
    source = lax.rem(at + n_z - by, n_z)
    per = n_z // 2
    quarters = [ref[(*lead, per * lax.rem(source, 2) + i, source // 2)] for i in range(per)]
    return jnp.concatenate(quarters, axis=0)


def product_kernel(n_z, at_ref, matrix_ref, operand_ref, out_ref):
    width = matrix_ref.shape[1] // n_z
    total = None
    for by in range(n_z):
        rows = split(band_rows(operand_ref, (), at_ref[0], by, n_z))
        term = mul(split(matrix_ref[:, by * width : (by + 1) * width]), rows)
        total = term if total is None else total + term
    out_ref[0] = total


def apply_matrix(at_z, matrix, pieces, n_y):
    rows, band = matrix.shape
    slab = pieces.shape[-1]
    return pl.pallas_call(
        functools.partial(product_kernel, pieces.shape[0]),
        grid=(n_y,),
        in_specs=[
            SMEM,
            pl.BlockSpec((rows // n_y, band), lambda i: (i, 0)),
            pl.BlockSpec(pieces.shape, lambda i: (0, 0, 0, 0)),
        ],
        out_specs=pl.BlockSpec((1, rows // n_y, slab), lambda i: (i, 0, 0)),
        out_shape=jax.ShapeDtypeStruct((n_y, rows // n_y, slab), F32),
        cost_estimate=pl.CostEstimate(
            flops=6 * rows * band * slab, bytes_accessed=4 * rows * band, transcendentals=0
        ),
    )(at_z, matrix, pieces)


def trail_kernel(n_z, n_x, with_gram, one_list, at_ref, *refs):
    lists = refs[:1] if one_list else refs[:n_x]
    refs = refs[len(lists) :]
    factor = refs[: 2 * n_z]
    refs = refs[2 * n_z :]
    gram = refs[: 2 * n_z] if with_gram else ()
    start_ref, out_ref = refs[len(gram) :]
    at_x, at_z = at_ref[0], at_ref[1]
    blocks, quarter, _ = factor[0].shape
    slab = out_ref.shape[-1]
    half = blocks * quarter
    operands = []
    for by in range(n_z):
        cols = [
            band_rows(lists[0], (i,), at_z, by, n_z) if one_list else band_rows(lists[i], (), at_z, by, n_z)
            for i in range(n_x)
        ]
        operands.append(split(jnp.concatenate(cols, axis=1)))
    for side in range(2):
        total = None
        for by in range(n_z):
            piece = factor[side * n_z + by][...]
            term = mul(split(piece.reshape(half, piece.shape[-1])), operands[by])
            total = term if total is None else total + term
        placed = None
        for by in range(n_z if with_gram else 0):
            piece = gram[side * n_z + by][...]
            high, low = split(piece.reshape(half, piece.shape[-1]))
            chosen = start_ref[lax.rem(at_z + n_z - by, n_z)]
            term = jnp.dot(high, chosen, preferred_element_type=F32) + jnp.dot(low, chosen, preferred_element_type=F32)
            placed = term if placed is None else placed + term
        for i in range(n_x):
            at = i if one_list else lax.rem(at_x + i, n_x)
            mine = slice(i * slab, (i + 1) * slab)
            into = pl.ds(side * half, half)
            first = placed[:, mine] if with_gram else start_ref[at, into, :]
            out_ref[at, into, :] = first - total[:, mine]


def apply_trail(where, own, other, which, lists, start, with_gram, n_x, slots):
    n_z = len(own)
    blocks, quarter, depth = own[0].shape
    width = (depth - slots) // 2
    slab = lists[0].shape[-1]
    whole = lambda v: pl.BlockSpec(v.shape, lambda *_: (0,) * v.ndim)
    part = pl.BlockSpec((blocks, quarter, width), lambda *_: (0, 0, which))
    pieces = [*own, *other]
    specs = [SMEM] + [whole(v) for v in lists] + [part] * (2 * n_z)
    args = [where, *lists, *pieces]
    if with_gram:
        specs += [pl.BlockSpec((blocks, quarter, slots), lambda *_: (0, 0, 2 * width // slots))] * (2 * n_z)
        args += pieces
    rows = 2 * blocks * quarter
    return pl.pallas_call(
        functools.partial(trail_kernel, n_z, n_x, with_gram, len(lists) == 1),
        grid=(1,),
        in_specs=specs + [whole(start)],
        out_specs=pl.BlockSpec((n_x, rows, slab), lambda *_: (0, 0, 0)),
        out_shape=jax.ShapeDtypeStruct((n_x, rows, slab), F32),
        cost_estimate=pl.CostEstimate(
            flops=6 * rows * n_z * width * n_x * slab, bytes_accessed=12 * 2**20, transcendentals=0
        ),
    )(*args, start)


def rows_kernel(first_ref, second_ref, out_ref):
    n_y, wide = first_ref.shape[0], first_ref.shape[-1]
    for i in range(n_y):
        out_ref[0, :, i * wide : (i + 1) * wide] = first_ref[i, 0]
        out_ref[1, :, i * wide : (i + 1) * wide] = second_ref[i, 0]


def as_rows(first, second):
    n_y, n_z, quarter, wide = first.shape
    spec = pl.BlockSpec((n_y, 1, quarter, wide), lambda i: (0, i, 0, 0))
    return pl.pallas_call(
        rows_kernel,
        grid=(n_z,),
        in_specs=[spec, spec],
        out_specs=pl.BlockSpec((2, quarter, n_y * wide), lambda i: (0, i, 0)),
        out_shape=jax.ShapeDtypeStruct((2, n_z * quarter, n_y * wide), F32),
    )(first, second)


def body(cells, gram_slots, diag_inverse, lower_block, trail_factor):
    n_x, n_core, n_y, n_z = (lax.axis_size(a) for a in ROWS + COLS)
    n_rows, n_cols = n_x * n_core, n_y * n_z
    col = lax.axis_index(COLS)
    row = lax.axis_index(ROWS)
    core = lax.axis_index("core")
    x_at = lax.axis_index("x")
    z_at = lax.axis_index("z")
    list_len = cells.shape[0]
    run_len = list_len // n_cols
    slab = list_len // n_rows
    runs_in_slab = slab // run_len
    block_rows = gram_slots.shape[1]
    capacity = gram_slots.shape[2]
    per_run = capacity // n_cols
    slab_slots = runs_in_slab * per_run
    width = diag_inverse.shape[2]
    trail_blocks = trail_factor.shape[0]
    quarter = block_rows // n_z
    sub = n_core * quarter

    owners = cells // (NCELL // n_cols)
    onehot = (owners[:, None] == jnp.arange(n_cols, dtype=jnp.int32)[None, :]).astype(jnp.int32)
    blocked = onehot.reshape(n_cols, run_len, n_cols)
    lower = jnp.tril(jnp.ones((run_len, run_len), F32), -1)
    in_run = jnp.einsum("ij,bjo->bio", lower, blocked.astype(F32)).astype(jnp.int32)
    run_total = jnp.sum(blocked, axis=1)
    runs = jnp.arange(n_cols)
    before = jnp.sum(jnp.where(runs[:, None, None] > runs[None, :, None], run_total[None, :, :], 0), axis=1)
    pair_rank = jnp.sum(in_run * blocked, axis=2).reshape(list_len)
    slots_of = pair_rank + jnp.sum(before[:, None, :] * blocked, axis=2).reshape(list_len)
    mine = owners == col
    position = jnp.arange(list_len, dtype=jnp.int32) // run_len * per_run + pair_rank
    slot_range = jnp.arange(capacity, dtype=jnp.int32)
    to_list = ((slots_of[None, :] == slot_range[:, None]) & mine[None, :]).astype(F32)
    to_runs = dot(
        ((position[None, :] == slot_range[:, None]) & mine[None, :]).astype(F32),
        to_list,
        ((1,), (1,)),
        lax.Precision.DEFAULT,
    )

    def quarters(cut):
        return [cut(z_at)] + [shift(cut((z_at + by) % n_z), "z", by) for by in range(1, n_z)]

    def rows_at(matrix, at):
        return lax.dynamic_slice_in_dim(matrix, at * quarter, quarter, matrix.ndim - 2)

    def all_rows(pieces):
        return lax.all_gather(jnp.concatenate(pieces, axis=1), ROWS, axis=0, tiled=True)

    inverse_0 = all_rows(quarters(lambda at: rows_at(diag_inverse[0], at)))
    later = quarters(lambda at: jnp.stack([rows_at(lower_block, at), rows_at(diag_inverse[1], at)]))

    outgoing = lax.dot_general(
        to_runs, gram_slots[0:2], (((1,), (2,)), ((), ())), precision=HIGHEST, preferred_element_type=F32
    )
    slab_gram = exchange(outgoing.reshape(n_rows, slab_slots, 2, block_rows), ROWS)
    slab_gram = slab_gram.reshape(n_y, n_core, slab_slots, 2, n_z, quarter).transpose(0, 4, 2, 3, 1, 5)
    sub_gram = exchange(slab_gram.reshape(n_cols, slab_slots, 2 * sub), COLS)
    slab_owner = lax.dynamic_slice_in_dim(owners, row * slab, slab)
    slab_rank = lax.dynamic_slice_in_dim(pair_rank, row * slab, slab)
    slab_slot = jnp.arange(slab, dtype=jnp.int32) // run_len * per_run + slab_rank
    from_owner = (
        jnp.arange(n_cols * slab_slots, dtype=jnp.int32)[:, None] == (slab_owner * slab_slots + slab_slot)[None, :]
    ).astype(F32)
    rhs = dot(sub_gram.reshape(n_cols * slab_slots, 2 * sub), from_owner, ((0,), (0,)), HIGHEST)
    rhs = rhs.reshape(2, sub, slab)

    below = all_rows([v[0] for v in later])
    inverse_1 = all_rows([v[1] for v in later])
    where_z = z_at.astype(jnp.int32).reshape(1)

    def spread_z(block):
        return spread(block, "z").reshape(n_z, n_core, quarter, slab)

    def product(matrix, pieces):
        return jnp.sum(exchange(apply_matrix(where_z, matrix, pieces, n_y), "y"), axis=0)

    axes = ROWS + COLS
    sizes = (n_x, n_core, n_y, n_z)

    def device(x, k, y, z):
        return ((x * n_core + k) * n_y + y) * n_z + z

    def solution_rows(block):
        pieces = block.reshape(n_core, quarter, slab)
        moved = []
        for m in range(n_core):
            to = [
                (device(x, k, y, z), device(y, k ^ m, x, z))
                for x in range(n_x)
                for k in range(n_core)
                for y in range(n_y)
                for z in range(n_z)
            ]
            moved.append(lax.ppermute(lax.dynamic_index_in_dim(pieces, core ^ m, 0, keepdims=False), axes, to))
        piece = jnp.where(core == 0, jnp.concatenate(moved, axis=1), jnp.concatenate(moved[::-1], axis=1))
        return lax.all_gather(piece, COLS, axis=0, tiled=False)

    first = product(inverse_0, spread_z(rhs[0]))
    first_pieces = spread_z(first)
    first_out = solution_rows(first)
    second_rhs = rhs[1] - product(below, first_pieces)

    factor, trail_gram, _ = lax.optimization_barrier((trail_factor, gram_slots[2:], rhs))
    own = quarters(
        lambda at: jnp.concatenate(
            [rows_at(factor[:, 0], at), rows_at(factor[:, 1], at), rows_at(trail_gram, at)], axis=2
        )
    )
    other = [shift(v, "core", 1) for v in own]
    trail_owner = col // n_z * n_z + jnp.arange(n_z, dtype=jnp.int32)
    slab_order = ((x_at + jnp.arange(n_x, dtype=jnp.int32)) % n_x * n_core + core)[:, None] * slab
    list_order = (slab_order + jnp.arange(slab, dtype=jnp.int32)[None, :]).reshape(-1)
    core_lists = lambda v: jnp.take(v, list_order)
    to_lists = (
        (core_lists(slots_of)[None, None, :] == slot_range[None, :, None])
        & (core_lists(owners)[None, None, :] == trail_owner[:, None, None])
    ).astype(BF16)
    where = jnp.stack([x_at, z_at]).astype(jnp.int32)
    first_all = [first_pieces] + [shift(first_pieces, "x", -d) for d in range(1, n_x)]
    base = apply_trail(where, own, other, 0, first_all, to_lists, True, n_x, capacity)

    second = product(inverse_1, spread_z(second_rhs))
    second_out = solution_rows(second)
    second_all = spread(second, ("x", "z")).reshape(n_x, n_z, n_core, quarter, slab)
    terms = apply_trail(where, own, other, 1, [second_all], base, False, n_x, capacity)
    total = jnp.sum(exchange(terms, "y"), axis=0).reshape(n_core, trail_blocks, quarter, slab)
    kept, given = total[0], total[1]
    got = shift(given, "core", 1)
    pair = jnp.where(core == 0, jnp.stack([kept, got]), jnp.stack([got, kept]))
    pair = pair.reshape(n_core, trail_blocks, quarter, n_z // n_core, run_len).transpose(0, 3, 1, 2, 4)
    out = exchange(pair.reshape(n_z, trail_blocks, quarter, run_len), "z")
    trail_out = out.transpose(1, 0, 2, 3).reshape(trail_blocks, block_rows, run_len)
    return as_rows(*(v.reshape(n_y, n_z, quarter, n_core * slab) for v in (first_out, second_out))), trail_out


def solution(mesh):
    n_rows, n_cols = mesh.devices.shape
    side = int(round(n_cols**0.5))
    mesh = Mesh(mesh.devices.reshape(n_rows // 2, 2, side, n_cols // side), ROWS + COLS)
    return jax.shard_map(
        body,
        mesh=mesh,
        in_specs=(
            P(),
            P(None, ROWS, COLS),
            P(None, ROWS, COLS),
            P(ROWS, COLS),
            P(None, None, ROWS, COLS),
        ),
        out_specs=(P(None, ROWS, None), P(None, ROWS, COLS)),
        check_vma=False,
    )
```

profile of v0, /device:TPU:0, one launch (start us, length us, event | category | flops | bytes accessed | tf_op | source)
XLA Modules:
  0.0 378.2 jit_solution(17567457115840252983)
XLA Ops:
  7.3 1.3 fusion.37
  8.6 2.1 collective-permute-start
  10.7 3.6 collective-permute-start.1
  14.3 1.0 collective-permute-start.2
  15.3 1.0 collective-permute-done
  16.3 4.0 %collective-permute-done.1 = f32[128,256]{1,0:T(8,128)S(1)} collective-permute-done((f32[128,256]{1,0:T(8,128)S(1)}, f32[128,256]{1,0:T(8,128)S(1)}, u32[]{:S(2)}, u32[]{:S(2)}) %collective-permute-start.1) | collective-permute-done | bytes 131104 | tf_op jit(solution)/shard_map/ppermute | solution.py:26
  20.3 0.8 pad_maximum_fusion.5
  21.6 1.3 collective-permute-start.5
  22.9 2.5 collective-permute-start.6
  25.4 1.3 collective-permute-start.7
  26.7 4.1 %collective-permute-done.5 = f32[2,128,256]{2,1,0:T(8,128)S(1)} collective-permute-done((f32[2,128,256]{2,1,0:T(8,128)S(1)}, f32[2,128,256]{2,1,0:T(8,128)S(1)}, u32[]{:S(2)}, u32[]{:S(2)}) %collective-permute-start.5) | collective-permute-done | bytes 262176 | tf_op jit(solution)/shard_map/ppermute | solution.py:26
  30.8 5.6 %collective-permute-done.6 = f32[2,128,256]{2,1,0:T(8,128)S(1)} collective-permute-done((f32[2,128,256]{2,1,0:T(8,128)S(1)}, f32[2,128,256]{2,1,0:T(8,128)S(1)}, u32[]{:S(2)}, u32[]{:S(2)}) %collective-permute-start.6) | collective-permute-done | bytes 262176 | tf_op jit(solution)/shard_map/ppermute | solution.py:26
  36.5 0.9 pad_maximum_fusion.7
  37.5 0.9 pad_maximum_fusion.6
  40.5 17.7 %all_to_all.55 = f32[8,16,2,512]{3,1,2,0:T(8,128)S(1)} all-to-all(f32[8,16,2,512]{3,1,2,0:T(8,128)S(1)} %copy.15), channel_id=1, replica_groups=mesh['x'=4,'core'=2,'y'=4,'z'=4] {'x','core'}, dimensions={0} | all-to-all | bytes 1048576 | tf_op jit(solution)/shard_map/all_to_all | solution.py:30
  58.8 1.2 reshape.348
  60.0 7.0 %all-to-all-start.1 = ((f32[16,16,512]{2,1,0:T(8,128)}), f32[16,16,512]{2,1,0:T(8,128)S(1)}, u32[]{:S(2)}, u32[]{:S(2)}) async-start(f32[16,16,512]{2,1,0:T(8,128)} %reshape.348), calls=%async_computation.1 | async-start | bytes 1048576 | tf_op jit(solution)/shard_map/all_to_all | solution.py:30
  67.1 11.5 %all-to-all-done.1 = f32[16,16,512]{2,1,0:T(8,128)S(1)} async-done(((f32[16,16,512]{2,1,0:T(8,128)}), f32[16,16,512]{2,1,0:T(8,128)S(1)}, u32[]{:S(2)}, u32[]{:S(2)}) %all-to-all-start.1) | async-done | bytes 524320 | tf_op jit(solution)/shard_map/all_to_all | solution.py:30
  80.0 11.4 %all_to_all.56 = f32[4,256,128]{2,1,0:T(8,128)} all-to-all(f32[4,256,128]{2,1,0:T(8,128)S(1)} %broadcast_in_dim.45), channel_id=1, replica_groups=mesh['x'=4,'core'=2,'y'=4,'z'=4] {'z'}, dimensions={0} | all-to-all | bytes 1048576 | tf_op jit(solution)/shard_map/all_to_all | solution.py:30
  91.4 5.1 %shard_map.68 = f32[4,256,128]{2,1,0:T(8,128)} custom-call(s32[1]{0:T(128)} %bitcast.at_ref, f32[1024,1024]{1,0:T(8,128)} %all-gather.6.cloned.1.call-done.matrix_ref, f32[4,2,128,128]{3,2,1,0:T(8,128)} %bitcast.114), custom_call_target="tpu_custom_call" | custom-call | flops 805306368 | bytes 4194304 | tf_op jit(solution)/shard_map/pallas_call | solution.py:67
  96.5 3.5 all-to-all-start.3
  100.0 8.0 %all-to-all-done.3 = f32[4,256,128]{2,1,0:T(8,128)S(1)} async-done(((f32[4,256,128]{2,1,0:T(8,128)}), f32[4,256,128]{2,1,0:T(8,128)S(1)}, u32[]{:S(2)}, u32[]{:S(2)}) %all-to-all-start.3) | async-done | bytes 524320 | tf_op jit(solution)/shard_map/all_to_all | solution.py:30
  109.0 1.2 collective-permute-done.4
  110.9 0.9 constant_dynamic-slice_fusion
  111.9 4.0 %fusion.36 = (f32[4,1,512,256]{3,2,1,0:T(8,128)S(1)}, f32[4,1,512,256]{3,2,1,0:T(8,128)}) fusion(f32[4,2,512,256]{3,2,1,0:T(8,128)} %param.11), kind=kLoop, calls=%fused_computation.126 | loop fusion | bytes 8388608 | tf_op jit(solution)/shard_map/slice | solution.py:275
  115.8 0.8 broadcast_in_dim.46
  116.7 3.5 all-to-all-start.4
  120.2 3.1 dynamic-slice_bitcast_fusion
  123.3 1.2 pad_maximum_fusion.2
  124.5 3.5 collective-permute-start.11
  128.0 3.0 all-to-all-done.4
  131.8 5.1 %shard_map.69 = f32[4,256,128]{2,1,0:T(8,128)} custom-call(s32[1]{0:T(128)} %bitcast.at_ref, f32[1024,1024]{1,0:T(8,128)} %all-gather.12.cloned.1.call-done.matrix_ref, f32[4,2,128,128]{3,2,1,0:T(8,128)} %bitcast.104), custom_call_target="tpu_custom_call" | custom-call | flops 805306368 | bytes 4194304 | tf_op jit(solution)/shard_map/pallas_call | solution.py:67
  136.9 15.7 %all-to-all-start.5 = ((f32[4,256,128]{2,1,0:T(8,128)}), f32[4,256,128]{2,1,0:T(8,128)}, u32[]{:S(2)}, u32[]{:S(2)}) async-start(f32[4,256,128]{2,1,0:T(8,128)} %shard_map.69), calls=%async_computation.5 | async-start | bytes 1048576 | tf_op jit(solution)/shard_map/all_to_all | solution.py:30
  152.6 2.4 pad_maximum_fusion.3
  155.6 1.2 pad_maximum_fusion.1
  156.8 1.4 collective-permute-start.10
  158.2 3.3 all-to-all-done.5
  161.5 1.1 reduce_sum.77
  162.6 0.9 slice_subtract_fusion
  163.5 0.9 broadcast_in_dim.47
  164.4 4.1 %all-to-all-start.6 = ((f32[4,256,128]{2,1,0:T(8,128)}), f32[4,256,128]{2,1,0:T(8,128)}, u32[]{:S(2)}, u32[]{:S(2)}) async-start(f32[4,256,128]{2,1,0:T(8,128)} %broadcast_in_dim.47), calls=%async_computation.6 | async-start | bytes 1048576 | tf_op jit(solution)/shard_map/all_to_all | solution.py:30
  168.6 1.1 pad_maximum_fusion.refs_4_.refs_12_.refs_1_
  170.0 32.7 %all-to-all-done.6 = f32[4,256,128]{2,1,0:T(8,128)} async-done(((f32[4,256,128]{2,1,0:T(8,128)}), f32[4,256,128]{2,1,0:T(8,128)}, u32[]{:S(2)}, u32[]{:S(2)}) %all-to-all-start.6) | async-done | bytes 524320 | tf_op jit(solution)/shard_map/all_to_all | solution.py:30
  202.7 5.1 %shard_map.70 = f32[4,256,128]{2,1,0:T(8,128)} custom-call(s32[1]{0:T(128)} %bitcast.at_ref, f32[1024,1024]{1,0:T(8,128)} %all-gather.10.cloned.1.call-done.matrix_ref, f32[4,2,128,128]{3,2,1,0:T(8,128)} %bitcast.29.operand_ref), custom_call_target="tpu_custom_call" | custom-call | flops 805306368 | bytes 4194304 | tf_op jit(solution)/shard_map/pallas_call | solution.py:67
  207.9 15.7 %all-to-all-start.7 = ((f32[4,256,128]{2,1,0:T(8,128)}), f32[4,256,128]{2,1,0:T(8,128)S(1)}, u32[]{:S(2)}, u32[]{:S(2)}) async-start(f32[4,256,128]{2,1,0:T(8,128)} %shard_map.70), calls=%async_computation.7 | async-start | bytes 1048576 | tf_op jit(solution)/shard_map/all_to_all | solution.py:30
  223.7 9.1 %all-to-all-done.7 = f32[4,256,128]{2,1,0:T(8,128)S(1)} async-done(((f32[4,256,128]{2,1,0:T(8,128)}), f32[4,256,128]{2,1,0:T(8,128)S(1)}, u32[]{:S(2)}, u32[]{:S(2)}) %all-to-all-start.7) | async-done | bytes 524320 | tf_op jit(solution)/shard_map/all_to_all | solution.py:30
  232.8 1.5 broadcast_in_dim.48
  234.3 5.6 %all-to-all-start.8 = ((f32[16,256,128]{2,1,0:T(8,128)}), f32[16,256,128]{2,1,0:T(8,128)}, u32[]{:S(2)}, u32[]{:S(2)}) async-start(f32[16,256,128]{2,1,0:T(8,128)} %broadcast_in_dim.48), calls=%async_computation.8 | async-start | bytes 4194304 | tf_op jit(solution)/shard_map/all_to_all | solution.py:30
  240.0 2.3 gather_fusion
  242.3 2.3 gather_fusion.1
  246.3 9.1 %collective-permute-start.17 = (f32[4,2,128,128]{3,2,1,0:T(8,128)S(1)}, f32[4,2,128,128]{3,2,1,0:T(8,128)S(1)}, u32[]{:S(2)}, u32[]{:S(2)}) collective-permute-start(f32[4,2,128,128]{3,2,1,0:T(8,128)S(1)} %bitcast.106), channel_id=1, source_target_pairs={{0,96},{32,0},{64,32},{96,64},{1,97},{33,1},{65,33},{97,65},{2,98}... | collective-permute-start | bytes 1572872 | tf_op jit(solution)/shard_map/ppermute | solution.py:26
  255.3 12.6 %collective-permute-start.18 = (f32[4,2,128,128]{3,2,1,0:T(8,128)S(1)}, f32[4,2,128,128]{3,2,1,0:T(8,128)S(1)}, u32[]{:S(2)}, u32[]{:S(2)}) collective-permute-start(f32[4,2,128,128]{3,2,1,0:T(8,128)S(1)} %bitcast.107), channel_id=1, source_target_pairs={{0,64},{32,96},{64,0},{96,32},{1,65},{33,97},{65,1},{97,33},{2,66}... | collective-permute-start | bytes 1572872 | tf_op jit(solution)/shard_map/ppermute | solution.py:26
  268.0 14.7 %collective-permute-start.19 = (f32[4,2,128,128]{3,2,1,0:T(8,128)S(1)}, f32[4,2,128,128]{3,2,1,0:T(8,128)S(1)}, u32[]{:S(2)}, u32[]{:S(2)}) collective-permute-start(f32[4,2,128,128]{3,2,1,0:T(8,128)S(1)} %bitcast.108), channel_id=1, source_target_pairs={{0,32},{32,64},{64,96},{96,0},{1,33},{33,65},{65,97},{97,1},{2,34}... | collective-permute-start | bytes 1572872 | tf_op jit(solution)/shard_map/ppermute | solution.py:26
  284.1 0.9 and_convert_fusion.refs_20_
  285.0 7.5 %collective-permute-done.19.refs_3_ = f32[4,2,128,128]{3,2,1,0:T(8,128)S(1)} collective-permute-done((f32[4,2,128,128]{3,2,1,0:T(8,128)S(1)}, f32[4,2,128,128]{3,2,1,0:T(8,128)S(1)}, u32[]{:S(2)}, u32[]{:S(2)}) %collective-permute-start.19) | collective-permute-done | bytes 524320 | tf_op jit(solution)/shard_map/ppermute | solution.py:26
  293.3 10.6 %shard_map.72.refs_9_ = f32[4,1024,128]{2,1,0:T(8,128)} custom-call(s32[2]{0:T(128)} %pad_add_fusion.at_ref, f32[4,2,128,128]{3,2,1,0:T(8,128)} %bitcast.105, f32[4,2,128,128]{3,2,1,0:T(8,128)} %copy-done.11, f32[4,2,128,128]{3,2,1,0:T(8,128)} %copy-done.12, f32[4,2,128,128]{3,2,1,0:T(8,128)} %copy-done.13, f32[4,128,640]{2,1,0:T(8,128)} %copy-done, ...), custom_call_target="tpu_custom_call" | custom-call | flops 3221225472 | bytes 12582912 | tf_op jit(solution)/shard_map/pallas_call | solution.py:136
  303.9 8.3 %shard_map.73 = f32[4,1024,128]{2,1,0:T(8,128)} custom-call(s32[2]{0:T(128)} %pad_add_fusion.at_ref, f32[4,4,2,128,128]{4,3,2,1,0:T(8,128)} %bitcast.37.refs_0_, f32[4,128,640]{2,1,0:T(8,128)} %copy-done, f32[4,128,640]{2,1,0:T(8,128)} %collective-permute-done.10.refs_5_.refs_13_.refs_2_, f32[4,128,640]{2,1,0:T(8,128)} %copy-done.1, ...), custom_call_target="tpu_custom_call" | custom-call | flops 3221225472 | bytes 12582912 | tf_op jit(solution)/shard_map/pallas_call | solution.py:136
  312.2 41.8 %all_to_all.57 = f32[4,1024,128]{2,1,0:T(8,128)S(1)} all-to-all(f32[4,1024,128]{2,1,0:T(8,128)} %shard_map.73), channel_id=1, replica_groups=mesh['x'=4,'core'=2,'y'=4,'z'=4] {'y'}, dimensions={0} | all-to-all | bytes 4194304 | tf_op jit(solution)/shard_map/all_to_all | solution.py:30
  354.3 1.5 collective-permute-done.20
  356.2 1.1 copy.17
  357.3 3.5 all-to-all-start.10
  360.8 4.7 %shard_map.71 = f32[2,512,1024]{2,1,0:T(8,128)} custom-call(f32[4,4,128,256]{3,2,1,0:T(8,128)} %bitcast.112, f32[4,4,128,256]{3,2,1,0:T(8,128)} %bitcast.113), custom_call_target="tpu_custom_call" | custom-call | tf_op jit(solution)/shard_map/pallas_call | solution.py:158
  365.5 5.3 %all-to-all-done.10 = f32[4,4,128,64]{2,3,1,0:T(8,128)S(1)} async-done(((f32[4,4,128,64]{2,3,1,0:T(8,128)}), f32[4,4,128,64]{2,3,1,0:T(8,128)S(1)}, u32[]{:S(2)}, u32[]{:S(2)}) %all-to-all-start.10) | async-done | bytes 524320 | tf_op jit(solution)/shard_map/all_to_all | solution.py:30
  370.8 0.9 copy_bitcast_fusion
  (122 shorter events, 12.7 us)
Async XLA Ops:
  7.2 84.2 %all-gather.6.cloned.1.call-start = ((), (), s32[]{:S(2)}) async-start(), calls=%async_computation.11 | async-start | bytes 4718592 | tf_op jit(solution)/shard_map/all_gather | solution.py:216
  8.6 7.7 %collective-permute-start = (f32[128,256]{1,0:T(8,128)S(1)}, f32[128,256]{1,0:T(8,128)S(1)}, u32[]{:S(2)}, u32[]{:S(2)}) collective-permute-start(f32[128,256]{1,0:T(8,128)S(1)} %get-tuple-element.40), channel_id=1, source_target_pairs={{0,1},{1,2},{2,3},{3,0},{4,5},{5,6},{6,7},{7,4},{8,9},{9,10},{10,1... | collective-permute-start | bytes 393224 | tf_op jit(solution)/shard_map/ppermute | solution.py:26
  10.7 9.6 %collective-permute-start.1 = (f32[128,256]{1,0:T(8,128)S(1)}, f32[128,256]{1,0:T(8,128)S(1)}, u32[]{:S(2)}, u32[]{:S(2)}) collective-permute-start(f32[128,256]{1,0:T(8,128)S(1)} %get-tuple-element.39), channel_id=1, source_target_pairs={{0,2},{1,3},{2,0},{3,1},{4,6},{5,7},{6,4},{7,5},{8,10},{9,11},{10,... | collective-permute-start | bytes 393224 | tf_op jit(solution)/shard_map/ppermute | solution.py:26
  14.3 6.0 %collective-permute-start.2 = (f32[128,256]{1,0:T(8,128)S(1)}, f32[128,256]{1,0:T(8,128)S(1)}, u32[]{:S(2)}, u32[]{:S(2)}) collective-permute-start(f32[128,256]{1,0:T(8,128)S(1)} %get-tuple-element.38), channel_id=1, source_target_pairs={{0,3},{1,0},{2,1},{3,2},{4,7},{5,4},{6,5},{7,6},{8,11},{9,8},{10,9... | collective-permute-start | bytes 393224 | tf_op jit(solution)/shard_map/ppermute | solution.py:26
  20.3 1.2 copy-start.14
  21.1 106.9 %all-gather.12.cloned.1.call-start = ((), (), s32[]{:S(2)}) async-start(), calls=%async_computation.14 | async-start | bytes 4718592 | tf_op jit(solution)/shard_map/all_gather | solution.py:216
  21.6 9.2 %collective-permute-start.5 = (f32[2,128,256]{2,1,0:T(8,128)S(1)}, f32[2,128,256]{2,1,0:T(8,128)S(1)}, u32[]{:S(2)}, u32[]{:S(2)}) collective-permute-start(f32[2,128,256]{2,1,0:T(8,128)S(1)} %pad_maximum_fusion.8), channel_id=1, source_target_pairs={{0,1},{1,2},{2,3},{3,0},{4,5},{5,6},{6,7},{7,4},{8,9},{9,10},{10,1... | collective-permute-start | bytes 786440 | tf_op jit(solution)/shard_map/ppermute | solution.py:26
  22.9 13.6 %collective-permute-start.6 = (f32[2,128,256]{2,1,0:T(8,128)S(1)}, f32[2,128,256]{2,1,0:T(8,128)S(1)}, u32[]{:S(2)}, u32[]{:S(2)}) collective-permute-start(f32[2,128,256]{2,1,0:T(8,128)S(1)} %pad_maximum_fusion.9), channel_id=1, source_target_pairs={{0,2},{1,3},{2,0},{3,1},{4,6},{5,7},{6,4},{7,5},{8,10},{9,11},{10,... | collective-permute-start | bytes 786440 | tf_op jit(solution)/shard_map/ppermute | solution.py:26
  25.4 11.1 %collective-permute-start.7 = (f32[2,128,256]{2,1,0:T(8,128)S(1)}, f32[2,128,256]{2,1,0:T(8,128)S(1)}, u32[]{:S(2)}, u32[]{:S(2)}) collective-permute-start(f32[2,128,256]{2,1,0:T(8,128)S(1)} %pad_maximum_fusion.10), channel_id=1, source_target_pairs={{0,3},{1,0},{2,1},{3,2},{4,7},{5,4},{6,5},{7,6},{8,11},{9,8},{10,9... | collective-permute-start | bytes 786440 | tf_op jit(solution)/shard_map/ppermute | solution.py:26
  37.4 1.0 copy-start.15
  37.4 2.4 copy-start.4
  37.4 132.6 %all-gather.10.cloned.1.call-start = ((), (), s32[]{:S(2)}) async-start(), calls=%async_computation.13 | async-start | bytes 4718592 | tf_op jit(solution)/shard_map/all_gather | solution.py:216
  60.0 18.6 %all-to-all-start.1 = ((f32[16,16,512]{2,1,0:T(8,128)}), f32[16,16,512]{2,1,0:T(8,128)S(1)}, u32[]{:S(2)}, u32[]{:S(2)}) async-start(f32[16,16,512]{2,1,0:T(8,128)} %reshape.348), calls=%async_computation.1 | async-start | bytes 1048576 | tf_op jit(solution)/shard_map/all_to_all | solution.py:30
  79.2 0.7 copy-start.10
  96.5 11.5 %all-to-all-start.3 = ((f32[4,256,128]{2,1,0:T(8,128)}), f32[4,256,128]{2,1,0:T(8,128)S(1)}, u32[]{:S(2)}, u32[]{:S(2)}) async-start(f32[4,256,128]{2,1,0:T(8,128)} %shard_map.68), calls=%async_computation.3 | async-start | bytes 1048576 | tf_op jit(solution)/shard_map/all_to_all | solution.py:30
  100.0 260.8 %all-gather.8.cloned.1.call-start = ((), (), s32[]{:S(2)}) async-start(), calls=%async_computation.12 | async-start | bytes 2228224 | tf_op jit(solution)/shard_map/all_gather | solution.py:265
  108.1 2.9 slice-start
  108.1 0.9 collective-permute-start.3
  108.9 1.3 collective-permute-start.4
  116.7 14.3 %all-to-all-start.4 = ((f32[4,256,128]{2,1,0:T(8,128)}), f32[4,256,128]{2,1,0:T(8,128)S(1)}, u32[]{:S(2)}, u32[]{:S(2)}) async-start(f32[4,256,128]{2,1,0:T(8,128)} %broadcast_in_dim.46), calls=%async_computation.4 | async-start | bytes 1048576 | tf_op jit(solution)/shard_map/all_to_all | solution.py:30
  120.1 3.2 copy-start.9
  124.5 99.1 %collective-permute-start.11 = (f32[4,128,640]{2,1,0:T(8,128)}, f32[4,128,640]{2,1,0:T(8,128)S(1)}, u32[]{:S(2)}, u32[]{:S(2)}) collective-permute-start(f32[4,128,640]{2,1,0:T(8,128)} %pad_maximum_fusion.2), channel_id=1, source_target_pairs={{0,2},{1,3},{2,0},{3,1},{4,6},{5,7},{6,4},{7,5},{8,10},{9,11},{10,... | collective-permute-start | bytes 3932168 | tf_op jit(solution)/shard_map/ppermute | solution.py:26
  131.0 0.8 copy-start.2
  136.9 15.7 %copy-start.7 = (f32[4,128,256]{2,1,0:T(8,128)S(1)}, f32[4,128,256]{2,1,0:T(8,128)}, u32[]{:S(2)}) copy-start(f32[4,128,256]{2,1,0:T(8,128)} %get-tuple-element.15) | copy-start | bytes 1572868
  136.9 24.6 %all-to-all-start.5 = ((f32[4,256,128]{2,1,0:T(8,128)}), f32[4,256,128]{2,1,0:T(8,128)}, u32[]{:S(2)}, u32[]{:S(2)}) async-start(f32[4,256,128]{2,1,0:T(8,128)} %shard_map.69), calls=%async_computation.5 | async-start | bytes 1048576 | tf_op jit(solution)/shard_map/all_to_all | solution.py:30
  152.6 3.0 copy-start.6
  152.6 3.0 copy-start.8
  155.0 89.6 %collective-permute-start.12 = (f32[4,128,640]{2,1,0:T(8,128)}, f32[4,128,640]{2,1,0:T(8,128)}, u32[]{:S(2)}, u32[]{:S(2)}) collective-permute-start(f32[4,128,640]{2,1,0:T(8,128)} %pad_maximum_fusion.3), channel_id=1, source_target_pairs={{0,3},{1,0},{2,1},{3,2},{4,7},{5,4},{6,5},{7,6},{8,11},{9,8},{10,9... | collective-permute-start | bytes 3932168 | tf_op jit(solution)/shard_map/ppermute | solution.py:26
  156.8 11.7 %copy-start.5 = (f32[4,128,256]{2,1,0:T(8,128)S(1)}, f32[4,128,256]{2,1,0:T(8,128)}, u32[]{:S(2)}) copy-start(f32[4,128,256]{2,1,0:T(8,128)} %get-tuple-element.18) | copy-start | bytes 1572868
  156.8 87.9 %collective-permute-start.10 = (f32[4,128,640]{2,1,0:T(8,128)}, f32[4,128,640]{2,1,0:T(8,128)}, u32[]{:S(2)}, u32[]{:S(2)}) collective-permute-start(f32[4,128,640]{2,1,0:T(8,128)} %pad_maximum_fusion.1), channel_id=1, source_target_pairs={{0,1},{1,2},{2,3},{3,0},{4,5},{5,6},{6,7},{7,4},{8,9},{9,10},{10,1... | collective-permute-start | bytes 3932168 | tf_op jit(solution)/shard_map/ppermute | solution.py:26
  164.4 38.3 %all-to-all-start.6 = ((f32[4,256,128]{2,1,0:T(8,128)}), f32[4,256,128]{2,1,0:T(8,128)}, u32[]{:S(2)}, u32[]{:S(2)}) async-start(f32[4,256,128]{2,1,0:T(8,128)} %broadcast_in_dim.47), calls=%async_computation.6 | async-start | bytes 1048576 | tf_op jit(solution)/shard_map/all_to_all | solution.py:30
  169.7 38.2 %copy-start = (f32[4,128,640]{2,1,0:T(8,128)}, f32[4,128,640]{2,1,0:T(8,128)S(1)}, u32[]{:S(2)}) copy-start(f32[4,128,640]{2,1,0:T(8,128)S(1)} %pad_maximum_fusion.refs_4_.refs_12_.refs_1_) | copy-start | bytes 3932164
  169.7 76.3 %collective-permute-start.13 = (f32[4,128,640]{2,1,0:T(8,128)S(1)}, f32[4,128,640]{2,1,0:T(8,128)}, u32[]{:S(2)}, u32[]{:S(2)}) collective-permute-start(f32[4,128,640]{2,1,0:T(8,128)S(1)} %pad_maximum_fusion.refs_4_.refs_12_.refs_1_), channel_id=1, source_target_pairs={{0,16},{16,0},{1,17},{17,1},{2,18},{18,2},{3,19},{19,3},{4,20},{20... | collective-permute-start | bytes 3932168 | tf_op jit(solution)/shard_map/ppermute | solution.py:26
  207.9 24.9 %all-to-all-start.7 = ((f32[4,256,128]{2,1,0:T(8,128)}), f32[4,256,128]{2,1,0:T(8,128)S(1)}, u32[]{:S(2)}, u32[]{:S(2)}) async-start(f32[4,256,128]{2,1,0:T(8,128)} %shard_map.70), calls=%async_computation.7 | async-start | bytes 1048576 | tf_op jit(solution)/shard_map/all_to_all | solution.py:30
  223.5 10.7 %copy-start.1 = (f32[4,128,640]{2,1,0:T(8,128)}, f32[4,128,640]{2,1,0:T(8,128)S(1)}, u32[]{:S(2)}) copy-start(f32[4,128,640]{2,1,0:T(8,128)S(1)} %collective-permute-done.11.refs_6_.refs_14_.refs_3_) | copy-start | bytes 3932164
  223.5 22.7 %collective-permute-start.15 = (f32[4,128,640]{2,1,0:T(8,128)S(1)}, f32[4,128,640]{2,1,0:T(8,128)}, u32[]{:S(2)}, u32[]{:S(2)}) collective-permute-start(f32[4,128,640]{2,1,0:T(8,128)S(1)} %collective-permute-done.11.refs_6_.refs_14_.refs_3_), channel_id=1, source_target_pairs={{0,16},{16,0},{1,17},{17,1},{2,18},{18,2},{3,19},{19,3},{4,20},{20... | collective-permute-start | bytes 3932168 | tf_op jit(solution)/shard_map/ppermute | solution.py:26
  234.3 69.6 %all-to-all-start.8 = ((f32[16,256,128]{2,1,0:T(8,128)}), f32[16,256,128]{2,1,0:T(8,128)}, u32[]{:S(2)}, u32[]{:S(2)}) async-start(f32[16,256,128]{2,1,0:T(8,128)} %broadcast_in_dim.48), calls=%async_computation.8 | async-start | bytes 4194304 | tf_op jit(solution)/shard_map/all_to_all | solution.py:30
  239.9 120.9 %all-gather.14.cloned.1.call-start = ((), (), s32[]{:S(2)}) async-start(), calls=%async_computation.15 | async-start | bytes 2228224 | tf_op jit(solution)/shard_map/all_gather | solution.py:265
  242.3 3.9 %copy-start.3 = (f32[4,256,128]{2,1,0:T(8,128)S(1)}, f32[4,256,128]{2,1,0:T(8,128)}, u32[]{:S(2)}) copy-start(f32[4,256,128]{2,1,0:T(8,128)} %copy-done.2) | copy-start | bytes 1572868
  244.7 40.3 %collective-permute-start.16 = (f32[4,128,640]{2,1,0:T(8,128)}, f32[4,128,640]{2,1,0:T(8,128)}, u32[]{:S(2)}, u32[]{:S(2)}) collective-permute-start(f32[4,128,640]{2,1,0:T(8,128)} %collective-permute-done.12.refs_7_.refs_15_.refs_4_), channel_id=1, source_target_pairs={{0,16},{16,0},{1,17},{17,1},{2,18},{18,2},{3,19},{19,3},{4,20},{20... | collective-permute-start | bytes 3932168 | tf_op jit(solution)/shard_map/ppermute | solution.py:26
  244.8 40.2 %collective-permute-start.14 = (f32[4,128,640]{2,1,0:T(8,128)}, f32[4,128,640]{2,1,0:T(8,128)}, u32[]{:S(2)}, u32[]{:S(2)}) collective-permute-start(f32[4,128,640]{2,1,0:T(8,128)} %collective-permute-done.10.refs_5_.refs_13_.refs_2_), channel_id=1, source_target_pairs={{0,16},{16,0},{1,17},{17,1},{2,18},{18,2},{3,19},{19,3},{4,20},{20... | collective-permute-start | bytes 3932168 | tf_op jit(solution)/shard_map/ppermute | solution.py:26
  245.4 9.9 %collective-permute-start.8 = (f32[128,128]{1,0:T(8,128)S(1)}, f32[128,128]{1,0:T(8,128)S(1)}, u32[]{:S(2)}, u32[]{:S(2)}) collective-permute-start(f32[128,128]{1,0:T(8,128)S(1)} %get-tuple-element.47), channel_id=1, source_target_pairs={{0,0},{1,1},{2,2},{3,3},{4,32},{5,33},{6,34},{7,35},{8,64},{9,65},... | collective-permute-start | bytes 196616 | tf_op jit(solution)/shard_map/ppermute | solution.py:263
  246.1 21.9 %collective-permute-start.9 = (f32[128,128]{1,0:T(8,128)S(1)}, f32[128,128]{1,0:T(8,128)S(1)}, u32[]{:S(2)}, u32[]{:S(2)}) collective-permute-start(f32[128,128]{1,0:T(8,128)S(1)} %get-tuple-element.48), channel_id=1, source_target_pairs={{0,16},{1,17},{2,18},{3,19},{4,48},{5,49},{6,50},{7,51},{8,80},{9,... | collective-permute-start | bytes 196616 | tf_op jit(solution)/shard_map/ppermute | solution.py:263
  246.3 38.7 %collective-permute-start.17 = (f32[4,2,128,128]{3,2,1,0:T(8,128)S(1)}, f32[4,2,128,128]{3,2,1,0:T(8,128)S(1)}, u32[]{:S(2)}, u32[]{:S(2)}) collective-permute-start(f32[4,2,128,128]{3,2,1,0:T(8,128)S(1)} %bitcast.106), channel_id=1, source_target_pairs={{0,96},{32,0},{64,32},{96,64},{1,97},{33,1},{65,33},{97,65},{2,98}... | collective-permute-start | bytes 1572872 | tf_op jit(solution)/shard_map/ppermute | solution.py:26
  255.3 29.7 %collective-permute-start.18 = (f32[4,2,128,128]{3,2,1,0:T(8,128)S(1)}, f32[4,2,128,128]{3,2,1,0:T(8,128)S(1)}, u32[]{:S(2)}, u32[]{:S(2)}) collective-permute-start(f32[4,2,128,128]{3,2,1,0:T(8,128)S(1)} %bitcast.107), channel_id=1, source_target_pairs={{0,64},{32,96},{64,0},{96,32},{1,65},{33,97},{65,1},{97,33},{2,66}... | collective-permute-start | bytes 1572872 | tf_op jit(solution)/shard_map/ppermute | solution.py:26
  268.0 24.5 %collective-permute-start.19 = (f32[4,2,128,128]{3,2,1,0:T(8,128)S(1)}, f32[4,2,128,128]{3,2,1,0:T(8,128)S(1)}, u32[]{:S(2)}, u32[]{:S(2)}) collective-permute-start(f32[4,2,128,128]{3,2,1,0:T(8,128)S(1)} %bitcast.108), channel_id=1, source_target_pairs={{0,32},{32,64},{64,96},{96,0},{1,33},{33,65},{65,97},{97,1},{2,34}... | collective-permute-start | bytes 1572872 | tf_op jit(solution)/shard_map/ppermute | solution.py:26
  285.0 7.5 %copy-start.11 = (f32[4,2,128,128]{3,2,1,0:T(8,128)}, f32[4,2,128,128]{3,2,1,0:T(8,128)S(1)}, u32[]{:S(2)}) copy-start(f32[4,2,128,128]{3,2,1,0:T(8,128)S(1)} %collective-permute-done.17.refs_1_) | copy-start | bytes 1572868
  285.0 7.5 %copy-start.12 = (f32[4,2,128,128]{3,2,1,0:T(8,128)}, f32[4,2,128,128]{3,2,1,0:T(8,128)S(1)}, u32[]{:S(2)}) copy-start(f32[4,2,128,128]{3,2,1,0:T(8,128)S(1)} %collective-permute-done.18.refs_2_) | copy-start | bytes 1572868
  292.5 0.8 copy-start.13
  354.2 1.6 collective-permute-start.20
  357.3 13.5 %all-to-all-start.10 = ((f32[4,4,128,64]{2,3,1,0:T(8,128)}), f32[4,4,128,64]{2,3,1,0:T(8,128)S(1)}, u32[]{:S(2)}, u32[]{:S(2)}) async-start(f32[4,4,128,64]{2,3,1,0:T(8,128)} %bitcast.50), calls=%async_computation.10 | async-start | bytes 1048576 | tf_op jit(solution)/shard_map/all_to_all | solution.py:30
Sparse Core Ops, SparseCore 0:
  21.3 37.2 all-gather.5
  60.2 32.0 all-gather.11
  94.0 37.6 all-gather.9
  133.7 64.9 all-gather.7
  283.5 45.4 all-gather.13
where the time goes:
time: 380 us; the launch traced here: 378 us
  starting transfers between devices  115 us (30%)
  waiting for transfers between devices  97.9 us (26%)
  blocking collectives  70.9 us (19%)
  Pallas kernels  39.1 us (10%)
  local copies, waits for them, and re-layouts  24.2 us (6%)
  other arithmetic  14.7 us (4%)
  between operations  14.4 us (4%)
    all_to_all x8, waiting for transfers between devices, exchange(): return lax.all_to_all(value, axes, 0, 0, tiled=True)  72.8 us
    all_to_all x3, blocking collectives, exchange(): return lax.all_to_all(value, axes, 0, 0, tiled=True)  70.9 us
    all_to_all x8, starting transfers between devices, exchange(): return lax.all_to_all(value, axes, 0, 0, tiled=True)  58.5 us
    ppermute x17, starting transfers between devices, shift(): lax.ppermute(value, axis, [(i, (i + by) % size) for i in range(size)])  54.7 us
    ppermute x17, waiting for transfers between devices, shift(): lax.ppermute(value, axis, [(i, (i + by) % size) for i in range(size)])  23.8 us
    pallas_call x2, Pallas kernels, apply_trail(): pl.pallas_call(functools.partial(trail_kernel, n_z, n_x, with_gram, len(l...  18.9 us
    pallas_call x3, Pallas kernels, apply_matrix(): pl.pallas_call(functools.partial(product_kernel, pieces.shape[0]), grid=(...  15.4 us
  transfers between devices with their start and end apart: 34, of which 14 were waited for; matrix products, arithmetic and copies ran while one was open for 9% of the time, Pallas kernels for 10%

commit v1 on v0

--- a/solution.py
+++ b/solution.py
@@ -53,12 +53,15 @@
 
 def product_kernel(n_z, at_ref, matrix_ref, operand_ref, out_ref):
     width = matrix_ref.shape[1] // n_z
+    slab = operand_ref.shape[-1]
     total = None
     for by in range(n_z):
-        rows = split(band_rows(operand_ref, (), at_ref[0], by, n_z))
-        term = mul(split(matrix_ref[:, by * width : (by + 1) * width]), rows)
+        high, low = split(band_rows(operand_ref, (), at_ref[0], by, n_z))
+        left = split(matrix_ref[:, by * width : (by + 1) * width])
+        both = jnp.dot(left[0], jnp.concatenate([high, low], axis=1), preferred_element_type=F32)
+        term = both[:, :slab] + (both[:, slab:] + jnp.dot(left[1], high, preferred_element_type=F32))
         total = term if total is None else total + term
-    out_ref[0] = total
+    out_ref[...] = total.reshape(out_ref.shape)
 
 
 def apply_matrix(at_z, matrix, pieces, n_y):
@@ -66,13 +69,13 @@
     slab = pieces.shape[-1]
     return pl.pallas_call(
         functools.partial(product_kernel, pieces.shape[0]),
-        grid=(n_y,),
+        grid=(2,),
         in_specs=[
             SMEM,
-            pl.BlockSpec((rows // n_y, band), lambda i: (i, 0)),
+            pl.BlockSpec((rows // 2, band), lambda i: (i, 0)),
             pl.BlockSpec(pieces.shape, lambda i: (0, 0, 0, 0)),
         ],
-        out_specs=pl.BlockSpec((1, rows // n_y, slab), lambda i: (i, 0, 0)),
+        out_specs=pl.BlockSpec((n_y // 2, rows // n_y, slab), lambda i: (i, 0, 0)),
         out_shape=jax.ShapeDtypeStruct((n_y, rows // n_y, slab), F32),
         cost_estimate=pl.CostEstimate(
             flops=6 * rows * band * slab, bytes_accessed=4 * rows * band, transcendentals=0
@@ -119,18 +122,18 @@
             out_ref[at, into, :] = first - total[:, mine]
 
 
-def apply_trail(where, own, other, which, lists, start, with_gram, n_x, slots):
+def apply_trail(where, own, other, width, lists, start, with_gram, n_x):
     n_z = len(own)
     blocks, quarter, depth = own[0].shape
-    width = (depth - slots) // 2
+    slots = depth - width
     slab = lists[0].shape[-1]
     whole = lambda v: pl.BlockSpec(v.shape, lambda *_: (0,) * v.ndim)
-    part = pl.BlockSpec((blocks, quarter, width), lambda *_: (0, 0, which))
+    part = pl.BlockSpec((blocks, quarter, width), lambda *_: (0, 0, 0))
     pieces = [*own, *other]
     specs = [SMEM] + [whole(v) for v in lists] + [part] * (2 * n_z)
     args = [where, *lists, *pieces]
     if with_gram:
-        specs += [pl.BlockSpec((blocks, quarter, slots), lambda *_: (0, 0, 2 * width // slots))] * (2 * n_z)
+        specs += [pl.BlockSpec((blocks, quarter, slots), lambda *_: (0, 0, width // slots))] * (2 * n_z)
         args += pieces
     rows = 2 * blocks * quarter
     return pl.pallas_call(
@@ -162,6 +165,10 @@
         out_specs=pl.BlockSpec((2, quarter, n_y * wide), lambda i: (0, i, 0)),
         out_shape=jax.ShapeDtypeStruct((2, n_z * quarter, n_y * wide), F32),
     )(first, second)
+
+
+def after(value, *others):
+    return lax.optimization_barrier((value, *others))[0]
 
 
 def body(cells, gram_slots, diag_inverse, lower_block, trail_factor):
@@ -206,8 +213,11 @@
         lax.Precision.DEFAULT,
     )
 
+    def moved(cut, by):
+        return shift(cut((z_at + by) % n_z), "z", by) if by else cut(z_at)
+
     def quarters(cut):
-        return [cut(z_at)] + [shift(cut((z_at + by) % n_z), "z", by) for by in range(1, n_z)]
+        return [moved(cut, by) for by in range(n_z)]
 
     def rows_at(matrix, at):
         return lax.dynamic_slice_in_dim(matrix, at * quarter, quarter, matrix.ndim - 2)
@@ -215,9 +225,9 @@
     def all_rows(pieces):
         return lax.all_gather(jnp.concatenate(pieces, axis=1), ROWS, axis=0, tiled=True)
 
-    inverse_0 = all_rows(quarters(lambda at: rows_at(diag_inverse[0], at)))
-    later = quarters(lambda at: jnp.stack([rows_at(lower_block, at), rows_at(diag_inverse[1], at)]))
-
+    matrices = (diag_inverse[0], lower_block, diag_inverse[1])
+    pieces = quarters(lambda at: jnp.stack([rows_at(m, at) for m in matrices]))
+    inverse_0, below, inverse_1 = (all_rows([v[i] for v in pieces]) for i in range(3))
     outgoing = lax.dot_general(
         to_runs, gram_slots[0:2], (((1,), (2,)), ((), ())), precision=HIGHEST, preferred_element_type=F32
     )
@@ -233,8 +243,6 @@
     rhs = dot(sub_gram.reshape(n_cols * slab_slots, 2 * sub), from_owner, ((0,), (0,)), HIGHEST)
     rhs = rhs.reshape(2, sub, slab)
 
-    below = all_rows([v[0] for v in later])
-    inverse_1 = all_rows([v[1] for v in later])
     where_z = z_at.astype(jnp.int32).reshape(1)
 
     def spread_z(block):
@@ -264,34 +272,44 @@
         piece = jnp.where(core == 0, jnp.concatenate(moved, axis=1), jnp.concatenate(moved[::-1], axis=1))
         return lax.all_gather(piece, COLS, axis=0, tiled=False)
 
-    first = product(inverse_0, spread_z(rhs[0]))
+    def trail_0(at):
+        return jnp.concatenate([rows_at(early[0], at), rows_at(early[1], at)], axis=2)
+
+    def trail_1(at):
+        return rows_at(late, at)
+
+    rhs_pieces = spread_z(rhs[0])
+    early = lax.optimization_barrier((trail_factor[:, 0], gram_slots[2:], rhs_pieces))
+    own_0 = {by: moved(trail_0, by) for by in range(n_z) if by != n_z // 2}
+    first = after(product(inverse_0, rhs_pieces), *own_0.values())
     first_pieces = spread_z(first)
     first_out = solution_rows(first)
+    early = lax.optimization_barrier((trail_factor[:, 0], gram_slots[2:], first_pieces))
+    own_0[n_z // 2] = moved(trail_0, n_z // 2)
+    first_all = [first_pieces] + [shift(first_pieces, "x", -d) for d in range(1, n_x)]
     second_rhs = rhs[1] - product(below, first_pieces)
-
-    factor, trail_gram, _ = lax.optimization_barrier((trail_factor, gram_slots[2:], rhs))
-    own = quarters(
-        lambda at: jnp.concatenate(
-            [rows_at(factor[:, 0], at), rows_at(factor[:, 1], at), rows_at(trail_gram, at)], axis=2
-        )
-    )
-    other = [shift(v, "core", 1) for v in own]
+    second_rhs = after(second_rhs, own_0[n_z // 2], *first_all)
+    second_pieces = spread_z(second_rhs)
+    late = after(trail_factor[:, 1], second_pieces)
+    own_0 = [own_0[by] for by in range(n_z)]
+    own_1 = quarters(trail_1)
+    other_0 = [shift(v, "core", 1) for v in own_0]
+    other_1 = [shift(v, "core", 1) for v in own_1]
+
     trail_owner = col // n_z * n_z + jnp.arange(n_z, dtype=jnp.int32)
     slab_order = ((x_at + jnp.arange(n_x, dtype=jnp.int32)) % n_x * n_core + core)[:, None] * slab
     list_order = (slab_order + jnp.arange(slab, dtype=jnp.int32)[None, :]).reshape(-1)
-    core_lists = lambda v: jnp.take(v, list_order)
     to_lists = (
-        (core_lists(slots_of)[None, None, :] == slot_range[None, :, None])
-        & (core_lists(owners)[None, None, :] == trail_owner[:, None, None])
+        (jnp.take(slots_of, list_order)[None, None, :] == slot_range[None, :, None])
+        & (jnp.take(owners, list_order)[None, None, :] == trail_owner[:, None, None])
     ).astype(BF16)
     where = jnp.stack([x_at, z_at]).astype(jnp.int32)
-    first_all = [first_pieces] + [shift(first_pieces, "x", -d) for d in range(1, n_x)]
-    base = apply_trail(where, own, other, 0, first_all, to_lists, True, n_x, capacity)
-
-    second = product(inverse_1, spread_z(second_rhs))
+    base = apply_trail(where, own_0, other_0, width, first_all, to_lists, True, n_x)
+
+    second = after(product(inverse_1, second_pieces), base, *own_1)
     second_out = solution_rows(second)
     second_all = spread(second, ("x", "z")).reshape(n_x, n_z, n_core, quarter, slab)
-    terms = apply_trail(where, own, other, 1, [second_all], base, False, n_x, capacity)
+    terms = apply_trail(where, own_1, other_1, width, [second_all], base, False, n_x)
     total = jnp.sum(exchange(terms, "y"), axis=0).reshape(n_core, trail_blocks, quarter, slab)
     kept, given = total[0], total[1]
     got = shift(given, "core", 1)

time: 380 us -> 347 us (0.913)
  starting transfers between devices: 115 us -> 68.5 us
  waiting for transfers between devices: 97.9 us -> 123 us
  blocking collectives: 70.9 us -> 63.3 us
  local copies, waits for them, and re-layouts: 24.2 us -> 29.1 us
  Pallas kernels: 39.1 us -> 35.2 us
    ppermute x17 -> x21, starting transfers between devices: 54.7 us -> 19.9 us  [shift(): lax.ppermute(value, axis, [(i, (i + by) % size) for i in range(size)])]
    ppermute x17 -> x21, waiting for transfers between devices: 23.8 us -> 50.6 us  [shift(): lax.ppermute(value, axis, [(i, (i + by) % size) for i in range(size)])]
    all_to_all x8 -> x9, starting transfers between devices: 58.5 us -> 46.9 us  [exchange(): return lax.all_to_all(value, axes, 0, 0, tiled=True)]
    all_to_all x3 -> x2, blocking collectives: 70.9 us -> 63.3 us  [exchange(): return lax.all_to_all(value, axes, 0, 0, tiled=True)]
    squeeze x3 -> x4, local copies, waits for them, and re-layouts: 0.06 us -> 4.51 us  [the longest x1 4.43 us: body(): late = after(trail_factor[:, 1], second_pieces)]
    slice x3 -> x2, local copies, waits for them, and re-layouts: 5.27 us -> 1.33 us  [the longest x1 1.32 us: body(): matrices = (diag_inverse[0], lower_block, diag_inverse[1])]
    all_to_all x8 -> x9, waiting for transfers between devices: 72.8 us -> 69.7 us  [exchange(): return lax.all_to_all(value, axes, 0, 0, tiled=True)]
  transfers between devices with their start and end apart: 34 -> 39, of which waited for: 14 -> 22; matrix products, arithmetic and copies ran while one was open for 9% -> 10% of each run, Pallas kernels for 10% -> 10%
where the time goes in v1:
time: 347 us; the launch traced here: 346 us
  waiting for transfers between devices  123 us (35%)
  starting transfers between devices  68.5 us (20%)
  blocking collectives  63.3 us (18%)
  Pallas kernels  35.2 us (10%)
  local copies, waits for them, and re-layouts  29.1 us (8%)
  between operations  14.4 us (4%)
  other arithmetic  10.9 us (3%)
    all_to_all x9, waiting for transfers between devices, exchange(): return lax.all_to_all(value, axes, 0, 0, tiled=True)  69.7 us
    all_to_all x2, blocking collectives, exchange(): return lax.all_to_all(value, axes, 0, 0, tiled=True)  63.3 us
    ppermute x21, waiting for transfers between devices, shift(): lax.ppermute(value, axis, [(i, (i + by) % size) for i in range(size)])  50.6 us
    all_to_all x9, starting transfers between devices, exchange(): return lax.all_to_all(value, axes, 0, 0, tiled=True)  46.9 us
    ppermute x21, starting transfers between devices, shift(): lax.ppermute(value, axis, [(i, (i + by) % size) for i in range(size)])  19.9 us
    pallas_call x2, Pallas kernels, apply_trail(): pl.pallas_call(functools.partial(trail_kernel, n_z, n_x, with_gram, len(l...  18.8 us
    pallas_call x3, Pallas kernels, apply_matrix(): pl.pallas_call(functools.partial(product_kernel, pieces.shape[0]), grid=(...  11.7 us
  transfers between devices with their start and end apart: 39, of which 22 were waited for; matrix products, arithmetic and copies ran while one was open for 10% of the time, Pallas kernels for 10%

profile of v1, /device:TPU:0, one launch (start us, length us, event | category | flops | bytes accessed | tf_op | source)
XLA Modules:
  0.0 346.0 jit_solution(18228767553644477553)
XLA Ops:
  7.3 1.3 fusion.36
  8.8 2.1 collective-permute-start
  10.9 3.7 %collective-permute-start.1 = (f32[3,128,256]{2,1,0:T(8,128)S(1)}, f32[3,128,256]{2,1,0:T(8,128)S(1)}, u32[]{:S(2)}, u32[]{:S(2)}) collective-permute-start(f32[3,128,256]{2,1,0:T(8,128)S(1)} %pad_maximum_fusion.9), channel_id=1, source_target_pairs={{0,2},{1,3},{2,0},{3,1},{4,6},{5,7},{6,4},{7,5},{8,10},{9,11},{10,... | collective-permute-start | bytes 1179656 | tf_op jit(solution)/shard_map/ppermute | solution.py:26
  14.6 1.1 collective-permute-start.2
  15.7 6.4 %collective-permute-done = f32[3,128,256]{2,1,0:T(8,128)S(1)} collective-permute-done((f32[3,128,256]{2,1,0:T(8,128)S(1)}, f32[3,128,256]{2,1,0:T(8,128)S(1)}, u32[]{:S(2)}, u32[]{:S(2)}) %collective-permute-start) | collective-permute-done | bytes 393248 | tf_op jit(solution)/shard_map/ppermute | solution.py:26
  22.2 9.6 %collective-permute-done.1 = f32[3,128,256]{2,1,0:T(8,128)S(1)} collective-permute-done((f32[3,128,256]{2,1,0:T(8,128)S(1)}, f32[3,128,256]{2,1,0:T(8,128)S(1)}, u32[]{:S(2)}, u32[]{:S(2)}) %collective-permute-start.1) | collective-permute-done | bytes 393248 | tf_op jit(solution)/shard_map/ppermute | solution.py:26
  33.7 0.9 pad_maximum_fusion.6
  36.6 18.6 %all_to_all.55 = f32[8,16,2,512]{3,1,2,0:T(8,128)S(1)} all-to-all(f32[8,16,2,512]{3,1,2,0:T(8,128)S(1)} %copy.23), channel_id=1, replica_groups=mesh['x'=4,'core'=2,'y'=4,'z'=4] {'x','core'}, dimensions={0} | all-to-all | bytes 1048576 | tf_op jit(solution)/shard_map/all_to_all | solution.py:30
  55.8 1.2 reshape.340
  57.1 5.6 %all-to-all-start.1 = ((f32[16,16,512]{2,1,0:T(8,128)}), f32[16,16,512]{2,1,0:T(8,128)S(1)}, u32[]{:S(2)}, u32[]{:S(2)}) async-start(f32[16,16,512]{2,1,0:T(8,128)} %reshape.340), calls=%async_computation.1 | async-start | bytes 1048576 | tf_op jit(solution)/shard_map/all_to_all | solution.py:30
  62.8 10.4 %all-to-all-done.1 = f32[16,16,512]{2,1,0:T(8,128)S(1)} async-done(((f32[16,16,512]{2,1,0:T(8,128)}), f32[16,16,512]{2,1,0:T(8,128)S(1)}, u32[]{:S(2)}, u32[]{:S(2)}) %all-to-all-start.1) | async-done | bytes 524320 | tf_op jit(solution)/shard_map/all_to_all | solution.py:30
  74.6 3.5 %all-to-all-start.2 = ((f32[4,256,128]{2,1,0:T(8,128)}), f32[4,256,128]{2,1,0:T(8,128)S(1)}, u32[]{:S(2)}, u32[]{:S(2)}) async-start(f32[4,256,128]{2,1,0:T(8,128)} %broadcast_in_dim.43), calls=%async_computation.2 | async-start | bytes 1048576 | tf_op jit(solution)/shard_map/all_to_all | solution.py:30
  78.1 1.1 slice.79
  79.2 4.4 %slice_bitcast_fusion = (f32[4,512,256]{2,1,0:T(8,128)}, f32[4,512,256]{2,1,0:T(8,128)S(1)}) fusion(f32[4,2,512,256]{3,2,1,0:T(8,128)} %param.11), kind=kLoop, calls=%fused_computation.2 | loop fusion | bytes 8388608 | tf_op jit(solution)/shard_map/squeeze | solution.py:293
  83.6 2.6 all-to-all-done.2
  86.9 1.9 constant_dynamic-slice_fusion.7
  89.0 0.9 pad_maximum_fusion.3
  89.9 1.1 collective-permute-start.4
  91.1 0.9 pad_maximum_fusion.2
  92.0 0.9 collective-permute-start.3
  92.9 3.9 %shard_map.68 = f32[4,256,128]{2,1,0:T(8,128)} custom-call(s32[1]{0:T(128)} %bitcast.at_ref, f32[1024,1024]{1,0:T(8,128)} %all-gather.6.cloned.1.call-done.matrix_ref, f32[4,2,128,128]{3,2,1,0:T(8,128)} %bitcast.107), custom_call_target="tpu_custom_call" | custom-call | flops 805306368 | bytes 4194304 | tf_op jit(solution)/shard_map/pallas_call | solution.py:70
  96.8 4.2 %all-to-all-start.3 = ((f32[4,256,128]{2,1,0:T(8,128)}), f32[4,256,128]{2,1,0:T(8,128)}, u32[]{:S(2)}, u32[]{:S(2)}) async-start(f32[4,256,128]{2,1,0:T(8,128)} %shard_map.68), calls=%async_computation.3 | async-start | bytes 1048576 | tf_op jit(solution)/shard_map/all_to_all | solution.py:30
  101.0 1.0 pad_maximum_fusion.1.refs_4_.refs_12_
  102.0 7.1 %all-to-all-done.3 = f32[4,256,128]{2,1,0:T(8,128)} async-done(((f32[4,256,128]{2,1,0:T(8,128)}), f32[4,256,128]{2,1,0:T(8,128)}, u32[]{:S(2)}, u32[]{:S(2)}) %all-to-all-start.3) | async-done | bytes 524320 | tf_op jit(solution)/shard_map/all_to_all | solution.py:30
  109.1 1.1 reduce_sum.76
  111.1 3.6 %all-to-all-start.4 = ((f32[4,256,128]{2,1,0:T(8,128)}), f32[4,256,128]{2,1,0:T(8,128)S(1)}, u32[]{:S(2)}, u32[]{:S(2)}) async-start(f32[4,256,128]{2,1,0:T(8,128)} %broadcast_in_dim.44), calls=%async_computation.4 | async-start | bytes 1048576 | tf_op jit(solution)/shard_map/all_to_all | solution.py:30
  115.5 1.2 collective-permute-done.6
  117.4 5.4 %all-to-all-done.4 = f32[4,256,128]{2,1,0:T(8,128)S(1)} async-done(((f32[4,256,128]{2,1,0:T(8,128)}), f32[4,256,128]{2,1,0:T(8,128)S(1)}, u32[]{:S(2)}, u32[]{:S(2)}) %all-to-all-start.4) | async-done | bytes 524320 | tf_op jit(solution)/shard_map/all_to_all | solution.py:30
  122.8 1.1 constant_dynamic-slice_fusion.4
  124.7 3.9 %shard_map.69 = f32[4,256,128]{2,1,0:T(8,128)} custom-call(s32[1]{0:T(128)} %bitcast.at_ref, f32[1024,1024]{1,0:T(8,128)} %all-gather.12.cloned.1.call-done.matrix_ref, f32[4,2,128,128]{3,2,1,0:T(8,128)} %bitcast.96), custom_call_target="tpu_custom_call" | custom-call | flops 805306368 | bytes 4194304 | tf_op jit(solution)/shard_map/pallas_call | solution.py:70
  128.6 12.9 %all-to-all-start.5 = ((f32[4,256,128]{2,1,0:T(8,128)}), f32[4,256,128]{2,1,0:T(8,128)S(1)}, u32[]{:S(2)}, u32[]{:S(2)}) async-start(f32[4,256,128]{2,1,0:T(8,128)} %shard_map.69), calls=%async_computation.5 | async-start | bytes 1048576 | tf_op jit(solution)/shard_map/all_to_all | solution.py:30
  141.6 2.3 gather_fusion
  143.9 2.3 gather_fusion.1
  146.3 3.2 collective-permute-start.8
  150.4 1.2 all-to-all-done.5
  151.6 10.3 %collective-permute-done.10.refs_3_ = f32[4,2,128,128]{3,2,1,0:T(8,128)S(1)} collective-permute-done((f32[4,2,128,128]{3,2,1,0:T(8,128)S(1)}, f32[4,2,128,128]{3,2,1,0:T(8,128)S(1)}, u32[]{:S(2)}, u32[]{:S(2)}) %collective-permute-start.10) | collective-permute-done | bytes 524320 | tf_op jit(solution)/shard_map/ppermute | solution.py:26
  161.9 10.0 %collective-permute-done.8.refs_1_ = f32[4,2,128,128]{3,2,1,0:T(8,128)} collective-permute-done((f32[4,2,128,128]{3,2,1,0:T(8,128)S(1)}, f32[4,2,128,128]{3,2,1,0:T(8,128)}, u32[]{:S(2)}, u32[]{:S(2)}) %collective-permute-start.8) | collective-permute-done | bytes 524320 | tf_op jit(solution)/shard_map/ppermute | solution.py:26
  171.9 1.4 collective-permute-done.9.refs_2_
  174.1 3.5 %all-to-all-start.6 = ((f32[4,256,128]{2,1,0:T(8,128)}), f32[4,256,128]{2,1,0:T(8,128)S(1)}, u32[]{:S(2)}, u32[]{:S(2)}) async-start(f32[4,256,128]{2,1,0:T(8,128)} %broadcast_in_dim.45), calls=%async_computation.6 | async-start | bytes 1048576 | tf_op jit(solution)/shard_map/all_to_all | solution.py:30
  178.9 11.6 %all-to-all-done.6 = f32[4,256,128]{2,1,0:T(8,128)S(1)} async-done(((f32[4,256,128]{2,1,0:T(8,128)}), f32[4,256,128]{2,1,0:T(8,128)S(1)}, u32[]{:S(2)}, u32[]{:S(2)}) %all-to-all-start.6) | async-done | bytes 524320 | tf_op jit(solution)/shard_map/all_to_all | solution.py:30
  191.3 3.9 %shard_map.70 = f32[4,256,128]{2,1,0:T(8,128)} custom-call(s32[1]{0:T(128)} %bitcast.at_ref, f32[1024,1024]{1,0:T(8,128)} %all-gather.10.cloned.1.call-done.matrix_ref, f32[4,2,128,128]{3,2,1,0:T(8,128)} %bitcast.108), custom_call_target="tpu_custom_call" | custom-call | flops 805306368 | bytes 4194304 | tf_op jit(solution)/shard_map/pallas_call | solution.py:70
  195.2 3.5 %all-to-all-start.7 = ((f32[4,256,128]{2,1,0:T(8,128)}), f32[4,256,128]{2,1,0:T(8,128)S(1)}, u32[]{:S(2)}, u32[]{:S(2)}) async-start(f32[4,256,128]{2,1,0:T(8,128)} %shard_map.70), calls=%async_computation.7 | async-start | bytes 1048576 | tf_op jit(solution)/shard_map/all_to_all | solution.py:30
  198.6 1.4 constant_dynamic-slice_fusion
  200.7 2.2 collective-permute-start.16
  202.9 1.8 collective-permute-start.17
  204.7 0.9 and_convert_fusion.refs_20_
  205.6 2.3 all-to-all-done.7
  207.9 10.5 %shard_map.71.refs_9_ = f32[4,1024,128]{2,1,0:T(8,128)} custom-call(s32[2]{0:T(128)} %pad_add_fusion.at_ref, f32[4,2,128,128]{3,2,1,0:T(8,128)} %bitcast.97, f32[4,2,128,128]{3,2,1,0:T(8,128)} %collective-permute-done.8.refs_1_, f32[4,2,128,128]{3,2,1,0:T(8,128)} %collective-permute-done.9.refs_2_, f32[4,2,128,128]{3,2,1,0:T(8,128)} %copy-done.10, ...), custom_call_target="tpu_custom_call" | custom-call | flops 3221225472 | bytes 12582912 | tf_op jit(solution)/shard_map/pallas_call | solution.py:139
  218.5 7.4 %collective-permute-done.15.refs_2_ = f32[4,128,256]{2,1,0:T(8,128)S(1)} collective-permute-done((f32[4,128,256]{2,1,0:T(8,128)}, f32[4,128,256]{2,1,0:T(8,128)S(1)}, u32[]{:S(2)}, u32[]{:S(2)}) %collective-permute-start.15) | collective-permute-done | bytes 524320 | tf_op jit(solution)/shard_map/ppermute | solution.py:26
  226.7 1.5 broadcast_in_dim.48
  228.2 6.1 %all-to-all-start.8 = ((f32[16,256,128]{2,1,0:T(8,128)}), f32[16,256,128]{2,1,0:T(8,128)S(1)}, u32[]{:S(2)}, u32[]{:S(2)}) async-start(f32[16,256,128]{2,1,0:T(8,128)} %broadcast_in_dim.48), calls=%async_computation.8 | async-start | bytes 4194304 | tf_op jit(solution)/shard_map/all_to_all | solution.py:30
  235.2 1.2 collective-permute-done.19
  238.3 0.9 collective-permute-done.20.refs_5_
  239.1 2.2 collective-permute-done.21.refs_6_
  243.0 24.2 %all-to-all-done.8 = f32[16,256,128]{2,1,0:T(8,128)S(1)} async-done(((f32[16,256,128]{2,1,0:T(8,128)}), f32[16,256,128]{2,1,0:T(8,128)S(1)}, u32[]{:S(2)}, u32[]{:S(2)}) %all-to-all-start.8) | async-done | bytes 2097184 | tf_op jit(solution)/shard_map/all_to_all | solution.py:30
  267.2 1.3 copy-done.4
  268.5 8.3 %shard_map.73 = f32[4,1024,128]{2,1,0:T(8,128)} custom-call(s32[2]{0:T(128)} %pad_add_fusion.at_ref, f32[4,4,2,128,128]{4,3,2,1,0:T(8,128)} %bitcast.101, f32[4,128,256]{2,1,0:T(8,128)} %get-tuple-element.26.refs_1_, f32[4,128,256]{2,1,0:T(8,128)} %copy-done.14, f32[4,128,256]{2,1,0:T(8,128)} %copy-done.15, f32[4,128,256]{2,1,0:T(8,128)} %copy-done.16, ...), custom_call_target="tpu_custom_call" | custom-call | flops 3221225472 | bytes 12582912 | tf_op jit(solution)/shard_map/pallas_call | solution.py:139
  276.8 44.7 %all_to_all.56 = f32[4,1024,128]{2,1,0:T(8,128)S(1)} all-to-all(f32[4,1024,128]{2,1,0:T(8,128)} %shard_map.73), channel_id=1, replica_groups=mesh['x'=4,'core'=2,'y'=4,'z'=4] {'y'}, dimensions={0} | all-to-all | bytes 4194304 | tf_op jit(solution)/shard_map/all_to_all | solution.py:30
  321.8 1.5 collective-permute-done.24
  323.6 1.1 copy.27
  324.8 4.1 %all-to-all-start.10 = ((f32[4,4,128,64]{2,3,1,0:T(8,128)}), f32[4,4,128,64]{2,3,1,0:T(8,128)S(1)}, u32[]{:S(2)}, u32[]{:S(2)}) async-start(f32[4,4,128,64]{2,3,1,0:T(8,128)} %bitcast.44), calls=%async_computation.10 | async-start | bytes 1048576 | tf_op jit(solution)/shard_map/all_to_all | solution.py:30
  328.8 4.7 %shard_map.72 = f32[2,512,1024]{2,1,0:T(8,128)} custom-call(f32[4,4,128,256]{3,2,1,0:T(8,128)} %bitcast.105, f32[4,4,128,256]{3,2,1,0:T(8,128)} %bitcast.106), custom_call_target="tpu_custom_call" | custom-call | tf_op jit(solution)/shard_map/pallas_call | solution.py:161
  333.5 5.1 %all-to-all-done.10 = f32[4,4,128,64]{2,3,1,0:T(8,128)S(1)} async-done(((f32[4,4,128,64]{2,3,1,0:T(8,128)}), f32[4,4,128,64]{2,3,1,0:T(8,128)S(1)}, u32[]{:S(2)}, u32[]{:S(2)}) %all-to-all-start.10) | async-done | bytes 524320 | tf_op jit(solution)/shard_map/all_to_all | solution.py:30
  338.6 0.9 copy_bitcast_fusion
  (140 shorter events, 20.7 us)
Async XLA Ops:
  7.2 1.4 copy-start.11
  7.2 85.7 %all-gather.6.cloned.1.call-start = ((), (), s32[]{:S(2)}) async-start(), calls=%async_computation.11 | async-start | bytes 4718592 | tf_op jit(solution)/shard_map/all_gather | solution.py:226
  8.8 13.3 %collective-permute-start = (f32[3,128,256]{2,1,0:T(8,128)S(1)}, f32[3,128,256]{2,1,0:T(8,128)S(1)}, u32[]{:S(2)}, u32[]{:S(2)}) collective-permute-start(f32[3,128,256]{2,1,0:T(8,128)S(1)} %pad_maximum_fusion.8), channel_id=1, source_target_pairs={{0,1},{1,2},{2,3},{3,0},{4,5},{5,6},{6,7},{7,4},{8,9},{9,10},{10,1... | collective-permute-start | bytes 1179656 | tf_op jit(solution)/shard_map/ppermute | solution.py:26
  10.9 20.8 %collective-permute-start.1 = (f32[3,128,256]{2,1,0:T(8,128)S(1)}, f32[3,128,256]{2,1,0:T(8,128)S(1)}, u32[]{:S(2)}, u32[]{:S(2)}) collective-permute-start(f32[3,128,256]{2,1,0:T(8,128)S(1)} %pad_maximum_fusion.9), channel_id=1, source_target_pairs={{0,2},{1,3},{2,0},{3,1},{4,6},{5,7},{6,4},{7,5},{8,10},{9,11},{10,... | collective-permute-start | bytes 1179656 | tf_op jit(solution)/shard_map/ppermute | solution.py:26
  14.6 17.1 %collective-permute-start.2 = (f32[3,128,256]{2,1,0:T(8,128)S(1)}, f32[3,128,256]{2,1,0:T(8,128)S(1)}, u32[]{:S(2)}, u32[]{:S(2)}) collective-permute-start(f32[3,128,256]{2,1,0:T(8,128)S(1)} %pad_maximum_fusion.10), channel_id=1, source_target_pairs={{0,3},{1,0},{2,1},{3,2},{4,7},{5,4},{6,5},{7,6},{8,11},{9,8},{10,9... | collective-permute-start | bytes 1179656 | tf_op jit(solution)/shard_map/ppermute | solution.py:26
  32.7 1.9 copy-start.13
  32.7 3.3 copy-start.7
  32.7 92.0 %all-gather.12.cloned.1.call-start = ((), (), s32[]{:S(2)}) async-start(), calls=%async_computation.14 | async-start | bytes 4718592 | tf_op jit(solution)/shard_map/all_gather | solution.py:226
  33.6 156.9 %all-gather.10.cloned.1.call-start = ((), (), s32[]{:S(2)}) async-start(), calls=%async_computation.13 | async-start | bytes 4718592 | tf_op jit(solution)/shard_map/all_gather | solution.py:226
  57.1 16.1 %all-to-all-start.1 = ((f32[16,16,512]{2,1,0:T(8,128)}), f32[16,16,512]{2,1,0:T(8,128)S(1)}, u32[]{:S(2)}, u32[]{:S(2)}) async-start(f32[16,16,512]{2,1,0:T(8,128)} %reshape.340), calls=%async_computation.1 | async-start | bytes 1048576 | tf_op jit(solution)/shard_map/all_to_all | solution.py:30
  73.7 9.9 %copy-start.8 = (f32[512,128]{1,0:T(8,128)}, f32[512,128]{1,0:T(8,128)S(1)}, u32[]{:S(2)}) copy-start(f32[512,128]{1,0:T(8,128)S(1)} %fusion.12) | copy-start | bytes 786436
  74.6 11.5 %all-to-all-start.2 = ((f32[4,256,128]{2,1,0:T(8,128)}), f32[4,256,128]{2,1,0:T(8,128)S(1)}, u32[]{:S(2)}, u32[]{:S(2)}) async-start(f32[4,256,128]{2,1,0:T(8,128)} %broadcast_in_dim.43), calls=%async_computation.2 | async-start | bytes 1048576 | tf_op jit(solution)/shard_map/all_to_all | solution.py:30
  86.2 0.8 copy-start.5
  89.9 20.3 %collective-permute-start.4 = (f32[4,128,384]{2,1,0:T(8,128)}, f32[4,128,384]{2,1,0:T(8,128)}, u32[]{:S(2)}, u32[]{:S(2)}) collective-permute-start(f32[4,128,384]{2,1,0:T(8,128)} %pad_maximum_fusion.3), channel_id=1, source_target_pairs={{0,3},{1,0},{2,1},{3,2},{4,7},{5,4},{6,5},{7,6},{8,11},{9,8},{10,9... | collective-permute-start | bytes 2359304 | tf_op jit(solution)/shard_map/ppermute | solution.py:26
  92.0 18.2 %collective-permute-start.3 = (f32[4,128,384]{2,1,0:T(8,128)}, f32[4,128,384]{2,1,0:T(8,128)}, u32[]{:S(2)}, u32[]{:S(2)}) collective-permute-start(f32[4,128,384]{2,1,0:T(8,128)} %pad_maximum_fusion.2), channel_id=1, source_target_pairs={{0,1},{1,2},{2,3},{3,0},{4,5},{5,6},{6,7},{7,4},{8,9},{9,10},{10,1... | collective-permute-start | bytes 2359304 | tf_op jit(solution)/shard_map/ppermute | solution.py:26
  96.8 12.3 %all-to-all-start.3 = ((f32[4,256,128]{2,1,0:T(8,128)}), f32[4,256,128]{2,1,0:T(8,128)}, u32[]{:S(2)}, u32[]{:S(2)}) async-start(f32[4,256,128]{2,1,0:T(8,128)} %shard_map.68), calls=%async_computation.3 | async-start | bytes 1048576 | tf_op jit(solution)/shard_map/all_to_all | solution.py:30
  102.0 48.3 %copy-start.1 = (f32[4,128,384]{2,1,0:T(8,128)}, f32[4,128,384]{2,1,0:T(8,128)S(1)}, u32[]{:S(2)}) copy-start(f32[4,128,384]{2,1,0:T(8,128)S(1)} %pad_maximum_fusion.1.refs_4_.refs_12_) | copy-start | bytes 2359300
  111.1 11.7 %all-to-all-start.4 = ((f32[4,256,128]{2,1,0:T(8,128)}), f32[4,256,128]{2,1,0:T(8,128)S(1)}, u32[]{:S(2)}, u32[]{:S(2)}) async-start(f32[4,256,128]{2,1,0:T(8,128)} %broadcast_in_dim.44), calls=%async_computation.4 | async-start | bytes 1048576 | tf_op jit(solution)/shard_map/all_to_all | solution.py:30
  114.7 214.1 %all-gather.8.cloned.1.call-start = ((), (), s32[]{:S(2)}) async-start(), calls=%async_computation.12 | async-start | bytes 2228224 | tf_op jit(solution)/shard_map/all_gather | solution.py:273
  114.7 0.8 collective-permute-start.5
  115.4 1.3 collective-permute-start.6
  122.8 2.0 copy-start.2
  124.0 49.3 %collective-permute-start.7 = (f32[4,128,384]{2,1,0:T(8,128)S(1)}, f32[4,128,384]{2,1,0:T(8,128)}, u32[]{:S(2)}, u32[]{:S(2)}) collective-permute-start(f32[4,128,384]{2,1,0:T(8,128)S(1)} %pad_maximum_fusion.4), channel_id=1, source_target_pairs={{0,2},{1,3},{2,0},{3,1},{4,6},{5,7},{6,4},{7,5},{8,10},{9,11},{10,... | collective-permute-start | bytes 2359304 | tf_op jit(solution)/shard_map/ppermute | solution.py:26
  128.6 23.0 %all-to-all-start.5 = ((f32[4,256,128]{2,1,0:T(8,128)}), f32[4,256,128]{2,1,0:T(8,128)S(1)}, u32[]{:S(2)}, u32[]{:S(2)}) async-start(f32[4,256,128]{2,1,0:T(8,128)} %shard_map.69), calls=%async_computation.5 | async-start | bytes 1048576 | tf_op jit(solution)/shard_map/all_to_all | solution.py:30
  141.6 4.6 %copy-start.3 = (f32[4,256,128]{2,1,0:T(8,128)S(1)}, f32[4,256,128]{2,1,0:T(8,128)}, u32[]{:S(2)}) copy-start(f32[4,256,128]{2,1,0:T(8,128)} %copy-done.2) | copy-start | bytes 1572868
  141.6 10.0 %copy-start.9 = (f32[512,128]{1,0:T(8,128)S(1)}, f32[512,128]{1,0:T(8,128)}, u32[]{:S(2)}) copy-start(f32[512,128]{1,0:T(8,128)} %copy-done.8) | copy-start | bytes 786436
  146.2 15.7 %collective-permute-start.10 = (f32[4,2,128,128]{3,2,1,0:T(8,128)S(1)}, f32[4,2,128,128]{3,2,1,0:T(8,128)S(1)}, u32[]{:S(2)}, u32[]{:S(2)}) collective-permute-start(f32[4,2,128,128]{3,2,1,0:T(8,128)S(1)} %bitcast.98), channel_id=1, source_target_pairs={{0,32},{32,64},{64,96},{96,0},{1,33},{33,65},{65,97},{97,1},{2,34}... | collective-permute-start | bytes 1572872 | tf_op jit(solution)/shard_map/ppermute | solution.py:26
  146.3 25.6 %collective-permute-start.8 = (f32[4,2,128,128]{3,2,1,0:T(8,128)S(1)}, f32[4,2,128,128]{3,2,1,0:T(8,128)}, u32[]{:S(2)}, u32[]{:S(2)}) collective-permute-start(f32[4,2,128,128]{3,2,1,0:T(8,128)S(1)} %bitcast.99), channel_id=1, source_target_pairs={{0,96},{32,0},{64,32},{96,64},{1,97},{33,1},{65,33},{97,65},{2,98}... | collective-permute-start | bytes 1572872 | tf_op jit(solution)/shard_map/ppermute | solution.py:26
  149.5 23.8 %collective-permute-start.9 = (f32[4,2,128,128]{3,2,1,0:T(8,128)S(1)}, f32[4,2,128,128]{3,2,1,0:T(8,128)}, u32[]{:S(2)}, u32[]{:S(2)}) collective-permute-start(f32[4,2,128,128]{3,2,1,0:T(8,128)S(1)} %bitcast.100), channel_id=1, source_target_pairs={{0,64},{32,96},{64,0},{96,32},{1,65},{33,97},{65,1},{97,33},{2,66}... | collective-permute-start | bytes 1572872 | tf_op jit(solution)/shard_map/ppermute | solution.py:26
  150.3 50.3 %collective-permute-start.11 = (f32[4,128,384]{2,1,0:T(8,128)S(1)}, f32[4,128,384]{2,1,0:T(8,128)}, u32[]{:S(2)}, u32[]{:S(2)}) collective-permute-start(f32[4,128,384]{2,1,0:T(8,128)S(1)} %pad_maximum_fusion.1.refs_4_.refs_12_), channel_id=1, source_target_pairs={{0,16},{16,0},{1,17},{17,1},{2,18},{18,2},{3,19},{19,3},{4,20},{20... | collective-permute-start | bytes 2359304 | tf_op jit(solution)/shard_map/ppermute | solution.py:26
  161.9 28.6 %copy-start.10 = (f32[4,2,128,128]{3,2,1,0:T(8,128)}, f32[4,2,128,128]{3,2,1,0:T(8,128)S(1)}, u32[]{:S(2)}) copy-start(f32[4,2,128,128]{3,2,1,0:T(8,128)S(1)} %collective-permute-done.10.refs_3_) | copy-start | bytes 1572868
  161.9 41.0 %collective-permute-start.14 = (f32[4,128,384]{2,1,0:T(8,128)}, f32[4,128,384]{2,1,0:T(8,128)}, u32[]{:S(2)}, u32[]{:S(2)}) collective-permute-start(f32[4,128,384]{2,1,0:T(8,128)} %collective-permute-done.4.refs_7_.refs_15_), channel_id=1, source_target_pairs={{0,16},{16,0},{1,17},{17,1},{2,18},{18,2},{3,19},{19,3},{4,20},{20... | collective-permute-start | bytes 2359304 | tf_op jit(solution)/shard_map/ppermute | solution.py:26
  174.1 16.4 %all-to-all-start.6 = ((f32[4,256,128]{2,1,0:T(8,128)}), f32[4,256,128]{2,1,0:T(8,128)S(1)}, u32[]{:S(2)}, u32[]{:S(2)}) async-start(f32[4,256,128]{2,1,0:T(8,128)} %broadcast_in_dim.45), calls=%async_computation.6 | async-start | bytes 1048576 | tf_op jit(solution)/shard_map/all_to_all | solution.py:30
  177.7 30.2 %collective-permute-start.12 = (f32[4,128,384]{2,1,0:T(8,128)}, f32[4,128,384]{2,1,0:T(8,128)}, u32[]{:S(2)}, u32[]{:S(2)}) collective-permute-start(f32[4,128,384]{2,1,0:T(8,128)} %collective-permute-done.3.refs_5_.refs_13_), channel_id=1, source_target_pairs={{0,16},{16,0},{1,17},{17,1},{2,18},{18,2},{3,19},{19,3},{4,20},{20... | collective-permute-start | bytes 2359304 | tf_op jit(solution)/shard_map/ppermute | solution.py:26
  177.7 30.2 %collective-permute-start.13 = (f32[4,128,384]{2,1,0:T(8,128)}, f32[4,128,384]{2,1,0:T(8,128)}, u32[]{:S(2)}, u32[]{:S(2)}) collective-permute-start(f32[4,128,384]{2,1,0:T(8,128)} %collective-permute-done.7.refs_6_.refs_14_), channel_id=1, source_target_pairs={{0,16},{16,0},{1,17},{17,1},{2,18},{18,2},{3,19},{19,3},{4,20},{20... | collective-permute-start | bytes 2359304 | tf_op jit(solution)/shard_map/ppermute | solution.py:26
  190.5 0.8 copy-start.6
  190.5 8.1 %copy-start = (f32[4,512,256]{2,1,0:T(8,128)S(1)}, f32[4,512,256]{2,1,0:T(8,128)}, u32[]{:S(2)}) copy-start(f32[4,512,256]{2,1,0:T(8,128)} %get-tuple-element.17) | copy-start | bytes 6291460
  195.2 12.7 %all-to-all-start.7 = ((f32[4,256,128]{2,1,0:T(8,128)}), f32[4,256,128]{2,1,0:T(8,128)S(1)}, u32[]{:S(2)}, u32[]{:S(2)}) async-start(f32[4,256,128]{2,1,0:T(8,128)} %shard_map.70), calls=%async_computation.7 | async-start | bytes 1048576 | tf_op jit(solution)/shard_map/all_to_all | solution.py:30
  200.0 25.8 %collective-permute-start.15 = (f32[4,128,256]{2,1,0:T(8,128)}, f32[4,128,256]{2,1,0:T(8,128)S(1)}, u32[]{:S(2)}, u32[]{:S(2)}) collective-permute-start(f32[4,128,256]{2,1,0:T(8,128)} %get-tuple-element.25), channel_id=1, source_target_pairs={{0,1},{1,2},{2,3},{3,0},{4,5},{5,6},{6,7},{7,4},{8,9},{9,10},{10,1... | collective-permute-start | bytes 1572872 | tf_op jit(solution)/shard_map/ppermute | solution.py:26
  200.7 25.2 %collective-permute-start.16 = (f32[4,128,256]{2,1,0:T(8,128)}, f32[4,128,256]{2,1,0:T(8,128)S(1)}, u32[]{:S(2)}, u32[]{:S(2)}) collective-permute-start(f32[4,128,256]{2,1,0:T(8,128)} %get-tuple-element.24), channel_id=1, source_target_pairs={{0,2},{1,3},{2,0},{3,1},{4,6},{5,7},{6,4},{7,5},{8,10},{9,11},{10,... | collective-permute-start | bytes 1572872 | tf_op jit(solution)/shard_map/ppermute | solution.py:26
  202.9 23.6 %collective-permute-start.17 = (f32[4,128,256]{2,1,0:T(8,128)}, f32[4,128,256]{2,1,0:T(8,128)S(1)}, u32[]{:S(2)}, u32[]{:S(2)}) collective-permute-start(f32[4,128,256]{2,1,0:T(8,128)} %get-tuple-element.23), channel_id=1, source_target_pairs={{0,3},{1,0},{2,1},{3,2},{4,7},{5,4},{6,5},{7,6},{8,11},{9,8},{10,9... | collective-permute-start | bytes 1572872 | tf_op jit(solution)/shard_map/ppermute | solution.py:26
  225.8 11.5 %copy-start.14 = (f32[4,128,256]{2,1,0:T(8,128)}, f32[4,128,256]{2,1,0:T(8,128)S(1)}, u32[]{:S(2)}) copy-start(f32[4,128,256]{2,1,0:T(8,128)S(1)} %collective-permute-done.15.refs_2_) | copy-start | bytes 1572868
  225.8 0.9 copy-start.15
  226.5 1.8 copy-start.16
  228.2 8.9 %copy-start.12 = (f32[4,128,256]{2,1,0:T(8,128)S(1)}, f32[4,128,256]{2,1,0:T(8,128)}, u32[]{:S(2)}) copy-start(f32[4,128,256]{2,1,0:T(8,128)} %get-tuple-element.26.refs_1_) | copy-start | bytes 1572868
  228.2 38.9 %all-to-all-start.8 = ((f32[16,256,128]{2,1,0:T(8,128)}), f32[16,256,128]{2,1,0:T(8,128)S(1)}, u32[]{:S(2)}, u32[]{:S(2)}) async-start(f32[16,256,128]{2,1,0:T(8,128)} %broadcast_in_dim.48), calls=%async_computation.8 | async-start | bytes 4194304 | tf_op jit(solution)/shard_map/all_to_all | solution.py:30
  234.4 94.5 %all-gather.14.cloned.1.call-start = ((), (), s32[]{:S(2)}) async-start(), calls=%async_computation.15 | async-start | bytes 2228224 | tf_op jit(solution)/shard_map/all_gather | solution.py:273
  234.4 0.8 collective-permute-start.18
  235.1 1.3 collective-permute-start.19
  237.2 2.0 collective-permute-start.20
  237.4 4.0 %collective-permute-start.21 = (f32[4,128,256]{2,1,0:T(8,128)S(1)}, f32[4,128,256]{2,1,0:T(8,128)S(1)}, u32[]{:S(2)}, u32[]{:S(2)}) collective-permute-start(f32[4,128,256]{2,1,0:T(8,128)S(1)} %collective-permute-done.15.refs_2_), channel_id=1, source_target_pairs={{0,16},{16,0},{1,17},{17,1},{2,18},{18,2},{3,19},{19,3},{4,20},{20... | collective-permute-start | bytes 1572872 | tf_op jit(solution)/shard_map/ppermute | solution.py:26
  237.7 3.9 %collective-permute-start.22 = (f32[4,128,256]{2,1,0:T(8,128)}, f32[4,128,256]{2,1,0:T(8,128)S(1)}, u32[]{:S(2)}, u32[]{:S(2)}) collective-permute-start(f32[4,128,256]{2,1,0:T(8,128)} %copy-done.15), channel_id=1, source_target_pairs={{0,16},{16,0},{1,17},{17,1},{2,18},{18,2},{3,19},{19,3},{4,20},{20... | collective-permute-start | bytes 1572872 | tf_op jit(solution)/shard_map/ppermute | solution.py:26
  237.9 5.1 %collective-permute-start.23 = (f32[4,128,256]{2,1,0:T(8,128)}, f32[4,128,256]{2,1,0:T(8,128)}, u32[]{:S(2)}, u32[]{:S(2)}) collective-permute-start(f32[4,128,256]{2,1,0:T(8,128)} %copy-done.16), channel_id=1, source_target_pairs={{0,16},{16,0},{1,17},{17,1},{2,18},{18,2},{3,19},{19,3},{4,20},{20... | collective-permute-start | bytes 1572872 | tf_op jit(solution)/shard_map/ppermute | solution.py:26
  239.1 2.5 copy-start.17
  241.4 0.8 copy-start.18
  242.2 0.8 copy-start.19
  267.2 1.3 copy-start.4
  321.7 1.6 collective-permute-start.24
  324.8 13.8 %all-to-all-start.10 = ((f32[4,4,128,64]{2,3,1,0:T(8,128)}), f32[4,4,128,64]{2,3,1,0:T(8,128)S(1)}, u32[]{:S(2)}, u32[]{:S(2)}) async-start(f32[4,4,128,64]{2,3,1,0:T(8,128)} %bitcast.44), calls=%async_computation.10 | async-start | bytes 1048576 | tf_op jit(solution)/shard_map/all_to_all | solution.py:30
Sparse Core Ops, SparseCore 0:
  32.8 36.4 all-gather.5
  71.0 31.1 all-gather.11
  103.9 36.2 all-gather.9
  142.2 46.5 all-gather.7
  237.3 84.0 all-gather.13

commit v2 on v1

--- a/solution.py
+++ b/solution.py
@@ -62,6 +62,38 @@
         term = both[:, :slab] + (both[:, slab:] + jnp.dot(left[1], high, preferred_element_type=F32))
         total = term if total is None else total + term
     out_ref[...] = total.reshape(out_ref.shape)
+
+
+def first_kernel(n_z, n_core, matrix_ref, operand_ref, out_ref):
+    high, low = split(operand_ref[...])
+    slab = operand_ref.shape[-1]
+    left = split(matrix_ref[...])
+    both = jnp.dot(left[0], jnp.concatenate([high, low], axis=1), preferred_element_type=F32)
+    total = both[:, :slab] + (both[:, slab:] + jnp.dot(left[1], high, preferred_element_type=F32))
+    quarter = out_ref.shape[-2]
+    for k in range(n_core):
+        for z in range(n_z):
+            at = (k * n_z + z) * quarter
+            out_ref[0, z, k] = total[at : at + quarter]
+
+
+def apply_first(matrix, operand, n_y, n_z, n_core):
+    rows, width = matrix.shape
+    slab = operand.shape[1]
+    quarter = rows // (n_y * n_z * n_core)
+    return pl.pallas_call(
+        functools.partial(first_kernel, n_z, n_core),
+        grid=(n_y,),
+        in_specs=[
+            pl.BlockSpec((rows // n_y, width), lambda i: (i, 0)),
+            pl.BlockSpec(operand.shape, lambda i: (0, 0)),
+        ],
+        out_specs=pl.BlockSpec((1, n_z, n_core, quarter, slab), lambda i: (i, 0, 0, 0, 0)),
+        out_shape=jax.ShapeDtypeStruct((n_y, n_z, n_core, quarter, slab), F32),
+        cost_estimate=pl.CostEstimate(
+            flops=6 * rows * width * slab, bytes_accessed=4 * rows * width, transcendentals=0
+        ),
+    )(matrix, operand)
 
 
 def apply_matrix(at_z, matrix, pieces, n_y):
@@ -89,37 +121,38 @@
     factor = refs[: 2 * n_z]
     refs = refs[2 * n_z :]
     gram = refs[: 2 * n_z] if with_gram else ()
-    start_ref, out_ref = refs[len(gram) :]
+    start_ref, out_ref, high_ref, low_ref, chosen_ref = refs[len(gram) :]
     at_x, at_z = at_ref[0], at_ref[1]
-    blocks, quarter, _ = factor[0].shape
+    width = factor[0].shape[-1]
+    slots = start_ref.shape[1] if with_gram else 0
     slab = out_ref.shape[-1]
-    half = blocks * quarter
-    operands = []
-    for by in range(n_z):
-        cols = [
-            band_rows(lists[0], (i,), at_z, by, n_z) if one_list else band_rows(lists[i], (), at_z, by, n_z)
-            for i in range(n_x)
-        ]
-        operands.append(split(jnp.concatenate(cols, axis=1)))
-    for side in range(2):
-        total = None
+
+    @pl.when(pl.program_id(0) == 0)
+    def _():
         for by in range(n_z):
-            piece = factor[side * n_z + by][...]
-            term = mul(split(piece.reshape(half, piece.shape[-1])), operands[by])
-            total = term if total is None else total + term
-        placed = None
-        for by in range(n_z if with_gram else 0):
-            piece = gram[side * n_z + by][...]
-            high, low = split(piece.reshape(half, piece.shape[-1]))
-            chosen = start_ref[lax.rem(at_z + n_z - by, n_z)]
-            term = jnp.dot(high, chosen, preferred_element_type=F32) + jnp.dot(low, chosen, preferred_element_type=F32)
-            placed = term if placed is None else placed + term
-        for i in range(n_x):
-            at = i if one_list else lax.rem(at_x + i, n_x)
-            mine = slice(i * slab, (i + 1) * slab)
-            into = pl.ds(side * half, half)
-            first = placed[:, mine] if with_gram else start_ref[at, into, :]
-            out_ref[at, into, :] = first - total[:, mine]
+            for i in range(n_x):
+                rows = band_rows(lists[0] if one_list else lists[i], (i,) if one_list else (), at_z, by, n_z)
+                into = slice(by * width, (by + 1) * width), slice(i * slab, (i + 1) * slab)
+                high_ref[into], low_ref[into] = split(rows)
+            if with_gram:
+                chosen_ref[by * slots : (by + 1) * slots, :] = start_ref[lax.rem(at_z + n_z - by, n_z)]
+
+    def left(pieces):
+        sides = [jnp.concatenate([v[0] for v in pieces[side * n_z :][:n_z]], axis=1) for side in range(2)]
+        return split(jnp.concatenate(sides, axis=0))
+
+    total = mul(left(factor), (high_ref[...], low_ref[...]))
+    if with_gram:
+        high, low = left(gram)
+        chosen = chosen_ref[...]
+        placed = jnp.dot(high, chosen, preferred_element_type=F32) + jnp.dot(low, chosen, preferred_element_type=F32)
+        total = placed - total
+    half = total.shape[0] // 2
+    for i in range(n_x):
+        at = i if one_list else lax.rem(at_x + i, n_x)
+        for side in range(2):
+            part = total[side * half : (side + 1) * half, i * slab : (i + 1) * slab]
+            out_ref[at, side, 0] = part if with_gram else start_ref[at, side, 0] - part
 
 
 def apply_trail(where, own, other, width, lists, start, with_gram, n_x):
@@ -128,22 +161,28 @@
     slots = depth - width
     slab = lists[0].shape[-1]
     whole = lambda v: pl.BlockSpec(v.shape, lambda *_: (0,) * v.ndim)
-    part = pl.BlockSpec((blocks, quarter, width), lambda *_: (0, 0, 0))
+    part = pl.BlockSpec((1, quarter, width), lambda t: (t, 0, 0))
+    ends = pl.BlockSpec((n_x, 2, 1, quarter, slab), lambda t: (0, 0, t, 0, 0))
     pieces = [*own, *other]
     specs = [SMEM] + [whole(v) for v in lists] + [part] * (2 * n_z)
     args = [where, *lists, *pieces]
     if with_gram:
-        specs += [pl.BlockSpec((blocks, quarter, slots), lambda *_: (0, 0, width // slots))] * (2 * n_z)
+        specs += [pl.BlockSpec((1, quarter, slots), lambda t: (t, 0, width // slots))] * (2 * n_z)
         args += pieces
-    rows = 2 * blocks * quarter
+    band, n_list = n_z * width, n_x * slab
     return pl.pallas_call(
         functools.partial(trail_kernel, n_z, n_x, with_gram, len(lists) == 1),
-        grid=(1,),
-        in_specs=specs + [whole(start)],
-        out_specs=pl.BlockSpec((n_x, rows, slab), lambda *_: (0, 0, 0)),
-        out_shape=jax.ShapeDtypeStruct((n_x, rows, slab), F32),
+        grid=(blocks,),
+        in_specs=specs + [whole(start) if with_gram else ends],
+        out_specs=ends,
+        out_shape=jax.ShapeDtypeStruct((n_x, 2, blocks, quarter, slab), F32),
+        scratch_shapes=[
+            pltpu.VMEM((band, n_list), BF16),
+            pltpu.VMEM((band, n_list), BF16),
+            pltpu.VMEM((n_z * max(slots, 16), n_list), BF16),
+        ],
         cost_estimate=pl.CostEstimate(
-            flops=6 * rows * n_z * width * n_x * slab, bytes_accessed=12 * 2**20, transcendentals=0
+            flops=12 * blocks * quarter * band * n_list, bytes_accessed=10 * 2**20, transcendentals=0
         ),
     )(*args, start)
 
@@ -225,23 +264,28 @@
     def all_rows(pieces):
         return lax.all_gather(jnp.concatenate(pieces, axis=1), ROWS, axis=0, tiled=True)
 
-    matrices = (diag_inverse[0], lower_block, diag_inverse[1])
-    pieces = quarters(lambda at: jnp.stack([rows_at(m, at) for m in matrices]))
-    inverse_0, below, inverse_1 = (all_rows([v[i] for v in pieces]) for i in range(3))
+    inverse_0 = lax.all_gather(diag_inverse[0], ROWS, axis=0, tiled=True)
+
     outgoing = lax.dot_general(
         to_runs, gram_slots[0:2], (((1,), (2,)), ((), ())), precision=HIGHEST, preferred_element_type=F32
     )
+    blocks = after(jnp.stack([lower_block, diag_inverse[1]]), outgoing)
+    pieces = quarters(lambda at: rows_at(blocks, at))
     slab_gram = exchange(outgoing.reshape(n_rows, slab_slots, 2, block_rows), ROWS)
-    slab_gram = slab_gram.reshape(n_y, n_core, slab_slots, 2, n_z, quarter).transpose(0, 4, 2, 3, 1, 5)
-    sub_gram = exchange(slab_gram.reshape(n_cols, slab_slots, 2 * sub), COLS)
+    pieces = list(lax.optimization_barrier((*pieces, slab_gram)))[:-1]
+    below, inverse_1 = (all_rows([v[i] for v in pieces]) for i in range(2))
+    by_width = slab_gram[:, :, 0].reshape(n_rows, slab_slots, block_rows // width, width)
+    by_width = by_width.transpose(0, 2, 1, 3).reshape(n_cols, slab_slots, width)
+    by_sub = slab_gram[:, :, 1].reshape(n_y, n_core, slab_slots, n_z, quarter).transpose(0, 3, 2, 1, 4)
+    by_sub = by_sub.reshape(n_cols, slab_slots, sub)
+    sub_gram = exchange(jnp.concatenate([by_width, by_sub], axis=2), COLS)
     slab_owner = lax.dynamic_slice_in_dim(owners, row * slab, slab)
     slab_rank = lax.dynamic_slice_in_dim(pair_rank, row * slab, slab)
     slab_slot = jnp.arange(slab, dtype=jnp.int32) // run_len * per_run + slab_rank
     from_owner = (
         jnp.arange(n_cols * slab_slots, dtype=jnp.int32)[:, None] == (slab_owner * slab_slots + slab_slot)[None, :]
     ).astype(F32)
-    rhs = dot(sub_gram.reshape(n_cols * slab_slots, 2 * sub), from_owner, ((0,), (0,)), HIGHEST)
-    rhs = rhs.reshape(2, sub, slab)
+    rhs = dot(sub_gram.reshape(n_cols * slab_slots, width + sub), from_owner, ((0,), (0,)), HIGHEST)
 
     where_z = z_at.astype(jnp.int32).reshape(1)
 
@@ -278,21 +322,25 @@
     def trail_1(at):
         return rows_at(late, at)
 
-    rhs_pieces = spread_z(rhs[0])
-    early = lax.optimization_barrier((trail_factor[:, 0], gram_slots[2:], rhs_pieces))
-    own_0 = {by: moved(trail_0, by) for by in range(n_z) if by != n_z // 2}
-    first = after(product(inverse_0, rhs_pieces), *own_0.values())
+    first = jnp.sum(
+        exchange(apply_first(inverse_0, rhs[:width], n_y, n_z, n_core).reshape(n_cols, sub, slab), COLS), axis=0
+    )
     first_pieces = spread_z(first)
     first_out = solution_rows(first)
     early = lax.optimization_barrier((trail_factor[:, 0], gram_slots[2:], first_pieces))
+    own_0 = {by: moved(trail_0, by) for by in range(n_z) if by != n_z // 2}
+    first_all = [first_pieces] + [shift(first_pieces, "x", -d) for d in range(1, n_x)]
+    second_rhs = rhs[width:] - product(below, first_pieces)
+    second_rhs = after(second_rhs, *own_0.values())
+    second_pieces = spread_z(second_rhs)
+    early = lax.optimization_barrier((trail_factor[:, 0], gram_slots[2:], second_pieces))
+    late = after(trail_factor[:, 1], second_pieces)
     own_0[n_z // 2] = moved(trail_0, n_z // 2)
-    first_all = [first_pieces] + [shift(first_pieces, "x", -d) for d in range(1, n_x)]
-    second_rhs = rhs[1] - product(below, first_pieces)
-    second_rhs = after(second_rhs, own_0[n_z // 2], *first_all)
-    second_pieces = spread_z(second_rhs)
-    late = after(trail_factor[:, 1], second_pieces)
     own_0 = [own_0[by] for by in range(n_z)]
-    own_1 = quarters(trail_1)
+    own_1 = {by: moved(trail_1, by) for by in range(n_z) if by != n_z // 2}
+    late = after(trail_factor[:, 1], outgoing)
+    own_1[n_z // 2] = after(moved(trail_1, n_z // 2), slab_gram)
+    own_1 = [own_1[by] for by in range(n_z)]
     other_0 = [shift(v, "core", 1) for v in own_0]
     other_1 = [shift(v, "core", 1) for v in own_1]
 
@@ -306,7 +354,7 @@
     where = jnp.stack([x_at, z_at]).astype(jnp.int32)
     base = apply_trail(where, own_0, other_0, width, first_all, to_lists, True, n_x)
 
-    second = after(product(inverse_1, second_pieces), base, *own_1)
+    second = after(product(inverse_1, second_pieces), own_0[n_z // 2], *own_1, *first_all)
     second_out = solution_rows(second)
     second_all = spread(second, ("x", "z")).reshape(n_x, n_z, n_core, quarter, slab)
     terms = apply_trail(where, own_1, other_1, width, [second_all], base, False, n_x)

time: 347 us -> 339 us (0.977)
  waiting for transfers between devices: 123 us -> 102 us
  starting transfers between devices: 68.5 us -> 85.3 us
  blocking collectives: 63.3 us -> 58.2 us
    ppermute x21, waiting for transfers between devices: 50.6 us -> 22.3 us  [shift(): lax.ppermute(value, axis, [(i, (i + by) % size) for i in range(size)])]
    ppermute x21, starting transfers between devices: 19.9 us -> 29.5 us  [shift(): lax.ppermute(value, axis, [(i, (i + by) % size) for i in range(size)])]
    all_to_all x9, waiting for transfers between devices: 69.7 us -> 78.2 us  [exchange(): return lax.all_to_all(value, axes, 0, 0, tiled=True)]
    all_to_all x9, starting transfers between devices: 46.9 us -> 54.1 us  [exchange(): return lax.all_to_all(value, axes, 0, 0, tiled=True)]
    pallas_call x0 -> x1, Pallas kernels: none -> 5.07 us  [apply_first(): pl.pallas_call(functools.partial(first_kernel, n_z, n_core), grid=(n_y,),...]
    all_to_all x2 -> x1, blocking collectives: 63.3 us -> 58.2 us  [exchange(): return lax.all_to_all(value, axes, 0, 0, tiled=True)]
    pallas_call x3 -> x2, Pallas kernels: 11.7 us -> 7.79 us  [apply_matrix(): pl.pallas_call(functools.partial(product_kernel, pieces.shape[0]), grid=(...]
    unnamed x40 -> x28, local copies, waits for them, and re-layouts: 4.54 us -> 0.88 us
  transfers between devices with their start and end apart: 39 -> 39, of which waited for: 22 -> 16; matrix products, arithmetic and copies ran while one was open for 10% -> 12% of each run, Pallas kernels for 10% -> 10%
where the time goes in v2:
time: 339 us; the launch traced here: 338 us
  waiting for transfers between devices  102 us (30%)
  starting transfers between devices  85.3 us (25%)
  blocking collectives  58.2 us (17%)
  Pallas kernels  34.8 us (10%)
  local copies, waits for them, and re-layouts  27.4 us (8%)
  between operations  14.3 us (4%)
  other arithmetic  12.7 us (4%)
    all_to_all x9, waiting for transfers between devices, exchange(): return lax.all_to_all(value, axes, 0, 0, tiled=True)  78.2 us
    all_to_all x1, blocking collectives, exchange(): return lax.all_to_all(value, axes, 0, 0, tiled=True)  58.2 us
    all_to_all x9, starting transfers between devices, exchange(): return lax.all_to_all(value, axes, 0, 0, tiled=True)  54.1 us
    ppermute x21, starting transfers between devices, shift(): lax.ppermute(value, axis, [(i, (i + by) % size) for i in range(size)])  29.5 us
    ppermute x21, waiting for transfers between devices, shift(): lax.ppermute(value, axis, [(i, (i + by) % size) for i in range(size)])  22.3 us
    pallas_call x2, Pallas kernels, apply_trail(): pl.pallas_call(functools.partial(trail_kernel, n_z, n_x, with_gram, len(l...  17.2 us
    pallas_call x2, Pallas kernels, apply_matrix(): pl.pallas_call(functools.partial(product_kernel, pieces.shape[0]), grid=(...  7.79 us
  transfers between devices with their start and end apart: 39, of which 16 were waited for; matrix products, arithmetic and copies ran while one was open for 12% of the time, Pallas kernels for 10%

profile of v2, /device:TPU:0, one launch (start us, length us, event | category | flops | bytes accessed | tf_op | source)
XLA Modules:
  0.0 337.8 jit_solution(6190021698215529165)
XLA Ops:
  7.2 2.1 fusion.36
  10.7 1.6 fusion.3
  13.2 4.4 %all-to-all-start = ((f32[8,16,2,512]{3,1,2,0:T(8,128)}), f32[8,16,2,512]{3,1,2,0:T(8,128)S(1)}, u32[]{:S(2)}, u32[]{:S(2)}) async-start(f32[8,16,2,512]{3,1,2,0:T(8,128)} %copy.23), calls=%async_computation | async-start | bytes 1048576 | tf_op jit(solution)/shard_map/all_to_all | solution.py:30
  17.9 2.0 collective-permute-start.2
  19.9 3.6 %collective-permute-start.3 = (f32[2,128,256]{2,1,0:T(8,128)S(1)}, f32[2,128,256]{2,1,0:T(8,128)S(1)}, u32[]{:S(2)}, u32[]{:S(2)}) collective-permute-start(f32[2,128,256]{2,1,0:T(8,128)S(1)} %get-tuple-element.45), channel_id=1, source_target_pairs={{0,2},{1,3},{2,0},{3,1},{4,6},{5,7},{6,4},{7,5},{8,10},{9,11},{10,... | collective-permute-start | bytes 786440 | tf_op jit(solution)/shard_map/ppermute | solution.py:26
  23.5 1.0 collective-permute-start.4
  24.5 4.5 %collective-permute-done.2 = f32[2,128,256]{2,1,0:T(8,128)S(1)} collective-permute-done((f32[2,128,256]{2,1,0:T(8,128)S(1)}, f32[2,128,256]{2,1,0:T(8,128)S(1)}, u32[]{:S(2)}, u32[]{:S(2)}) %collective-permute-start.2) | collective-permute-done | bytes 262176 | tf_op jit(solution)/shard_map/ppermute | solution.py:26
  28.9 6.8 %collective-permute-done.3 = f32[2,128,256]{2,1,0:T(8,128)S(1)} collective-permute-done((f32[2,128,256]{2,1,0:T(8,128)S(1)}, f32[2,128,256]{2,1,0:T(8,128)S(1)}, u32[]{:S(2)}, u32[]{:S(2)}) %collective-permute-start.3) | collective-permute-done | bytes 262176 | tf_op jit(solution)/shard_map/ppermute | solution.py:26
  35.8 0.9 pad_maximum_fusion.8
  36.7 0.9 pad_maximum_fusion.7
  38.4 0.9 pad_maximum_fusion.6
  39.3 6.2 %all-to-all-start.1 = ((f32[16,16,512]{2,1,0:T(8,128)}), f32[16,16,512]{2,1,0:T(8,128)S(1)}, u32[]{:S(2)}, u32[]{:S(2)}) async-start(f32[16,16,512]{2,1,0:T(8,128)} %pad_maximum_fusion.6), calls=%async_computation.1 | async-start | bytes 1048576 | tf_op jit(solution)/shard_map/all_to_all | solution.py:30
  45.6 11.6 %all-to-all-done.1 = f32[16,16,512]{2,1,0:T(8,128)S(1)} async-done(((f32[16,16,512]{2,1,0:T(8,128)}), f32[16,16,512]{2,1,0:T(8,128)S(1)}, u32[]{:S(2)}, u32[]{:S(2)}) %all-to-all-start.1) | async-done | bytes 524320 | tf_op jit(solution)/shard_map/all_to_all | solution.py:30
  59.2 5.1 %shard_map.68 = f32[4,4,2,128,128]{4,3,2,1,0:T(8,128)} custom-call(f32[4096,256]{1,0:T(8,128)} %bitcast.98, f32[256,128]{1,0:T(8,128)} %slice.97.operand_ref), custom_call_target="tpu_custom_call" | custom-call | flops 805306368 | bytes 4194304 | tf_op jit(solution)/shard_map/pallas_call | solution.py:84
  64.3 3.7 %all-to-all-start.2 = ((f32[16,256,128]{2,1,0:T(8,128)}), f32[16,256,128]{2,1,0:T(8,128)S(1)}, u32[]{:S(2)}, u32[]{:S(2)}) async-start(f32[16,256,128]{2,1,0:T(8,128)} %bitcast.92), calls=%async_computation.2 | async-start | bytes 4194304 | tf_op jit(solution)/shard_map/all_to_all | solution.py:30
  68.0 28.6 %all-to-all-done.2 = f32[16,256,128]{2,1,0:T(8,128)S(1)} async-done(((f32[16,256,128]{2,1,0:T(8,128)}), f32[16,256,128]{2,1,0:T(8,128)S(1)}, u32[]{:S(2)}, u32[]{:S(2)}) %all-to-all-start.2) | async-done | bytes 2097184 | tf_op jit(solution)/shard_map/all_to_all | solution.py:30
  97.5 3.5 %all-to-all-start.3 = ((f32[4,256,128]{2,1,0:T(8,128)}), f32[4,256,128]{2,1,0:T(8,128)S(1)}, u32[]{:S(2)}, u32[]{:S(2)}) async-start(f32[4,256,128]{2,1,0:T(8,128)} %broadcast_in_dim.41), calls=%async_computation.3 | async-start | bytes 1048576 | tf_op jit(solution)/shard_map/all_to_all | solution.py:30
  101.8 4.2 %slice_bitcast_fusion = (f32[4,512,256]{2,1,0:T(8,128)S(1)}, f32[4,512,256]{2,1,0:T(8,128)}) fusion(f32[4,2,512,256]{3,2,1,0:T(8,128)} %param.11), kind=kLoop, calls=%fused_computation.2 | loop fusion | bytes 8388608 | tf_op jit(solution)/shard_map/squeeze | solution.py:337
  106.0 1.0 slice.85
  107.8 1.3 all-to-all-done.3
  109.0 1.8 constant_dynamic-slice_fusion.7
  111.7 0.9 pad_maximum_fusion.4
  112.6 1.9 collective-permute-start.6
  114.5 1.0 pad_maximum_fusion.3
  115.6 3.9 %shard_map.69 = f32[4,256,128]{2,1,0:T(8,128)} custom-call(s32[1]{0:T(128)} %bitcast.16.at_ref, f32[1024,1024]{1,0:T(8,128)} %all-gather.11.cloned.1.call-done.matrix_ref, f32[4,2,128,128]{3,2,1,0:T(8,128)} %bitcast.93), custom_call_target="tpu_custom_call" | custom-call | flops 805306368 | bytes 4194304 | tf_op jit(solution)/shard_map/pallas_call | solution.py:102
  119.5 12.3 %all-to-all-start.4 = ((f32[4,256,128]{2,1,0:T(8,128)}), f32[4,256,128]{2,1,0:T(8,128)}, u32[]{:S(2)}, u32[]{:S(2)}) async-start(f32[4,256,128]{2,1,0:T(8,128)} %shard_map.69), calls=%async_computation.4 | async-start | bytes 1048576 | tf_op jit(solution)/shard_map/all_to_all | solution.py:30
  131.9 1.0 pad_maximum_fusion.2.refs_4_.refs_12_
  132.9 9.3 %all-to-all-done.4 = f32[4,256,128]{2,1,0:T(8,128)} async-done(((f32[4,256,128]{2,1,0:T(8,128)}), f32[4,256,128]{2,1,0:T(8,128)}, u32[]{:S(2)}, u32[]{:S(2)}) %all-to-all-start.4) | async-done | bytes 524320 | tf_op jit(solution)/shard_map/all_to_all | solution.py:30
  142.2 1.1 reduce_sum.77
  143.3 0.9 slice_subtract_fusion
  145.1 4.3 %all-to-all-start.5 = ((f32[4,256,128]{2,1,0:T(8,128)}), f32[4,256,128]{2,1,0:T(8,128)}, u32[]{:S(2)}, u32[]{:S(2)}) async-start(f32[4,256,128]{2,1,0:T(8,128)} %broadcast_in_dim.42), calls=%async_computation.5 | async-start | bytes 1048576 | tf_op jit(solution)/shard_map/all_to_all | solution.py:30
  150.2 3.5 %collective-permute-start.9 = (f32[4,128,256]{2,1,0:T(8,128)}, f32[4,128,256]{2,1,0:T(8,128)}, u32[]{:S(2)}, u32[]{:S(2)}) collective-permute-start(f32[4,128,256]{2,1,0:T(8,128)} %constant_dynamic-slice_fusion.1), channel_id=1, source_target_pairs={{0,2},{1,3},{2,0},{3,1},{4,6},{5,7},{6,4},{7,5},{8,10},{9,11},{10,... | collective-permute-start | bytes 1572872 | tf_op jit(solution)/shard_map/ppermute | solution.py:26
  153.7 5.1 %collective-permute-start.11 = (f32[4,2,128,128]{3,2,1,0:T(8,128)S(1)}, f32[4,2,128,128]{3,2,1,0:T(8,128)}, u32[]{:S(2)}, u32[]{:S(2)}) collective-permute-start(f32[4,2,128,128]{3,2,1,0:T(8,128)S(1)} %bitcast.95), channel_id=1, source_target_pairs={{0,96},{32,0},{64,32},{96,64},{1,97},{33,1},{65,33},{97,65},{2,98}... | collective-permute-start | bytes 1572872 | tf_op jit(solution)/shard_map/ppermute | solution.py:26
  158.8 4.6 %all-to-all-done.5 = f32[4,256,128]{2,1,0:T(8,128)} async-done(((f32[4,256,128]{2,1,0:T(8,128)}), f32[4,256,128]{2,1,0:T(8,128)}, u32[]{:S(2)}, u32[]{:S(2)}) %all-to-all-start.5) | async-done | bytes 524320 | tf_op jit(solution)/shard_map/all_to_all | solution.py:30
  163.4 1.0 constant_dynamic-slice_fusion.4
  164.3 1.1 constant_dynamic-slice_fusion.5
  165.4 0.9 pad_maximum_fusion.5
  166.4 6.1 %collective-permute-start.12 = (f32[4,2,128,128]{3,2,1,0:T(8,128)S(1)}, f32[4,2,128,128]{3,2,1,0:T(8,128)}, u32[]{:S(2)}, u32[]{:S(2)}) collective-permute-start(f32[4,2,128,128]{3,2,1,0:T(8,128)S(1)} %bitcast.96), channel_id=1, source_target_pairs={{0,64},{32,96},{64,0},{96,32},{1,65},{33,97},{65,1},{97,33},{2,66}... | collective-permute-start | bytes 1572872 | tf_op jit(solution)/shard_map/ppermute | solution.py:26
  172.5 2.2 collective-permute-start.13
  174.6 1.2 constant_dynamic-slice_fusion
  175.9 4.3 %collective-permute-done.9.refs_3_ = f32[4,128,256]{2,1,0:T(8,128)} collective-permute-done((f32[4,128,256]{2,1,0:T(8,128)}, f32[4,128,256]{2,1,0:T(8,128)}, u32[]{:S(2)}, u32[]{:S(2)}) %collective-permute-start.9) | collective-permute-done | bytes 524320 | tf_op jit(solution)/shard_map/ppermute | solution.py:26
  180.1 1.0 collective-permute-start.10
  181.2 1.0 collective-permute-start.8
  182.2 3.9 %shard_map.70 = f32[4,256,128]{2,1,0:T(8,128)} custom-call(s32[1]{0:T(128)} %bitcast.16.at_ref, f32[1024,1024]{1,0:T(8,128)} %all-gather.9.cloned.1.call-done.matrix_ref, f32[4,2,128,128]{3,2,1,0:T(8,128)} %bitcast.28.operand_ref), custom_call_target="tpu_custom_call" | custom-call | flops 805306368 | bytes 4194304 | tf_op jit(solution)/shard_map/pallas_call | solution.py:102
  186.0 5.6 %all-to-all-start.6 = ((f32[4,256,128]{2,1,0:T(8,128)}), f32[4,256,128]{2,1,0:T(8,128)S(1)}, u32[]{:S(2)}, u32[]{:S(2)}) async-start(f32[4,256,128]{2,1,0:T(8,128)} %shard_map.70), calls=%async_computation.6 | async-start | bytes 1048576 | tf_op jit(solution)/shard_map/all_to_all | solution.py:30
  191.7 8.1 %all-to-all-done.6 = f32[4,256,128]{2,1,0:T(8,128)S(1)} async-done(((f32[4,256,128]{2,1,0:T(8,128)}), f32[4,256,128]{2,1,0:T(8,128)S(1)}, u32[]{:S(2)}, u32[]{:S(2)}) %all-to-all-start.6) | async-done | bytes 524320 | tf_op jit(solution)/shard_map/all_to_all | solution.py:30
  199.8 3.4 %collective-permute-done.10.refs_4_ = f32[4,128,256]{2,1,0:T(8,128)S(1)} collective-permute-done((f32[4,128,256]{2,1,0:T(8,128)}, f32[4,128,256]{2,1,0:T(8,128)S(1)}, u32[]{:S(2)}, u32[]{:S(2)}) %collective-permute-start.10) | collective-permute-done | bytes 524320 | tf_op jit(solution)/shard_map/ppermute | solution.py:26
  203.2 1.5 collective-permute-done.8.refs_2_
  204.7 1.5 broadcast_in_dim.45
  206.2 9.9 %all-to-all-start.7 = ((f32[16,256,128]{2,1,0:T(8,128)}), f32[16,256,128]{2,1,0:T(8,128)}, u32[]{:S(2)}, u32[]{:S(2)}) async-start(f32[16,256,128]{2,1,0:T(8,128)} %broadcast_in_dim.45), calls=%async_computation.7 | async-start | bytes 4194304 | tf_op jit(solution)/shard_map/all_to_all | solution.py:30
  216.2 2.3 gather_fusion
  218.5 2.3 gather_fusion.1
  223.0 1.6 collective-permute-done.15
  227.0 0.9 and_convert_fusion.refs_20_
  228.0 9.1 %shard_map.72.refs_9_ = f32[4,2,4,128,128]{4,3,2,1,0:T(8,128)} custom-call(s32[2]{0:T(128)} %pad_add_fusion.at_ref, f32[4,2,128,128]{3,2,1,0:T(8,128)} %bitcast.94, f32[4,2,128,128]{3,2,1,0:T(8,128)} %collective-permute-done.11.refs_1_, f32[4,2,128,128]{3,2,1,0:T(8,128)} %collective-permute-done.12.refs_2_, ...), custom_call_target="tpu_custom_call" | custom-call | flops 3221225472 | bytes 10485760 | tf_op jit(solution)/shard_map/pallas_call | solution.py:173
  237.1 9.7 %all-to-all-done.7 = f32[16,256,128]{2,1,0:T(8,128)} async-done(((f32[16,256,128]{2,1,0:T(8,128)}), f32[16,256,128]{2,1,0:T(8,128)}, u32[]{:S(2)}, u32[]{:S(2)}) %all-to-all-start.7) | async-done | bytes 2097184 | tf_op jit(solution)/shard_map/all_to_all | solution.py:30
  246.9 8.1 %shard_map.73 = f32[4,2,4,128,128]{4,3,2,1,0:T(8,128)} custom-call(s32[2]{0:T(128)} %pad_add_fusion.at_ref, f32[4,4,2,128,128]{4,3,2,1,0:T(8,128)} %bitcast.37.refs_0_, f32[4,128,256]{2,1,0:T(8,128)} %get-tuple-element.37.refs_1_, f32[4,128,256]{2,1,0:T(8,128)} %copy-done.12, f32[4,128,256]{2,1,0:T(8,128)} %collective-permute-done.9.refs_3_, ...), custom_call_target="tpu_custom_call" | custom-call | flops 3221225472 | bytes 10485760 | tf_op jit(solution)/shard_map/pallas_call | solution.py:173
  255.0 58.2 %all_to_all.50 = f32[4,2,4,128,128]{4,3,2,1,0:T(8,128)S(1)} all-to-all(f32[4,2,4,128,128]{4,3,2,1,0:T(8,128)} %shard_map.73), channel_id=1, replica_groups=mesh['x'=4,'core'=2,'y'=4,'z'=4] {'y'}, dimensions={0} | all-to-all | bytes 4194304 | tf_op jit(solution)/shard_map/all_to_all | solution.py:30
  313.5 1.5 collective-permute-done.24
  315.4 1.1 copy.28
  316.5 4.1 %all-to-all-start.9 = ((f32[4,4,128,64]{2,3,1,0:T(8,128)}), f32[4,4,128,64]{2,3,1,0:T(8,128)S(1)}, u32[]{:S(2)}, u32[]{:S(2)}) async-start(f32[4,4,128,64]{2,3,1,0:T(8,128)} %bitcast.41), calls=%async_computation.9 | async-start | bytes 1048576 | tf_op jit(solution)/shard_map/all_to_all | solution.py:30
  320.6 4.7 %shard_map.71 = f32[2,512,1024]{2,1,0:T(8,128)} custom-call(f32[4,4,128,256]{3,2,1,0:T(8,128)} %bitcast.101, f32[4,4,128,256]{3,2,1,0:T(8,128)} %bitcast.102), custom_call_target="tpu_custom_call" | custom-call | tf_op jit(solution)/shard_map/pallas_call | solution.py:200
  325.3 5.1 %all-to-all-done.9 = f32[4,4,128,64]{2,3,1,0:T(8,128)S(1)} async-done(((f32[4,4,128,64]{2,3,1,0:T(8,128)}), f32[4,4,128,64]{2,3,1,0:T(8,128)S(1)}, u32[]{:S(2)}, u32[]{:S(2)}) %all-to-all-start.9) | async-done | bytes 524320 | tf_op jit(solution)/shard_map/all_to_all | solution.py:30
  330.4 0.9 copy_bitcast_fusion
  (126 shorter events, 15.9 us)
Async XLA Ops:
  7.2 2.2 copy-start.10
  7.2 52.0 %all-gather.15.cloned.1.call-start = ((), (), s32[]{:S(2)}) async-start(), calls=%async_computation.14 | async-start | bytes 4718592 | tf_op jit(solution)/shard_map/all_gather | solution.py:267
  9.3 8.3 %copy-start.9 = (f32[512,256]{1,0:T(8,128)S(1)}, f32[512,256]{1,0:T(8,128)}, u32[]{:S(2)}) copy-start(f32[512,256]{1,0:T(8,128)} %param.10) | copy-start | bytes 1572868
  13.2 22.5 %all-to-all-start = ((f32[8,16,2,512]{3,1,2,0:T(8,128)}), f32[8,16,2,512]{3,1,2,0:T(8,128)S(1)}, u32[]{:S(2)}, u32[]{:S(2)}) async-start(f32[8,16,2,512]{3,1,2,0:T(8,128)} %copy.23), calls=%async_computation | async-start | bytes 1048576 | tf_op jit(solution)/shard_map/all_to_all | solution.py:30
  17.6 98.0 %all-gather.11.cloned.1.call-start = ((), (), s32[]{:S(2)}) async-start(), calls=%async_computation.12 | async-start | bytes 4718592 | tf_op jit(solution)/shard_map/all_gather | solution.py:265
  17.9 11.0 %collective-permute-start.2 = (f32[2,128,256]{2,1,0:T(8,128)S(1)}, f32[2,128,256]{2,1,0:T(8,128)S(1)}, u32[]{:S(2)}, u32[]{:S(2)}) collective-permute-start(f32[2,128,256]{2,1,0:T(8,128)S(1)} %get-tuple-element.46), channel_id=1, source_target_pairs={{0,1},{1,2},{2,3},{3,0},{4,5},{5,6},{6,7},{7,4},{8,9},{9,10},{10,1... | collective-permute-start | bytes 786440 | tf_op jit(solution)/shard_map/ppermute | solution.py:26
  19.9 15.8 %collective-permute-start.3 = (f32[2,128,256]{2,1,0:T(8,128)S(1)}, f32[2,128,256]{2,1,0:T(8,128)S(1)}, u32[]{:S(2)}, u32[]{:S(2)}) collective-permute-start(f32[2,128,256]{2,1,0:T(8,128)S(1)} %get-tuple-element.45), channel_id=1, source_target_pairs={{0,2},{1,3},{2,0},{3,1},{4,6},{5,7},{6,4},{7,5},{8,10},{9,11},{10,... | collective-permute-start | bytes 786440 | tf_op jit(solution)/shard_map/ppermute | solution.py:26
  23.5 12.3 %collective-permute-start.4 = (f32[2,128,256]{2,1,0:T(8,128)S(1)}, f32[2,128,256]{2,1,0:T(8,128)S(1)}, u32[]{:S(2)}, u32[]{:S(2)}) collective-permute-start(f32[2,128,256]{2,1,0:T(8,128)S(1)} %get-tuple-element.44), channel_id=1, source_target_pairs={{0,3},{1,0},{2,1},{3,2},{4,7},{5,4},{6,5},{7,6},{8,11},{9,8},{10,9... | collective-permute-start | bytes 786440 | tf_op jit(solution)/shard_map/ppermute | solution.py:26
  36.7 145.5 %all-gather.9.cloned.1.call-start = ((), (), s32[]{:S(2)}) async-start(), calls=%async_computation.11 | async-start | bytes 4718592 | tf_op jit(solution)/shard_map/all_gather | solution.py:265
  39.3 18.0 %all-to-all-start.1 = ((f32[16,16,512]{2,1,0:T(8,128)}), f32[16,16,512]{2,1,0:T(8,128)S(1)}, u32[]{:S(2)}, u32[]{:S(2)}) async-start(f32[16,16,512]{2,1,0:T(8,128)} %pad_maximum_fusion.6), calls=%async_computation.1 | async-start | bytes 1048576 | tf_op jit(solution)/shard_map/all_to_all | solution.py:30
  57.8 0.7 copy-start.8
  64.3 32.3 %all-to-all-start.2 = ((f32[16,256,128]{2,1,0:T(8,128)}), f32[16,256,128]{2,1,0:T(8,128)S(1)}, u32[]{:S(2)}, u32[]{:S(2)}) async-start(f32[16,256,128]{2,1,0:T(8,128)} %bitcast.92), calls=%async_computation.2 | async-start | bytes 4194304 | tf_op jit(solution)/shard_map/all_to_all | solution.py:30
  97.5 11.5 %all-to-all-start.3 = ((f32[4,256,128]{2,1,0:T(8,128)}), f32[4,256,128]{2,1,0:T(8,128)S(1)}, u32[]{:S(2)}, u32[]{:S(2)}) async-start(f32[4,256,128]{2,1,0:T(8,128)} %broadcast_in_dim.41), calls=%async_computation.3 | async-start | bytes 1048576 | tf_op jit(solution)/shard_map/all_to_all | solution.py:30
  101.0 219.6 %all-gather.7.cloned.1.call-start = ((), (), s32[]{:S(2)}) async-start(), calls=%async_computation.10 | async-start | bytes 2228224 | tf_op jit(solution)/shard_map/all_gather | solution.py:317
  101.1 6.0 %collective-permute-start = (f32[128,128]{1,0:T(8,128)S(1)}, f32[128,128]{1,0:T(8,128)S(1)}, u32[]{:S(2)}, u32[]{:S(2)}) collective-permute-start(f32[128,128]{1,0:T(8,128)S(1)} %get-tuple-element.66), channel_id=1, source_target_pairs={{0,0},{1,1},{2,2},{3,3},{4,32},{5,33},{6,34},{7,35},{8,64},{9,65},... | collective-permute-start | bytes 196616 | tf_op jit(solution)/shard_map/ppermute | solution.py:315
  101.7 4.3 %copy-start.7 = (f32[6,512,128]{2,1,0:T(8,128)S(1)}, f32[6,512,128]{2,1,0:T(8,128)}, u32[]{:S(2)}) copy-start(f32[6,512,128]{2,1,0:T(8,128)} %param.8) | copy-start | bytes 4718596
  101.8 5.3 %collective-permute-start.1 = (f32[128,128]{1,0:T(8,128)S(1)}, f32[128,128]{1,0:T(8,128)S(1)}, u32[]{:S(2)}, u32[]{:S(2)}) collective-permute-start(f32[128,128]{1,0:T(8,128)S(1)} %get-tuple-element.67), channel_id=1, source_target_pairs={{0,16},{1,17},{2,18},{3,19},{4,48},{5,49},{6,50},{7,51},{8,80},{9,... | collective-permute-start | bytes 196616 | tf_op jit(solution)/shard_map/ppermute | solution.py:315
  109.0 2.6 copy-start.1
  109.0 1.9 copy-start.3
  112.6 31.6 %collective-permute-start.6 = (f32[4,128,384]{2,1,0:T(8,128)}, f32[4,128,384]{2,1,0:T(8,128)}, u32[]{:S(2)}, u32[]{:S(2)}) collective-permute-start(f32[4,128,384]{2,1,0:T(8,128)} %pad_maximum_fusion.4), channel_id=1, source_target_pairs={{0,3},{1,0},{2,1},{3,2},{4,7},{5,4},{6,5},{7,6},{8,11},{9,8},{10,9... | collective-permute-start | bytes 2359304 | tf_op jit(solution)/shard_map/ppermute | solution.py:26
  115.5 28.7 %collective-permute-start.5 = (f32[4,128,384]{2,1,0:T(8,128)}, f32[4,128,384]{2,1,0:T(8,128)}, u32[]{:S(2)}, u32[]{:S(2)}) collective-permute-start(f32[4,128,384]{2,1,0:T(8,128)} %pad_maximum_fusion.3), channel_id=1, source_target_pairs={{0,1},{1,2},{2,3},{3,0},{4,5},{5,6},{6,7},{7,4},{8,9},{9,10},{10,1... | collective-permute-start | bytes 2359304 | tf_op jit(solution)/shard_map/ppermute | solution.py:26
  119.5 22.7 %all-to-all-start.4 = ((f32[4,256,128]{2,1,0:T(8,128)}), f32[4,256,128]{2,1,0:T(8,128)}, u32[]{:S(2)}, u32[]{:S(2)}) async-start(f32[4,256,128]{2,1,0:T(8,128)} %shard_map.69), calls=%async_computation.4 | async-start | bytes 1048576 | tf_op jit(solution)/shard_map/all_to_all | solution.py:30
  132.9 88.0 %copy-start = (f32[4,128,384]{2,1,0:T(8,128)}, f32[4,128,384]{2,1,0:T(8,128)S(1)}, u32[]{:S(2)}) copy-start(f32[4,128,384]{2,1,0:T(8,128)S(1)} %pad_maximum_fusion.2.refs_4_.refs_12_) | copy-start | bytes 2359300
  132.9 20.8 %copy-start.2 = (f32[4,256,128]{2,1,0:T(8,128)S(1)}, f32[4,256,128]{2,1,0:T(8,128)}, u32[]{:S(2)}) copy-start(f32[4,256,128]{2,1,0:T(8,128)} %copy-done.1) | copy-start | bytes 1572868
  145.1 18.3 %all-to-all-start.5 = ((f32[4,256,128]{2,1,0:T(8,128)}), f32[4,256,128]{2,1,0:T(8,128)}, u32[]{:S(2)}, u32[]{:S(2)}) async-start(f32[4,256,128]{2,1,0:T(8,128)} %broadcast_in_dim.42), calls=%async_computation.5 | async-start | bytes 1048576 | tf_op jit(solution)/shard_map/all_to_all | solution.py:30
  150.2 29.9 %collective-permute-start.9 = (f32[4,128,256]{2,1,0:T(8,128)}, f32[4,128,256]{2,1,0:T(8,128)}, u32[]{:S(2)}, u32[]{:S(2)}) collective-permute-start(f32[4,128,256]{2,1,0:T(8,128)} %constant_dynamic-slice_fusion.1), channel_id=1, source_target_pairs={{0,2},{1,3},{2,0},{3,1},{4,6},{5,7},{6,4},{7,5},{8,10},{9,11},{10,... | collective-permute-start | bytes 1572872 | tf_op jit(solution)/shard_map/ppermute | solution.py:26
  153.7 27.5 %collective-permute-start.11 = (f32[4,2,128,128]{3,2,1,0:T(8,128)S(1)}, f32[4,2,128,128]{3,2,1,0:T(8,128)}, u32[]{:S(2)}, u32[]{:S(2)}) collective-permute-start(f32[4,2,128,128]{3,2,1,0:T(8,128)S(1)} %bitcast.95), channel_id=1, source_target_pairs={{0,96},{32,0},{64,32},{96,64},{1,97},{33,1},{65,33},{97,65},{2,98}... | collective-permute-start | bytes 1572872 | tf_op jit(solution)/shard_map/ppermute | solution.py:26
  166.4 38.3 %collective-permute-start.7 = (f32[4,128,384]{2,1,0:T(8,128)}, f32[4,128,384]{2,1,0:T(8,128)}, u32[]{:S(2)}, u32[]{:S(2)}) collective-permute-start(f32[4,128,384]{2,1,0:T(8,128)} %pad_maximum_fusion.5), channel_id=1, source_target_pairs={{0,2},{1,3},{2,0},{3,1},{4,6},{5,7},{6,4},{7,5},{8,10},{9,11},{10,... | collective-permute-start | bytes 2359304 | tf_op jit(solution)/shard_map/ppermute | solution.py:26
  166.4 33.4 %collective-permute-start.12 = (f32[4,2,128,128]{3,2,1,0:T(8,128)S(1)}, f32[4,2,128,128]{3,2,1,0:T(8,128)}, u32[]{:S(2)}, u32[]{:S(2)}) collective-permute-start(f32[4,2,128,128]{3,2,1,0:T(8,128)S(1)} %bitcast.96), channel_id=1, source_target_pairs={{0,64},{32,96},{64,0},{96,32},{1,65},{33,97},{65,1},{97,33},{2,66}... | collective-permute-start | bytes 1572872 | tf_op jit(solution)/shard_map/ppermute | solution.py:26
  172.5 27.3 %collective-permute-start.13 = (f32[4,2,128,128]{3,2,1,0:T(8,128)S(1)}, f32[4,2,128,128]{3,2,1,0:T(8,128)}, u32[]{:S(2)}, u32[]{:S(2)}) collective-permute-start(f32[4,2,128,128]{3,2,1,0:T(8,128)S(1)} %bitcast.97), channel_id=1, source_target_pairs={{0,32},{32,64},{64,96},{96,0},{1,33},{33,65},{65,97},{97,1},{2,34}... | collective-permute-start | bytes 1572872 | tf_op jit(solution)/shard_map/ppermute | solution.py:26
  180.1 23.1 %collective-permute-start.10 = (f32[4,128,256]{2,1,0:T(8,128)}, f32[4,128,256]{2,1,0:T(8,128)S(1)}, u32[]{:S(2)}, u32[]{:S(2)}) collective-permute-start(f32[4,128,256]{2,1,0:T(8,128)} %get-tuple-element.35), channel_id=1, source_target_pairs={{0,3},{1,0},{2,1},{3,2},{4,7},{5,4},{6,5},{7,6},{8,11},{9,8},{10,9... | collective-permute-start | bytes 1572872 | tf_op jit(solution)/shard_map/ppermute | solution.py:26
  181.2 23.5 %collective-permute-start.8 = (f32[4,128,256]{2,1,0:T(8,128)}, f32[4,128,256]{2,1,0:T(8,128)S(1)}, u32[]{:S(2)}, u32[]{:S(2)}) collective-permute-start(f32[4,128,256]{2,1,0:T(8,128)} %get-tuple-element.36), channel_id=1, source_target_pairs={{0,1},{1,2},{2,3},{3,0},{4,5},{5,6},{6,7},{7,4},{8,9},{9,10},{10,1... | collective-permute-start | bytes 1572872 | tf_op jit(solution)/shard_map/ppermute | solution.py:26
  186.0 13.7 %all-to-all-start.6 = ((f32[4,256,128]{2,1,0:T(8,128)}), f32[4,256,128]{2,1,0:T(8,128)S(1)}, u32[]{:S(2)}, u32[]{:S(2)}) async-start(f32[4,256,128]{2,1,0:T(8,128)} %shard_map.70), calls=%async_computation.6 | async-start | bytes 1048576 | tf_op jit(solution)/shard_map/all_to_all | solution.py:30
  203.2 3.0 copy-start.11
  204.7 1.5 copy-start.12
  206.2 40.7 %all-to-all-start.7 = ((f32[16,256,128]{2,1,0:T(8,128)}), f32[16,256,128]{2,1,0:T(8,128)}, u32[]{:S(2)}, u32[]{:S(2)}) async-start(f32[16,256,128]{2,1,0:T(8,128)} %broadcast_in_dim.45), calls=%async_computation.7 | async-start | bytes 4194304 | tf_op jit(solution)/shard_map/all_to_all | solution.py:30
  216.1 104.5 %all-gather.13.cloned.1.call-start = ((), (), s32[]{:S(2)}) async-start(), calls=%async_computation.13 | async-start | bytes 2228224 | tf_op jit(solution)/shard_map/all_gather | solution.py:317
  220.9 5.1 %collective-permute-start.20 = (f32[4,128,384]{2,1,0:T(8,128)S(1)}, f32[4,128,384]{2,1,0:T(8,128)S(1)}, u32[]{:S(2)}, u32[]{:S(2)}) collective-permute-start(f32[4,128,384]{2,1,0:T(8,128)S(1)} %pad_maximum_fusion.2.refs_4_.refs_12_), channel_id=1, source_target_pairs={{0,16},{16,0},{1,17},{17,1},{2,18},{18,2},{3,19},{19,3},{4,20},{20... | collective-permute-start | bytes 2359304 | tf_op jit(solution)/shard_map/ppermute | solution.py:26
  220.9 5.4 %collective-permute-start.23 = (f32[4,128,384]{2,1,0:T(8,128)}, f32[4,128,384]{2,1,0:T(8,128)S(1)}, u32[]{:S(2)}, u32[]{:S(2)}) collective-permute-start(f32[4,128,384]{2,1,0:T(8,128)} %collective-permute-done.6.refs_7_.refs_15_), channel_id=1, source_target_pairs={{0,16},{16,0},{1,17},{17,1},{2,18},{18,2},{3,19},{19,3},{4,20},{20... | collective-permute-start | bytes 2359304 | tf_op jit(solution)/shard_map/ppermute | solution.py:26
  221.4 5.5 %collective-permute-start.21 = (f32[4,128,384]{2,1,0:T(8,128)}, f32[4,128,384]{2,1,0:T(8,128)S(1)}, u32[]{:S(2)}, u32[]{:S(2)}) collective-permute-start(f32[4,128,384]{2,1,0:T(8,128)} %collective-permute-done.5.refs_5_.refs_13_), channel_id=1, source_target_pairs={{0,16},{16,0},{1,17},{17,1},{2,18},{18,2},{3,19},{19,3},{4,20},{20... | collective-permute-start | bytes 2359304 | tf_op jit(solution)/shard_map/ppermute | solution.py:26
  221.6 1.2 collective-permute-start.14
  222.3 5.7 %collective-permute-start.22 = (f32[4,128,384]{2,1,0:T(8,128)}, f32[4,128,384]{2,1,0:T(8,128)}, u32[]{:S(2)}, u32[]{:S(2)}) collective-permute-start(f32[4,128,384]{2,1,0:T(8,128)} %collective-permute-done.7.refs_6_.refs_14_), channel_id=1, source_target_pairs={{0,16},{16,0},{1,17},{17,1},{2,18},{18,2},{3,19},{19,3},{4,20},{20... | collective-permute-start | bytes 2359304 | tf_op jit(solution)/shard_map/ppermute | solution.py:26
  222.8 1.8 collective-permute-start.15
  225.8 11.2 %collective-permute-start.18 = (f32[4,128,256]{2,1,0:T(8,128)}, f32[4,128,256]{2,1,0:T(8,128)}, u32[]{:S(2)}, u32[]{:S(2)}) collective-permute-start(f32[4,128,256]{2,1,0:T(8,128)} %collective-permute-done.9.refs_3_), channel_id=1, source_target_pairs={{0,16},{16,0},{1,17},{17,1},{2,18},{18,2},{3,19},{19,3},{4,20},{20... | collective-permute-start | bytes 1572872 | tf_op jit(solution)/shard_map/ppermute | solution.py:26
  226.0 2.0 copy-start.4
  226.0 11.1 %collective-permute-start.16 = (f32[4,128,256]{2,1,0:T(8,128)}, f32[4,128,256]{2,1,0:T(8,128)S(1)}, u32[]{:S(2)}, u32[]{:S(2)}) collective-permute-start(f32[4,128,256]{2,1,0:T(8,128)} %get-tuple-element.37.refs_1_), channel_id=1, source_target_pairs={{0,16},{16,0},{1,17},{17,1},{2,18},{18,2},{3,19},{19,3},{4,20},{20... | collective-permute-start | bytes 1572872 | tf_op jit(solution)/shard_map/ppermute | solution.py:26
  226.4 1.6 copy-start.5
  226.4 10.7 %collective-permute-start.17 = (f32[4,128,256]{2,1,0:T(8,128)}, f32[4,128,256]{2,1,0:T(8,128)}, u32[]{:S(2)}, u32[]{:S(2)}) collective-permute-start(f32[4,128,256]{2,1,0:T(8,128)} %copy-done.12), channel_id=1, source_target_pairs={{0,16},{16,0},{1,17},{17,1},{2,18},{18,2},{3,19},{19,3},{4,20},{20... | collective-permute-start | bytes 1572872 | tf_op jit(solution)/shard_map/ppermute | solution.py:26
  226.9 1.1 copy-start.6
  226.9 10.2 %collective-permute-start.19 = (f32[4,128,256]{2,1,0:T(8,128)}, f32[4,128,256]{2,1,0:T(8,128)}, u32[]{:S(2)}, u32[]{:S(2)}) collective-permute-start(f32[4,128,256]{2,1,0:T(8,128)} %copy-done.11), channel_id=1, source_target_pairs={{0,16},{16,0},{1,17},{17,1},{2,18},{18,2},{3,19},{19,3},{4,20},{20... | collective-permute-start | bytes 1572872 | tf_op jit(solution)/shard_map/ppermute | solution.py:26
  237.1 9.8 %copy-start.13 = (f32[4,128,256]{2,1,0:T(8,128)}, f32[4,128,256]{2,1,0:T(8,128)S(1)}, u32[]{:S(2)}) copy-start(f32[4,128,256]{2,1,0:T(8,128)S(1)} %collective-permute-done.16.refs_5_) | copy-start | bytes 1572868
  313.4 1.6 collective-permute-start.24
  316.5 13.9 %all-to-all-start.9 = ((f32[4,4,128,64]{2,3,1,0:T(8,128)}), f32[4,4,128,64]{2,3,1,0:T(8,128)S(1)}, u32[]{:S(2)}, u32[]{:S(2)}) async-start(f32[4,4,128,64]{2,3,1,0:T(8,128)} %bitcast.41), calls=%async_computation.9 | async-start | bytes 1048576 | tf_op jit(solution)/shard_map/all_to_all | solution.py:30
Sparse Core Ops, SparseCore 0:
  10.3 36.1 all-gather.14
  48.2 32.5 all-gather.10
  82.5 37.6 all-gather.8
  122.2 52.5 all-gather.6
  225.4 85.7 all-gather.12

commit v3 on v2

--- a/solution.py
+++ b/solution.py
@@ -115,14 +115,12 @@
     )(at_z, matrix, pieces)
 
 
-def trail_kernel(n_z, n_x, with_gram, one_list, at_ref, *refs):
-    lists = refs[:1] if one_list else refs[:n_x]
-    refs = refs[len(lists) :]
+def trail_kernel(n_z, with_gram, at_ref, lists_ref, *refs):
     factor = refs[: 2 * n_z]
     refs = refs[2 * n_z :]
     gram = refs[: 2 * n_z] if with_gram else ()
     start_ref, out_ref, high_ref, low_ref, chosen_ref = refs[len(gram) :]
-    at_x, at_z = at_ref[0], at_ref[1]
+    n_x, at_z = lists_ref.shape[0], at_ref[0]
     width = factor[0].shape[-1]
     slots = start_ref.shape[1] if with_gram else 0
     slab = out_ref.shape[-1]
@@ -131,7 +129,7 @@
     def _():
         for by in range(n_z):
             for i in range(n_x):
-                rows = band_rows(lists[0] if one_list else lists[i], (i,) if one_list else (), at_z, by, n_z)
+                rows = band_rows(lists_ref, (i,), at_z, by, n_z)
                 into = slice(by * width, (by + 1) * width), slice(i * slab, (i + 1) * slab)
                 high_ref[into], low_ref[into] = split(rows)
             if with_gram:
@@ -149,29 +147,28 @@
         total = placed - total
     half = total.shape[0] // 2
     for i in range(n_x):
-        at = i if one_list else lax.rem(at_x + i, n_x)
         for side in range(2):
             part = total[side * half : (side + 1) * half, i * slab : (i + 1) * slab]
-            out_ref[at, side, 0] = part if with_gram else start_ref[at, side, 0] - part
-
-
-def apply_trail(where, own, other, width, lists, start, with_gram, n_x):
+            out_ref[i, side, 0] = part if with_gram else start_ref[i, side, 0] - part
+
+
+def apply_trail(where, own, other, width, lists, start, with_gram):
     n_z = len(own)
     blocks, quarter, depth = own[0].shape
     slots = depth - width
-    slab = lists[0].shape[-1]
+    n_x, slab = lists.shape[0], lists.shape[-1]
     whole = lambda v: pl.BlockSpec(v.shape, lambda *_: (0,) * v.ndim)
     part = pl.BlockSpec((1, quarter, width), lambda t: (t, 0, 0))
     ends = pl.BlockSpec((n_x, 2, 1, quarter, slab), lambda t: (0, 0, t, 0, 0))
     pieces = [*own, *other]
-    specs = [SMEM] + [whole(v) for v in lists] + [part] * (2 * n_z)
-    args = [where, *lists, *pieces]
+    specs = [SMEM, whole(lists)] + [part] * (2 * n_z)
+    args = [where, lists, *pieces]
     if with_gram:
         specs += [pl.BlockSpec((1, quarter, slots), lambda t: (t, 0, width // slots))] * (2 * n_z)
         args += pieces
     band, n_list = n_z * width, n_x * slab
     return pl.pallas_call(
-        functools.partial(trail_kernel, n_z, n_x, with_gram, len(lists) == 1),
+        functools.partial(trail_kernel, n_z, with_gram),
         grid=(blocks,),
         in_specs=specs + [whole(start) if with_gram else ends],
         out_specs=ends,
@@ -187,23 +184,26 @@
     )(*args, start)
 
 
-def rows_kernel(first_ref, second_ref, out_ref):
-    n_y, wide = first_ref.shape[0], first_ref.shape[-1]
-    for i in range(n_y):
-        out_ref[0, :, i * wide : (i + 1) * wide] = first_ref[i, 0]
-        out_ref[1, :, i * wide : (i + 1) * wide] = second_ref[i, 0]
-
-
-def as_rows(first, second):
+def rows_kernel(at_ref, first_ref, *refs):
+    seconds, out_ref = refs[:-1], refs[-1]
+    n_y, n_z, quarter, wide = first_ref.shape
+    for y in range(n_y):
+        at_y = pl.multiple_of(lax.rem(at_ref[0] + n_y - y, n_y) * wide, wide)
+        for z in range(n_z):
+            out_ref[0, z * quarter : (z + 1) * quarter, y * wide : (y + 1) * wide] = first_ref[y, z]
+            at_z = pl.multiple_of(lax.rem(at_ref[1] + n_z - z, n_z) * quarter, quarter)
+            out_ref[1, pl.ds(at_z, quarter), pl.ds(at_y, wide)] = seconds[y][z]
+
+
+def as_rows(where, first, seconds):
     n_y, n_z, quarter, wide = first.shape
-    spec = pl.BlockSpec((n_y, 1, quarter, wide), lambda i: (0, i, 0, 0))
     return pl.pallas_call(
         rows_kernel,
-        grid=(n_z,),
-        in_specs=[spec, spec],
-        out_specs=pl.BlockSpec((2, quarter, n_y * wide), lambda i: (0, i, 0)),
+        in_specs=[SMEM] + [pl.BlockSpec(memory_space=pltpu.VMEM)] * (1 + n_y),
+        out_specs=pl.BlockSpec(memory_space=pltpu.VMEM),
         out_shape=jax.ShapeDtypeStruct((2, n_z * quarter, n_y * wide), F32),
-    )(first, second)
+        cost_estimate=pl.CostEstimate(flops=0, bytes_accessed=8 * 2**20, transcendentals=0),
+    )(where, first, *seconds)
 
 
 def after(value, *others):
@@ -216,7 +216,7 @@
     col = lax.axis_index(COLS)
     row = lax.axis_index(ROWS)
     core = lax.axis_index("core")
-    x_at = lax.axis_index("x")
+    y_at = lax.axis_index("y")
     z_at = lax.axis_index("z")
     list_len = cells.shape[0]
     run_len = list_len // n_cols
@@ -252,8 +252,9 @@
         lax.Precision.DEFAULT,
     )
 
-    def moved(cut, by):
-        return shift(cut((z_at + by) % n_z), "z", by) if by else cut(z_at)
+    def moved(cut, by, ready=None):
+        value = cut((z_at + by) % n_z)
+        return shift(value if ready is None else after(value, ready), "z", by) if by else value
 
     def quarters(cut):
         return [moved(cut, by) for by in range(n_z)]
@@ -292,8 +293,8 @@
     def spread_z(block):
         return spread(block, "z").reshape(n_z, n_core, quarter, slab)
 
-    def product(matrix, pieces):
-        return jnp.sum(exchange(apply_matrix(where_z, matrix, pieces, n_y), "y"), axis=0)
+    def summed(terms, axes):
+        return jnp.sum(exchange(terms, axes), axis=0)
 
     axes = ROWS + COLS
     sizes = (n_x, n_core, n_y, n_z)
@@ -301,9 +302,9 @@
     def device(x, k, y, z):
         return ((x * n_core + k) * n_y + y) * n_z + z
 
-    def solution_rows(block):
+    def solution_piece(block):
         pieces = block.reshape(n_core, quarter, slab)
-        moved = []
+        arrived = []
         for m in range(n_core):
             to = [
                 (device(x, k, y, z), device(y, k ^ m, x, z))
@@ -312,60 +313,63 @@
                 for y in range(n_y)
                 for z in range(n_z)
             ]
-            moved.append(lax.ppermute(lax.dynamic_index_in_dim(pieces, core ^ m, 0, keepdims=False), axes, to))
-        piece = jnp.where(core == 0, jnp.concatenate(moved, axis=1), jnp.concatenate(moved[::-1], axis=1))
-        return lax.all_gather(piece, COLS, axis=0, tiled=False)
+            arrived.append(lax.ppermute(lax.dynamic_index_in_dim(pieces, core ^ m, 0, keepdims=False), axes, to))
+        return jnp.where(core == 0, jnp.concatenate(arrived, axis=1), jnp.concatenate(arrived[::-1], axis=1))
 
     def trail_0(at):
-        return jnp.concatenate([rows_at(early[0], at), rows_at(early[1], at)], axis=2)
+        return jnp.concatenate([rows_at(trail_factor[:, 0], at), rows_at(gram_slots[2:], at)], axis=2)
 
     def trail_1(at):
-        return rows_at(late, at)
-
-    first = jnp.sum(
-        exchange(apply_first(inverse_0, rhs[:width], n_y, n_z, n_core).reshape(n_cols, sub, slab), COLS), axis=0
-    )
+        return rows_at(trail_factor[:, 1], at)
+
+    far = n_z // 2
+    near = [by for by in range(1, n_z) if by != far]
+    own_0, own_1 = {0: trail_0(z_at)}, {0: trail_1(z_at)}
+    terms = apply_first(inverse_0, rhs[:width], n_y, n_z, n_core)
+    own_1[far] = moved(trail_1, far, slab_gram)
+    own_1.update({by: moved(trail_1, by, terms) for by in near})
+    first = after(summed(terms.reshape(n_cols, sub, slab), COLS), *own_1.values())
     first_pieces = spread_z(first)
-    first_out = solution_rows(first)
-    early = lax.optimization_barrier((trail_factor[:, 0], gram_slots[2:], first_pieces))
-    own_0 = {by: moved(trail_0, by) for by in range(n_z) if by != n_z // 2}
-    first_all = [first_pieces] + [shift(first_pieces, "x", -d) for d in range(1, n_x)]
-    second_rhs = rhs[width:] - product(below, first_pieces)
-    second_rhs = after(second_rhs, *own_0.values())
+    first_all = lax.all_gather(first_pieces, "x", axis=0, tiled=False)
+    first_piece = solution_piece(first)
+    first_out = lax.all_gather(first_piece, COLS, axis=0, tiled=False)
+
+    terms = apply_matrix(where_z, below, first_pieces, n_y)
+    own_0.update({by: moved(trail_0, by, terms) for by in near})
+    second_rhs = after(rhs[width:] - summed(terms, "y"), first_piece, *own_0.values())
     second_pieces = spread_z(second_rhs)
-    early = lax.optimization_barrier((trail_factor[:, 0], gram_slots[2:], second_pieces))
-    late = after(trail_factor[:, 1], second_pieces)
-    own_0[n_z // 2] = moved(trail_0, n_z // 2)
-    own_0 = [own_0[by] for by in range(n_z)]
-    own_1 = {by: moved(trail_1, by) for by in range(n_z) if by != n_z // 2}
-    late = after(trail_factor[:, 1], outgoing)
-    own_1[n_z // 2] = after(moved(trail_1, n_z // 2), slab_gram)
-    own_1 = [own_1[by] for by in range(n_z)]
+
+    terms = apply_matrix(where_z, inverse_1, second_pieces, n_y)
+    own_0[far] = moved(trail_0, far, terms)
+    own_0, own_1 = ([own[by] for by in range(n_z)] for own in (own_0, own_1))
     other_0 = [shift(v, "core", 1) for v in own_0]
     other_1 = [shift(v, "core", 1) for v in own_1]
 
     trail_owner = col // n_z * n_z + jnp.arange(n_z, dtype=jnp.int32)
-    slab_order = ((x_at + jnp.arange(n_x, dtype=jnp.int32)) % n_x * n_core + core)[:, None] * slab
+    slab_order = (jnp.arange(n_x, dtype=jnp.int32) * n_core + core)[:, None] * slab
     list_order = (slab_order + jnp.arange(slab, dtype=jnp.int32)[None, :]).reshape(-1)
     to_lists = (
         (jnp.take(slots_of, list_order)[None, None, :] == slot_range[None, :, None])
         & (jnp.take(owners, list_order)[None, None, :] == trail_owner[:, None, None])
     ).astype(BF16)
-    where = jnp.stack([x_at, z_at]).astype(jnp.int32)
-    base = apply_trail(where, own_0, other_0, width, first_all, to_lists, True, n_x)
-
-    second = after(product(inverse_1, second_pieces), own_0[n_z // 2], *own_1, *first_all)
-    second_out = solution_rows(second)
+    base = apply_trail(where_z, own_0, other_0, width, first_all, to_lists, True)
+
+    second = after(summed(terms, "y"), own_0[far])
+    piece = solution_piece(second)
+    piece = jnp.stack([piece] + [shift(piece, "z", by) for by in range(1, n_z)])
+    second_out = [piece] + [shift(piece, "y", by) for by in range(1, n_y)]
     second_all = spread(second, ("x", "z")).reshape(n_x, n_z, n_core, quarter, slab)
-    terms = apply_trail(where, own_1, other_1, width, [second_all], base, False, n_x)
-    total = jnp.sum(exchange(terms, "y"), axis=0).reshape(n_core, trail_blocks, quarter, slab)
+    terms = apply_trail(where_z, own_1, other_1, width, second_all, base, False)
+    terms = after(terms, *second_out)
+    total = summed(terms, "y").reshape(n_core, trail_blocks, quarter, slab)
     kept, given = total[0], total[1]
     got = shift(given, "core", 1)
     pair = jnp.where(core == 0, jnp.stack([kept, got]), jnp.stack([got, kept]))
     pair = pair.reshape(n_core, trail_blocks, quarter, n_z // n_core, run_len).transpose(0, 3, 1, 2, 4)
     out = exchange(pair.reshape(n_z, trail_blocks, quarter, run_len), "z")
     trail_out = out.transpose(1, 0, 2, 3).reshape(trail_blocks, block_rows, run_len)
-    return as_rows(*(v.reshape(n_y, n_z, quarter, n_core * slab) for v in (first_out, second_out))), trail_out
+    first_out = first_out.reshape(n_y, n_z, quarter, n_core * slab)
+    return as_rows(jnp.stack([y_at, z_at]).astype(jnp.int32), first_out, second_out), trail_out
 
 
 def solution(mesh):

time: 339 us -> 345 us (1.018)
  waiting for transfers between devices: 102 us -> 123 us
  blocking collectives: 58.2 us -> 37.8 us
  starting transfers between devices: 85.3 us -> 89.8 us
    ppermute x21 -> x24, waiting for transfers between devices: 22.3 us -> 61.7 us  [shift(): lax.ppermute(value, axis, [(i, (i + by) % size) for i in range(size)])]
    all_to_all x1, blocking collectives: 58.2 us -> 37.8 us  [exchange(): return lax.all_to_all(value, axes, 0, 0, tiled=True)]
    ppermute x21 -> x24, starting transfers between devices: 29.5 us -> 47.9 us  [shift(): lax.ppermute(value, axis, [(i, (i + by) % size) for i in range(size)])]
    all_to_all x9, waiting for transfers between devices: 78.2 us -> 60.8 us  [exchange(): return lax.all_to_all(value, axes, 0, 0, tiled=True)]
    all_to_all x9, starting transfers between devices: 54.1 us -> 39.5 us  [exchange(): return lax.all_to_all(value, axes, 0, 0, tiled=True)]
    squeeze x3 -> x2, local copies, waits for them, and re-layouts: 4.19 us -> 0.03 us  [solution_piece(): lax.dynamic_index_in_dim(pieces, core ^ m, 0, keepdims=False)]
    slice x3 -> x4, local copies, waits for them, and re-layouts: 1.91 us -> 5.94 us  [the longest x1 4.02 us: trail_0(): trail_factor[:, 0]]
  transfers between devices with their start and end apart: 39 -> 42, of which waited for: 16 -> 21; matrix products, arithmetic and copies ran while one was open for 12% -> 11% of each run, Pallas kernels for 10% -> 10%
where the time goes in v3:
time: 345 us; the launch traced here: 344 us
  waiting for transfers between devices  123 us (36%)
  starting transfers between devices  89.8 us (26%)
  blocking collectives  37.8 us (11%)
  Pallas kernels  34.3 us (10%)
  local copies, waits for them, and re-layouts  27.4 us (8%)
  other arithmetic  14.4 us (4%)
  between operations  14.4 us (4%)
    ppermute x24, waiting for transfers between devices, shift(): lax.ppermute(value, axis, [(i, (i + by) % size) for i in range(size)])  61.7 us
    all_to_all x9, waiting for transfers between devices, exchange(): return lax.all_to_all(value, axes, 0, 0, tiled=True)  60.8 us
    ppermute x24, starting transfers between devices, shift(): lax.ppermute(value, axis, [(i, (i + by) % size) for i in range(size)])  47.9 us
    all_to_all x9, starting transfers between devices, exchange(): return lax.all_to_all(value, axes, 0, 0, tiled=True)  39.5 us
    all_to_all x1, blocking collectives, exchange(): return lax.all_to_all(value, axes, 0, 0, tiled=True)  37.8 us
    pallas_call x2, Pallas kernels, apply_trail(): pl.pallas_call(functools.partial(trail_kernel, n_z, with_gram), grid=(blo...  17 us
    pallas_call x2, Pallas kernels, apply_matrix(): pl.pallas_call(functools.partial(product_kernel, pieces.shape[0]), grid=(...  7.73 us
  transfers between devices with their start and end apart: 42, of which 21 were waited for; matrix products, arithmetic and copies ran while one was open for 11% of the time, Pallas kernels for 10%

profile of v3, /device:TPU:0, one launch (start us, length us, event | category | flops | bytes accessed | tf_op | source)
XLA Modules:
  0.0 343.7 jit_solution(612459351219710208)
XLA Ops:
  7.2 2.1 fusion.33
  10.7 1.6 fusion.3
  13.2 4.4 %all-to-all-start = ((f32[8,16,2,512]{3,1,2,0:T(8,128)}), f32[8,16,2,512]{3,1,2,0:T(8,128)S(1)}, u32[]{:S(2)}, u32[]{:S(2)}) async-start(f32[8,16,2,512]{3,1,2,0:T(8,128)} %copy.15), calls=%async_computation | async-start | bytes 1048576 | tf_op jit(solution)/shard_map/all_to_all | solution.py:30
  17.9 2.0 collective-permute-start.5
  19.9 3.6 %collective-permute-start.6 = (f32[2,128,256]{2,1,0:T(8,128)S(1)}, f32[2,128,256]{2,1,0:T(8,128)S(1)}, u32[]{:S(2)}, u32[]{:S(2)}) collective-permute-start(f32[2,128,256]{2,1,0:T(8,128)S(1)} %get-tuple-element.50), channel_id=1, source_target_pairs={{0,2},{1,3},{2,0},{3,1},{4,6},{5,7},{6,4},{7,5},{8,10},{9,11},{10,... | collective-permute-start | bytes 786440 | tf_op jit(solution)/shard_map/ppermute | solution.py:26
  23.5 1.0 collective-permute-start.7
  24.5 4.5 %collective-permute-done.5 = f32[2,128,256]{2,1,0:T(8,128)S(1)} collective-permute-done((f32[2,128,256]{2,1,0:T(8,128)S(1)}, f32[2,128,256]{2,1,0:T(8,128)S(1)}, u32[]{:S(2)}, u32[]{:S(2)}) %collective-permute-start.5) | collective-permute-done | bytes 262176 | tf_op jit(solution)/shard_map/ppermute | solution.py:26
  28.9 6.8 %collective-permute-done.6 = f32[2,128,256]{2,1,0:T(8,128)S(1)} collective-permute-done((f32[2,128,256]{2,1,0:T(8,128)S(1)}, f32[2,128,256]{2,1,0:T(8,128)S(1)}, u32[]{:S(2)}, u32[]{:S(2)}) %collective-permute-start.6) | collective-permute-done | bytes 262176 | tf_op jit(solution)/shard_map/ppermute | solution.py:26
  38.4 0.9 pad_maximum_fusion.6
  39.3 6.2 %all-to-all-start.1 = ((f32[16,16,512]{2,1,0:T(8,128)}), f32[16,16,512]{2,1,0:T(8,128)S(1)}, u32[]{:S(2)}, u32[]{:S(2)}) async-start(f32[16,16,512]{2,1,0:T(8,128)} %pad_maximum_fusion.6), calls=%async_computation.1 | async-start | bytes 1048576 | tf_op jit(solution)/shard_map/all_to_all | solution.py:30
  45.6 11.6 %all-to-all-done.1 = f32[16,16,512]{2,1,0:T(8,128)S(1)} async-done(((f32[16,16,512]{2,1,0:T(8,128)}), f32[16,16,512]{2,1,0:T(8,128)S(1)}, u32[]{:S(2)}, u32[]{:S(2)}) %all-to-all-start.1) | async-done | bytes 524320 | tf_op jit(solution)/shard_map/all_to_all | solution.py:30
  59.2 5.1 %shard_map.68 = f32[4,4,2,128,128]{4,3,2,1,0:T(8,128)} custom-call(f32[4096,256]{1,0:T(8,128)} %bitcast.106, f32[256,128]{1,0:T(8,128)} %slice.103.operand_ref), custom_call_target="tpu_custom_call" | custom-call | flops 805306368 | bytes 4194304 | tf_op jit(solution)/shard_map/pallas_call | solution.py:84
  64.3 3.7 %all-to-all-start.2 = ((f32[16,256,128]{2,1,0:T(8,128)}), f32[16,256,128]{2,1,0:T(8,128)S(1)}, u32[]{:S(2)}, u32[]{:S(2)}) async-start(f32[16,256,128]{2,1,0:T(8,128)} %bitcast.103), calls=%async_computation.2 | async-start | bytes 4194304 | tf_op jit(solution)/shard_map/all_to_all | solution.py:30
  68.0 4.0 %fusion.32 = (f32[4,1,512,256]{3,2,1,0:T(8,128)}, f32[4,1,512,256]{3,2,1,0:T(8,128)S(1)}) fusion(f32[4,2,512,256]{3,2,1,0:T(8,128)} %param.11), kind=kLoop, calls=%fused_computation.115 | loop fusion | bytes 8388608 | tf_op jit(solution)/shard_map/slice | solution.py:320
  72.0 1.2 dynamic-slice_bitcast_fusion.4
  73.2 3.3 collective-permute-start
  76.5 1.2 collective-permute-start.2
  77.6 0.9 collective-permute-start.1
  78.5 1.1 slice.92
  79.6 17.0 %all-to-all-done.2 = f32[16,256,128]{2,1,0:T(8,128)S(1)} async-done(((f32[16,256,128]{2,1,0:T(8,128)}), f32[16,256,128]{2,1,0:T(8,128)S(1)}, u32[]{:S(2)}, u32[]{:S(2)}) %all-to-all-start.2) | async-done | bytes 2097184 | tf_op jit(solution)/shard_map/all_to_all | solution.py:30
  96.7 10.8 %collective-permute-done.refs_2_ = f32[4,128,256]{2,1,0:T(8,128)} collective-permute-done((f32[4,128,256]{2,1,0:T(8,128)}, f32[4,128,256]{2,1,0:T(8,128)}, u32[]{:S(2)}, u32[]{:S(2)}) %collective-permute-start) | collective-permute-done | bytes 524320 | tf_op jit(solution)/shard_map/ppermute | solution.py:26
  107.5 8.8 %collective-permute-done.2.refs_3_ = f32[4,128,256]{2,1,0:T(8,128)} collective-permute-done((f32[4,128,256]{2,1,0:T(8,128)}, f32[4,128,256]{2,1,0:T(8,128)}, u32[]{:S(2)}, u32[]{:S(2)}) %collective-permute-start.2) | collective-permute-done | bytes 524320 | tf_op jit(solution)/shard_map/ppermute | solution.py:26
  117.1 3.5 %all-to-all-start.3 = ((f32[4,256,128]{2,1,0:T(8,128)}), f32[4,256,128]{2,1,0:T(8,128)S(1)}, u32[]{:S(2)}, u32[]{:S(2)}) async-start(f32[4,256,128]{2,1,0:T(8,128)} %broadcast_in_dim.41), calls=%async_computation.3 | async-start | bytes 1048576 | tf_op jit(solution)/shard_map/all_to_all | solution.py:30
  120.6 2.0 constant_dynamic-slice_fusion
  122.6 1.2 dynamic-slice_bitcast_fusion
  123.8 1.3 pad_maximum_fusion.3
  125.1 4.8 %all-to-all-done.3 = f32[4,256,128]{2,1,0:T(8,128)S(1)} async-done(((f32[4,256,128]{2,1,0:T(8,128)}), f32[4,256,128]{2,1,0:T(8,128)S(1)}, u32[]{:S(2)}, u32[]{:S(2)}) %all-to-all-start.3) | async-done | bytes 524320 | tf_op jit(solution)/shard_map/all_to_all | solution.py:30
  130.7 3.9 %shard_map.69 = f32[4,256,128]{2,1,0:T(8,128)} custom-call(s32[1]{0:T(128)} %bitcast.1.at_ref, f32[1024,1024]{1,0:T(8,128)} %all-gather.11.cloned.1.call-done.matrix_ref, f32[4,2,128,128]{3,2,1,0:T(8,128)} %bitcast.104), custom_call_target="tpu_custom_call" | custom-call | flops 805306368 | bytes 4194304 | tf_op jit(solution)/shard_map/pallas_call | solution.py:102
  134.6 1.2 collective-permute-start.9
  136.6 3.7 %all-to-all-start.4 = ((f32[4,256,128]{2,1,0:T(8,128)}), f32[4,256,128]{2,1,0:T(8,128)S(1)}, u32[]{:S(2)}, u32[]{:S(2)}) async-start(f32[4,256,128]{2,1,0:T(8,128)} %shard_map.69), calls=%async_computation.4 | async-start | bytes 1048576 | tf_op jit(solution)/shard_map/all_to_all | solution.py:30
  140.3 1.1 pad_maximum_fusion.2.refs_0_.refs_8_
  141.5 7.0 %all-to-all-done.4 = f32[4,256,128]{2,1,0:T(8,128)S(1)} async-done(((f32[4,256,128]{2,1,0:T(8,128)}), f32[4,256,128]{2,1,0:T(8,128)S(1)}, u32[]{:S(2)}, u32[]{:S(2)}) %all-to-all-start.4) | async-done | bytes 524320 | tf_op jit(solution)/shard_map/all_to_all | solution.py:30
  148.5 0.9 slice_subtract_fusion
  149.4 3.1 collective-permute-done.9.refs_3_.refs_11_
  152.5 2.1 collective-permute-done.8.refs_1_.refs_9_
  155.4 3.5 %all-to-all-start.5 = ((f32[4,256,128]{2,1,0:T(8,128)}), f32[4,256,128]{2,1,0:T(8,128)S(1)}, u32[]{:S(2)}, u32[]{:S(2)}) async-start(f32[4,256,128]{2,1,0:T(8,128)} %broadcast_in_dim.42), calls=%async_computation.5 | async-start | bytes 1048576 | tf_op jit(solution)/shard_map/all_to_all | solution.py:30
  158.9 2.0 pad_maximum_fusion.5
  160.9 6.1 %all-to-all-done.5 = f32[4,256,128]{2,1,0:T(8,128)S(1)} async-done(((f32[4,256,128]{2,1,0:T(8,128)}), f32[4,256,128]{2,1,0:T(8,128)S(1)}, u32[]{:S(2)}, u32[]{:S(2)}) %all-to-all-start.5) | async-done | bytes 524320 | tf_op jit(solution)/shard_map/all_to_all | solution.py:30
  167.8 3.8 %shard_map.70 = f32[4,256,128]{2,1,0:T(8,128)} custom-call(s32[1]{0:T(128)} %bitcast.1.at_ref, f32[1024,1024]{1,0:T(8,128)} %all-gather.9.cloned.1.call-done.matrix_ref, f32[4,2,128,128]{3,2,1,0:T(8,128)} %bitcast.110), custom_call_target="tpu_custom_call" | custom-call | flops 805306368 | bytes 4194304 | tf_op jit(solution)/shard_map/pallas_call | solution.py:102
  172.7 4.3 %all-to-all-start.6 = ((f32[4,256,128]{2,1,0:T(8,128)}), f32[4,256,128]{2,1,0:T(8,128)}, u32[]{:S(2)}, u32[]{:S(2)}) async-start(f32[4,256,128]{2,1,0:T(8,128)} %shard_map.70), calls=%async_computation.6 | async-start | bytes 1048576 | tf_op jit(solution)/shard_map/all_to_all | solution.py:30
  177.2 9.7 %all-to-all-done.6 = f32[4,256,128]{2,1,0:T(8,128)} async-done(((f32[4,256,128]{2,1,0:T(8,128)}), f32[4,256,128]{2,1,0:T(8,128)}, u32[]{:S(2)}, u32[]{:S(2)}) %all-to-all-start.6) | async-done | bytes 524320 | tf_op jit(solution)/shard_map/all_to_all | solution.py:30
  186.9 1.1 reduce_sum.78
  188.0 0.9 collective-permute-done.10.refs_2_.refs_10_
  188.8 1.6 broadcast_in_dim.45
  190.4 5.9 %all-to-all-start.7 = ((f32[16,256,128]{2,1,0:T(8,128)}), f32[16,256,128]{2,1,0:T(8,128)}, u32[]{:S(2)}, u32[]{:S(2)}) async-start(f32[16,256,128]{2,1,0:T(8,128)} %broadcast_in_dim.45), calls=%async_computation.7 | async-start | bytes 4194304 | tf_op jit(solution)/shard_map/all_to_all | solution.py:30
  196.4 2.3 gather_fusion
  198.7 2.3 gather_fusion.1
  204.7 1.9 collective-permute-start.13
  207.3 2.8 collective-permute-start.14
  210.1 13.8 %collective-permute-done.13 = f32[128,256]{1,0:T(8,128)} collective-permute-done((f32[128,256]{1,0:T(8,128)S(1)}, f32[128,256]{1,0:T(8,128)}, u32[]{:S(2)}, u32[]{:S(2)}) %collective-permute-start.13) | collective-permute-done | bytes 131104 | tf_op jit(solution)/shard_map/ppermute | solution.py:26
  223.9 2.8 collective-permute-start.15
  226.7 0.9 and_convert_fusion.refs_16_
  229.2 1.7 pad_maximum_fusion.9.refs_0_
  231.0 15.9 %collective-permute-start.16 = (f32[4,128,256]{2,1,0:T(8,128)}, f32[4,128,256]{2,1,0:T(8,128)S(1)}, u32[]{:S(2)}, u32[]{:S(2)}) collective-permute-start(f32[4,128,256]{2,1,0:T(8,128)} %pad_maximum_fusion.9.refs_0_), channel_id=1, source_target_pairs={{0,4},{4,8},{8,12},{12,0},{1,5},{5,9},{9,13},{13,1},{2,6},{6,10},{... | collective-permute-start | bytes 1572872 | tf_op jit(solution)/shard_map/ppermute | solution.py:26
  246.9 8.6 %collective-permute-start.17 = (f32[4,128,256]{2,1,0:T(8,128)}, f32[4,128,256]{2,1,0:T(8,128)S(1)}, u32[]{:S(2)}, u32[]{:S(2)}) collective-permute-start(f32[4,128,256]{2,1,0:T(8,128)} %pad_maximum_fusion.9.refs_0_), channel_id=1, source_target_pairs={{0,8},{4,12},{8,0},{12,4},{1,9},{5,13},{9,1},{13,5},{2,10},{6,14},... | collective-permute-start | bytes 1572872 | tf_op jit(solution)/shard_map/ppermute | solution.py:26
  255.5 8.9 %shard_map.72.refs_8_ = f32[4,2,4,128,128]{4,3,2,1,0:T(8,128)} custom-call(s32[1]{0:T(128)} %bitcast.1.at_ref, f32[4,4,2,128,128]{4,3,2,1,0:T(8,128)} %all-gather.13.cloned.1.call-done.lists_ref, f32[4,128,384]{2,1,0:T(8,128)} %copy-done.1, f32[4,128,384]{2,1,0:T(8,128)} %copy-done.4, f32[4,128,384]{2,1,0:T(8,128)} %copy-done.5, f32[4,128,384]{2,1,0:T(8,128)} %copy-done.3, ...), custom_call_target="tpu_custom_call" | custom-call | flops 3221225472 | bytes 10485760 | tf_op jit(solution)/shard_map/pallas_call | solution.py:170
  264.5 8.1 %shard_map.73 = f32[4,2,4,128,128]{4,3,2,1,0:T(8,128)} custom-call(s32[1]{0:T(128)} %bitcast.1.at_ref, f32[4,4,2,128,128]{4,3,2,1,0:T(8,128)} %bitcast.45.lists_ref, f32[4,128,256]{2,1,0:T(8,128)} %get-tuple-element.44.refs_0_, f32[4,128,256]{2,1,0:T(8,128)} %collective-permute-done.1.refs_1_, f32[4,128,256]{2,1,0:T(8,128)} %collective-permute-done.refs_2_, ...), custom_call_target="tpu_custom_call" | custom-call | flops 3221225472 | bytes 10485760 | tf_op jit(solution)/shard_map/pallas_call | solution.py:170
  272.6 7.9 %collective-permute-done.17.refs_2_ = f32[4,128,256]{2,1,0:T(8,128)S(1)} collective-permute-done((f32[4,128,256]{2,1,0:T(8,128)}, f32[4,128,256]{2,1,0:T(8,128)S(1)}, u32[]{:S(2)}, u32[]{:S(2)}) %collective-permute-start.17) | collective-permute-done | bytes 524320 | tf_op jit(solution)/shard_map/ppermute | solution.py:26
  281.3 37.8 %all_to_all.50 = f32[4,2,4,128,128]{4,3,2,1,0:T(8,128)S(1)} all-to-all(f32[4,2,4,128,128]{4,3,2,1,0:T(8,128)} %shard_map.73), channel_id=1, replica_groups=mesh['x'=4,'core'=2,'y'=4,'z'=4] {'y'}, dimensions={0} | all-to-all | bytes 4194304 | tf_op jit(solution)/shard_map/all_to_all | solution.py:30
  319.4 1.5 collective-permute-done.27
  321.2 1.1 copy.18
  322.3 4.2 %all-to-all-start.9 = ((f32[4,4,128,64]{2,3,1,0:T(8,128)}), f32[4,4,128,64]{2,3,1,0:T(8,128)S(1)}, u32[]{:S(2)}, u32[]{:S(2)}) async-start(f32[4,4,128,64]{2,3,1,0:T(8,128)} %bitcast.50), calls=%async_computation.9 | async-start | bytes 1048576 | tf_op jit(solution)/shard_map/all_to_all | solution.py:30
  327.2 4.5 %shard_map.71 = f32[2,512,1024]{2,1,0:T(8,128)} custom-call(s32[2]{0:T(128)} %pad_add_fusion.at_ref, f32[4,4,128,256]{3,2,1,0:T(8,128)} %bitcast.109, f32[4,128,256]{2,1,0:T(8,128)} %pad_maximum_fusion.9.refs_0_, f32[4,128,256]{2,1,0:T(8,128)} %copy-done.11, f32[4,128,256]{2,1,0:T(8,128)} %copy-done.12, f32[4,128,256]{2,1,0:T(8,128)} %collective-permute-done.18.refs_3_), custom_call_target="tpu_custom_call" | custom-call | bytes 8388608 | tf_op jit(solution)/shard_map/pallas_call | solution.py:200
  331.7 4.6 %all-to-all-done.9 = f32[4,4,128,64]{2,3,1,0:T(8,128)S(1)} async-done(((f32[4,4,128,64]{2,3,1,0:T(8,128)}), f32[4,4,128,64]{2,3,1,0:T(8,128)S(1)}, u32[]{:S(2)}, u32[]{:S(2)}) %all-to-all-start.9) | async-done | bytes 524320 | tf_op jit(solution)/shard_map/all_to_all | solution.py:30
  (132 shorter events, 21.6 us)
Async XLA Ops:
  7.2 2.2 copy-start.14
  7.2 52.0 %all-gather.15.cloned.1.call-start = ((), (), s32[]{:S(2)}) async-start(), calls=%async_computation.14 | async-start | bytes 4718592 | tf_op jit(solution)/shard_map/all_gather | solution.py:268
  9.3 8.3 %copy-start.13 = (f32[512,256]{1,0:T(8,128)S(1)}, f32[512,256]{1,0:T(8,128)}, u32[]{:S(2)}) copy-start(f32[512,256]{1,0:T(8,128)} %param.10) | copy-start | bytes 1572868
  13.2 22.5 %all-to-all-start = ((f32[8,16,2,512]{3,1,2,0:T(8,128)}), f32[8,16,2,512]{3,1,2,0:T(8,128)S(1)}, u32[]{:S(2)}, u32[]{:S(2)}) async-start(f32[8,16,2,512]{3,1,2,0:T(8,128)} %copy.15), calls=%async_computation | async-start | bytes 1048576 | tf_op jit(solution)/shard_map/all_to_all | solution.py:30
  17.6 107.5 %all-gather.11.cloned.1.call-start = ((), (), s32[]{:S(2)}) async-start(), calls=%async_computation.12 | async-start | bytes 4718592 | tf_op jit(solution)/shard_map/all_gather | solution.py:266
  17.9 11.0 %collective-permute-start.5 = (f32[2,128,256]{2,1,0:T(8,128)S(1)}, f32[2,128,256]{2,1,0:T(8,128)S(1)}, u32[]{:S(2)}, u32[]{:S(2)}) collective-permute-start(f32[2,128,256]{2,1,0:T(8,128)S(1)} %get-tuple-element.51), channel_id=1, source_target_pairs={{0,1},{1,2},{2,3},{3,0},{4,5},{5,6},{6,7},{7,4},{8,9},{9,10},{10,1... | collective-permute-start | bytes 786440 | tf_op jit(solution)/shard_map/ppermute | solution.py:26
  19.9 15.8 %collective-permute-start.6 = (f32[2,128,256]{2,1,0:T(8,128)S(1)}, f32[2,128,256]{2,1,0:T(8,128)S(1)}, u32[]{:S(2)}, u32[]{:S(2)}) collective-permute-start(f32[2,128,256]{2,1,0:T(8,128)S(1)} %get-tuple-element.50), channel_id=1, source_target_pairs={{0,2},{1,3},{2,0},{3,1},{4,6},{5,7},{6,4},{7,5},{8,10},{9,11},{10,... | collective-permute-start | bytes 786440 | tf_op jit(solution)/shard_map/ppermute | solution.py:26
  23.5 12.3 %collective-permute-start.7 = (f32[2,128,256]{2,1,0:T(8,128)S(1)}, f32[2,128,256]{2,1,0:T(8,128)S(1)}, u32[]{:S(2)}, u32[]{:S(2)}) collective-permute-start(f32[2,128,256]{2,1,0:T(8,128)S(1)} %get-tuple-element.49), channel_id=1, source_target_pairs={{0,3},{1,0},{2,1},{3,2},{4,7},{5,4},{6,5},{7,6},{8,11},{9,8},{10,9... | collective-permute-start | bytes 786440 | tf_op jit(solution)/shard_map/ppermute | solution.py:26
  36.7 124.2 %all-gather.9.cloned.1.call-start = ((), (), s32[]{:S(2)}) async-start(), calls=%async_computation.11 | async-start | bytes 4718592 | tf_op jit(solution)/shard_map/all_gather | solution.py:266
  39.3 18.0 %all-to-all-start.1 = ((f32[16,16,512]{2,1,0:T(8,128)}), f32[16,16,512]{2,1,0:T(8,128)S(1)}, u32[]{:S(2)}, u32[]{:S(2)}) async-start(f32[16,16,512]{2,1,0:T(8,128)} %pad_maximum_fusion.6), calls=%async_computation.1 | async-start | bytes 1048576 | tf_op jit(solution)/shard_map/all_to_all | solution.py:30
  57.8 0.7 copy-start.10
  64.3 32.4 %all-to-all-start.2 = ((f32[16,256,128]{2,1,0:T(8,128)}), f32[16,256,128]{2,1,0:T(8,128)S(1)}, u32[]{:S(2)}, u32[]{:S(2)}) async-start(f32[16,256,128]{2,1,0:T(8,128)} %bitcast.103), calls=%async_computation.2 | async-start | bytes 4194304 | tf_op jit(solution)/shard_map/all_to_all | solution.py:30
  72.0 6.5 %copy-start.8 = (f32[6,512,128]{2,1,0:T(8,128)S(1)}, f32[6,512,128]{2,1,0:T(8,128)}, u32[]{:S(2)}) copy-start(f32[6,512,128]{2,1,0:T(8,128)} %param.8) | copy-start | bytes 4718596
  73.2 34.3 %collective-permute-start = (f32[4,128,256]{2,1,0:T(8,128)}, f32[4,128,256]{2,1,0:T(8,128)}, u32[]{:S(2)}, u32[]{:S(2)}) collective-permute-start(f32[4,128,256]{2,1,0:T(8,128)} %get-tuple-element.18), channel_id=1, source_target_pairs={{0,2},{1,3},{2,0},{3,1},{4,6},{5,7},{6,4},{7,5},{8,10},{9,11},{10,... | collective-permute-start | bytes 1572872 | tf_op jit(solution)/shard_map/ppermute | solution.py:26
  76.5 39.8 %collective-permute-start.2 = (f32[4,128,256]{2,1,0:T(8,128)}, f32[4,128,256]{2,1,0:T(8,128)}, u32[]{:S(2)}, u32[]{:S(2)}) collective-permute-start(f32[4,128,256]{2,1,0:T(8,128)} %get-tuple-element.20), channel_id=1, source_target_pairs={{0,3},{1,0},{2,1},{3,2},{4,7},{5,4},{6,5},{7,6},{8,11},{9,8},{10,9... | collective-permute-start | bytes 1572872 | tf_op jit(solution)/shard_map/ppermute | solution.py:26
  77.6 38.6 %collective-permute-start.1 = (f32[4,128,256]{2,1,0:T(8,128)S(1)}, f32[4,128,256]{2,1,0:T(8,128)}, u32[]{:S(2)}, u32[]{:S(2)}) collective-permute-start(f32[4,128,256]{2,1,0:T(8,128)S(1)} %get-tuple-element.19), channel_id=1, source_target_pairs={{0,1},{1,2},{2,3},{3,0},{4,5},{5,6},{6,7},{7,4},{8,9},{9,10},{10,1... | collective-permute-start | bytes 1572872 | tf_op jit(solution)/shard_map/ppermute | solution.py:26
  96.7 25.9 %copy-start = (f32[4,1,512,256]{3,2,1,0:T(8,128)S(1)}, f32[4,1,512,256]{3,2,1,0:T(8,128)}, u32[]{:S(2)}) copy-start(f32[4,1,512,256]{3,2,1,0:T(8,128)} %get-tuple-element.35) | copy-start | bytes 6291460
  117.1 12.8 %all-to-all-start.3 = ((f32[4,256,128]{2,1,0:T(8,128)}), f32[4,256,128]{2,1,0:T(8,128)S(1)}, u32[]{:S(2)}, u32[]{:S(2)}) async-start(f32[4,256,128]{2,1,0:T(8,128)} %broadcast_in_dim.41), calls=%async_computation.3 | async-start | bytes 1048576 | tf_op jit(solution)/shard_map/all_to_all | solution.py:30
  120.6 134.9 %all-gather.13.cloned.1.call-start = ((), (), s32[]{:S(2)}) async-start(), calls=%async_computation.13 | async-start | bytes 2621440 | tf_op jit(solution)/shard_map/all_gather | solution.py:333
  129.9 0.8 copy-start.2
  130.7 9.6 %copy-start.9 = (f32[4,128,128]{2,1,0:T(8,128)S(1)}, f32[4,128,128]{2,1,0:T(8,128)}, u32[]{:S(2)}) copy-start(f32[4,128,128]{2,1,0:T(8,128)} %get-tuple-element.48) | copy-start | bytes 786436
  134.6 17.9 %collective-permute-start.9 = (f32[4,128,384]{2,1,0:T(8,128)}, f32[4,128,384]{2,1,0:T(8,128)S(1)}, u32[]{:S(2)}, u32[]{:S(2)}) collective-permute-start(f32[4,128,384]{2,1,0:T(8,128)} %get-tuple-element.28), channel_id=1, source_target_pairs={{0,3},{1,0},{2,1},{3,2},{4,7},{5,4},{6,5},{7,6},{8,11},{9,8},{10,9... | collective-permute-start | bytes 2359304 | tf_op jit(solution)/shard_map/ppermute | solution.py:26
  135.8 18.8 %collective-permute-start.8 = (f32[4,128,384]{2,1,0:T(8,128)}, f32[4,128,384]{2,1,0:T(8,128)S(1)}, u32[]{:S(2)}, u32[]{:S(2)}) collective-permute-start(f32[4,128,384]{2,1,0:T(8,128)} %get-tuple-element.27), channel_id=1, source_target_pairs={{0,1},{1,2},{2,3},{3,0},{4,5},{5,6},{6,7},{7,4},{8,9},{9,10},{10,1... | collective-permute-start | bytes 2359304 | tf_op jit(solution)/shard_map/ppermute | solution.py:26
  136.6 11.8 %all-to-all-start.4 = ((f32[4,256,128]{2,1,0:T(8,128)}), f32[4,256,128]{2,1,0:T(8,128)S(1)}, u32[]{:S(2)}, u32[]{:S(2)}) async-start(f32[4,256,128]{2,1,0:T(8,128)} %shard_map.69), calls=%async_computation.4 | async-start | bytes 1048576 | tf_op jit(solution)/shard_map/all_to_all | solution.py:30
  141.5 30.8 %copy-start.1 = (f32[4,128,384]{2,1,0:T(8,128)}, f32[4,128,384]{2,1,0:T(8,128)S(1)}, u32[]{:S(2)}) copy-start(f32[4,128,384]{2,1,0:T(8,128)S(1)} %pad_maximum_fusion.2.refs_0_.refs_8_) | copy-start | bytes 2359300
  152.5 51.3 %copy-start.3 = (f32[4,128,384]{2,1,0:T(8,128)}, f32[4,128,384]{2,1,0:T(8,128)S(1)}, u32[]{:S(2)}) copy-start(f32[4,128,384]{2,1,0:T(8,128)S(1)} %collective-permute-done.9.refs_3_.refs_11_) | copy-start | bytes 2359300
  154.6 49.5 %copy-start.4 = (f32[4,128,384]{2,1,0:T(8,128)}, f32[4,128,384]{2,1,0:T(8,128)S(1)}, u32[]{:S(2)}) copy-start(f32[4,128,384]{2,1,0:T(8,128)S(1)} %collective-permute-done.8.refs_1_.refs_9_) | copy-start | bytes 2359300
  155.4 11.5 %all-to-all-start.5 = ((f32[4,256,128]{2,1,0:T(8,128)}), f32[4,256,128]{2,1,0:T(8,128)S(1)}, u32[]{:S(2)}, u32[]{:S(2)}) async-start(f32[4,256,128]{2,1,0:T(8,128)} %broadcast_in_dim.42), calls=%async_computation.5 | async-start | bytes 1048576 | tf_op jit(solution)/shard_map/all_to_all | solution.py:30
  167.0 0.8 copy-start.7
  171.7 17.2 %collective-permute-start.10 = (f32[4,128,384]{2,1,0:T(8,128)}, f32[4,128,384]{2,1,0:T(8,128)S(1)}, u32[]{:S(2)}, u32[]{:S(2)}) collective-permute-start(f32[4,128,384]{2,1,0:T(8,128)} %pad_maximum_fusion.5), channel_id=1, source_target_pairs={{0,2},{1,3},{2,0},{3,1},{4,6},{5,7},{6,4},{7,5},{8,10},{9,11},{10,... | collective-permute-start | bytes 2359304 | tf_op jit(solution)/shard_map/ppermute | solution.py:26
  172.2 31.8 %collective-permute-start.23 = (f32[4,128,384]{2,1,0:T(8,128)S(1)}, f32[4,128,384]{2,1,0:T(8,128)}, u32[]{:S(2)}, u32[]{:S(2)}) collective-permute-start(f32[4,128,384]{2,1,0:T(8,128)S(1)} %pad_maximum_fusion.2.refs_0_.refs_8_), channel_id=1, source_target_pairs={{0,16},{16,0},{1,17},{17,1},{2,18},{18,2},{3,19},{19,3},{4,20},{20... | collective-permute-start | bytes 2359304 | tf_op jit(solution)/shard_map/ppermute | solution.py:26
  172.2 31.6 %collective-permute-start.19 = (f32[4,128,256]{2,1,0:T(8,128)}, f32[4,128,256]{2,1,0:T(8,128)}, u32[]{:S(2)}, u32[]{:S(2)}) collective-permute-start(f32[4,128,256]{2,1,0:T(8,128)} %get-tuple-element.44.refs_0_), channel_id=1, source_target_pairs={{0,16},{16,0},{1,17},{17,1},{2,18},{18,2},{3,19},{19,3},{4,20},{20... | collective-permute-start | bytes 1572872 | tf_op jit(solution)/shard_map/ppermute | solution.py:26
  172.7 14.1 %all-to-all-start.6 = ((f32[4,256,128]{2,1,0:T(8,128)}), f32[4,256,128]{2,1,0:T(8,128)}, u32[]{:S(2)}, u32[]{:S(2)}) async-start(f32[4,256,128]{2,1,0:T(8,128)} %shard_map.70), calls=%async_computation.6 | async-start | bytes 1048576 | tf_op jit(solution)/shard_map/all_to_all | solution.py:30
  188.8 15.6 %copy-start.5 = (f32[4,128,384]{2,1,0:T(8,128)}, f32[4,128,384]{2,1,0:T(8,128)S(1)}, u32[]{:S(2)}) copy-start(f32[4,128,384]{2,1,0:T(8,128)S(1)} %collective-permute-done.10.refs_2_.refs_10_) | copy-start | bytes 2359300
  190.4 74.0 %all-to-all-start.7 = ((f32[16,256,128]{2,1,0:T(8,128)}), f32[16,256,128]{2,1,0:T(8,128)}, u32[]{:S(2)}, u32[]{:S(2)}) async-start(f32[16,256,128]{2,1,0:T(8,128)} %broadcast_in_dim.45), calls=%async_computation.7 | async-start | bytes 4194304 | tf_op jit(solution)/shard_map/all_to_all | solution.py:30
  196.4 130.9 %all-gather.7.cloned.1.call-start = ((), (), s32[]{:S(2)}) async-start(), calls=%async_computation.10 | async-start | bytes 2228224 | tf_op jit(solution)/shard_map/all_gather | solution.py:335
  201.2 6.1 %collective-permute-start.21 = (f32[4,128,256]{2,1,0:T(8,128)}, f32[4,128,256]{2,1,0:T(8,128)}, u32[]{:S(2)}, u32[]{:S(2)}) collective-permute-start(f32[4,128,256]{2,1,0:T(8,128)} %collective-permute-done.refs_2_), channel_id=1, source_target_pairs={{0,16},{16,0},{1,17},{17,1},{2,18},{18,2},{3,19},{19,3},{4,20},{20... | collective-permute-start | bytes 1572872 | tf_op jit(solution)/shard_map/ppermute | solution.py:26
  201.3 1.2 collective-permute-start.11
  201.9 1.5 collective-permute-start.12
  202.5 1.9 collective-permute-start.3
  203.4 1.3 collective-permute-start.4
  203.8 27.2 %collective-permute-start.26 = (f32[4,128,384]{2,1,0:T(8,128)S(1)}, f32[4,128,384]{2,1,0:T(8,128)}, u32[]{:S(2)}, u32[]{:S(2)}) collective-permute-start(f32[4,128,384]{2,1,0:T(8,128)S(1)} %collective-permute-done.9.refs_3_.refs_11_), channel_id=1, source_target_pairs={{0,16},{16,0},{1,17},{17,1},{2,18},{18,2},{3,19},{19,3},{4,20},{20... | collective-permute-start | bytes 2359304 | tf_op jit(solution)/shard_map/ppermute | solution.py:26
  204.0 42.8 %collective-permute-start.24 = (f32[4,128,384]{2,1,0:T(8,128)S(1)}, f32[4,128,384]{2,1,0:T(8,128)S(1)}, u32[]{:S(2)}, u32[]{:S(2)}) collective-permute-start(f32[4,128,384]{2,1,0:T(8,128)S(1)} %collective-permute-done.8.refs_1_.refs_9_), channel_id=1, source_target_pairs={{0,16},{16,0},{1,17},{17,1},{2,18},{18,2},{3,19},{19,3},{4,20},{20... | collective-permute-start | bytes 2359304 | tf_op jit(solution)/shard_map/ppermute | solution.py:26
  204.4 51.1 %collective-permute-start.25 = (f32[4,128,384]{2,1,0:T(8,128)S(1)}, f32[4,128,384]{2,1,0:T(8,128)}, u32[]{:S(2)}, u32[]{:S(2)}) collective-permute-start(f32[4,128,384]{2,1,0:T(8,128)S(1)} %collective-permute-done.10.refs_2_.refs_10_), channel_id=1, source_target_pairs={{0,16},{16,0},{1,17},{17,1},{2,18},{18,2},{3,19},{19,3},{4,20},{20... | collective-permute-start | bytes 2359304 | tf_op jit(solution)/shard_map/ppermute | solution.py:26
  204.7 19.2 %collective-permute-start.13 = (f32[128,256]{1,0:T(8,128)S(1)}, f32[128,256]{1,0:T(8,128)}, u32[]{:S(2)}, u32[]{:S(2)}) collective-permute-start(f32[128,256]{1,0:T(8,128)S(1)} %maximum_select_fusion.3), channel_id=1, source_target_pairs={{0,1},{1,2},{2,3},{3,0},{4,5},{5,6},{6,7},{7,4},{8,9},{9,10},{10,1... | collective-permute-start | bytes 393224 | tf_op jit(solution)/shard_map/ppermute | solution.py:26
  207.3 21.1 %collective-permute-start.14 = (f32[128,256]{1,0:T(8,128)S(1)}, f32[128,256]{1,0:T(8,128)S(1)}, u32[]{:S(2)}, u32[]{:S(2)}) collective-permute-start(f32[128,256]{1,0:T(8,128)S(1)} %maximum_select_fusion.3), channel_id=1, source_target_pairs={{0,2},{1,3},{2,0},{3,1},{4,6},{5,7},{6,4},{7,5},{8,10},{9,11},{10,... | collective-permute-start | bytes 393224 | tf_op jit(solution)/shard_map/ppermute | solution.py:26
  223.9 5.4 %collective-permute-start.15 = (f32[128,256]{1,0:T(8,128)S(1)}, f32[128,256]{1,0:T(8,128)S(1)}, u32[]{:S(2)}, u32[]{:S(2)}) collective-permute-start(f32[128,256]{1,0:T(8,128)S(1)} %maximum_select_fusion.3), channel_id=1, source_target_pairs={{0,3},{1,0},{2,1},{3,2},{4,7},{5,4},{6,5},{7,6},{8,11},{9,8},{10,9... | collective-permute-start | bytes 393224 | tf_op jit(solution)/shard_map/ppermute | solution.py:26
  228.4 36.1 %collective-permute-start.22 = (f32[4,128,256]{2,1,0:T(8,128)}, f32[4,128,256]{2,1,0:T(8,128)}, u32[]{:S(2)}, u32[]{:S(2)}) collective-permute-start(f32[4,128,256]{2,1,0:T(8,128)} %collective-permute-done.2.refs_3_), channel_id=1, source_target_pairs={{0,16},{16,0},{1,17},{17,1},{2,18},{18,2},{3,19},{19,3},{4,20},{20... | collective-permute-start | bytes 1572872 | tf_op jit(solution)/shard_map/ppermute | solution.py:26
  229.2 35.2 %collective-permute-start.20 = (f32[4,128,256]{2,1,0:T(8,128)}, f32[4,128,256]{2,1,0:T(8,128)}, u32[]{:S(2)}, u32[]{:S(2)}) collective-permute-start(f32[4,128,256]{2,1,0:T(8,128)} %collective-permute-done.1.refs_1_), channel_id=1, source_target_pairs={{0,16},{16,0},{1,17},{17,1},{2,18},{18,2},{3,19},{19,3},{4,20},{20... | collective-permute-start | bytes 1572872 | tf_op jit(solution)/shard_map/ppermute | solution.py:26
  231.0 41.6 %collective-permute-start.16 = (f32[4,128,256]{2,1,0:T(8,128)}, f32[4,128,256]{2,1,0:T(8,128)S(1)}, u32[]{:S(2)}, u32[]{:S(2)}) collective-permute-start(f32[4,128,256]{2,1,0:T(8,128)} %pad_maximum_fusion.9.refs_0_), channel_id=1, source_target_pairs={{0,4},{4,8},{8,12},{12,0},{1,5},{5,9},{9,13},{13,1},{2,6},{6,10},{... | collective-permute-start | bytes 1572872 | tf_op jit(solution)/shard_map/ppermute | solution.py:26
  246.9 8.7 %copy-start.6 = (f32[4,128,384]{2,1,0:T(8,128)}, f32[4,128,384]{2,1,0:T(8,128)S(1)}, u32[]{:S(2)}) copy-start(f32[4,128,384]{2,1,0:T(8,128)S(1)} %collective-permute-done.24.refs_5_.refs_13_) | copy-start | bytes 2359300
  246.9 33.6 %collective-permute-start.17 = (f32[4,128,256]{2,1,0:T(8,128)}, f32[4,128,256]{2,1,0:T(8,128)S(1)}, u32[]{:S(2)}, u32[]{:S(2)}) collective-permute-start(f32[4,128,256]{2,1,0:T(8,128)} %pad_maximum_fusion.9.refs_0_), channel_id=1, source_target_pairs={{0,8},{4,12},{8,0},{12,4},{1,9},{5,13},{9,1},{13,5},{2,10},{6,14},... | collective-permute-start | bytes 1572872 | tf_op jit(solution)/shard_map/ppermute | solution.py:26
  255.5 25.8 %collective-permute-start.18 = (f32[4,128,256]{2,1,0:T(8,128)}, f32[4,128,256]{2,1,0:T(8,128)}, u32[]{:S(2)}, u32[]{:S(2)}) collective-permute-start(f32[4,128,256]{2,1,0:T(8,128)} %pad_maximum_fusion.9.refs_0_), channel_id=1, source_target_pairs={{0,12},{4,0},{8,4},{12,8},{1,13},{5,1},{9,5},{13,9},{2,14},{6,2},{... | collective-permute-start | bytes 1572872 | tf_op jit(solution)/shard_map/ppermute | solution.py:26
  272.6 7.9 %copy-start.11 = (f32[4,128,256]{2,1,0:T(8,128)}, f32[4,128,256]{2,1,0:T(8,128)S(1)}, u32[]{:S(2)}) copy-start(f32[4,128,256]{2,1,0:T(8,128)S(1)} %collective-permute-done.16.refs_1_) | copy-start | bytes 1572868
  280.5 0.8 copy-start.12
  319.3 1.6 collective-permute-start.27
  322.3 14.0 %all-to-all-start.9 = ((f32[4,4,128,64]{2,3,1,0:T(8,128)}), f32[4,4,128,64]{2,3,1,0:T(8,128)S(1)}, u32[]{:S(2)}, u32[]{:S(2)}) async-start(f32[4,4,128,64]{2,3,1,0:T(8,128)} %bitcast.50), calls=%async_computation.9 | async-start | bytes 1048576 | tf_op jit(solution)/shard_map/all_to_all | solution.py:30
Sparse Core Ops, SparseCore 0:
  10.3 36.1 all-gather.14
  48.2 32.5 all-gather.10
  82.5 32.0 all-gather.8
  136.8 30.7 all-gather.12
  207.4 103.7 all-gather.6

commit v4 on v3

--- a/solution.py
+++ b/solution.py
@@ -328,19 +328,25 @@
     terms = apply_first(inverse_0, rhs[:width], n_y, n_z, n_core)
     own_1[far] = moved(trail_1, far, slab_gram)
     own_1.update({by: moved(trail_1, by, terms) for by in near})
-    first = after(summed(terms.reshape(n_cols, sub, slab), COLS), *own_1.values())
+    first = summed(terms.reshape(n_cols, sub, slab), COLS)
     first_pieces = spread_z(first)
+    first_out = lax.all_gather(solution_piece(first), COLS, axis=0, tiled=False)
     first_all = lax.all_gather(first_pieces, "x", axis=0, tiled=False)
-    first_piece = solution_piece(first)
-    first_out = lax.all_gather(first_piece, COLS, axis=0, tiled=False)
 
     terms = apply_matrix(where_z, below, first_pieces, n_y)
     own_0.update({by: moved(trail_0, by, terms) for by in near})
-    second_rhs = after(rhs[width:] - summed(terms, "y"), first_piece, *own_0.values())
+    second_rhs = rhs[width:] - summed(terms, "y")
+    held = [own_0[by] for by in near] + [own_1[by] for by in near]
+    second_rhs, *held = lax.optimization_barrier((second_rhs, *held))
+    own_0.update(zip(near, held[: len(near)]))
+    own_1.update(zip(near, held[len(near) :]))
     second_pieces = spread_z(second_rhs)
 
     terms = apply_matrix(where_z, inverse_1, second_pieces, n_y)
     own_0[far] = moved(trail_0, far, terms)
+    second, first_out, own_0[far], own_1[far] = lax.optimization_barrier(
+        (summed(terms, "y"), first_out, own_0[far], own_1[far])
+    )
     own_0, own_1 = ([own[by] for by in range(n_z)] for own in (own_0, own_1))
     other_0 = [shift(v, "core", 1) for v in own_0]
     other_1 = [shift(v, "core", 1) for v in own_1]
@@ -354,7 +360,6 @@
     ).astype(BF16)
     base = apply_trail(where_z, own_0, other_0, width, first_all, to_lists, True)
 
-    second = after(summed(terms, "y"), own_0[far])
     piece = solution_piece(second)
     piece = jnp.stack([piece] + [shift(piece, "z", by) for by in range(1, n_z)])
     second_out = [piece] + [shift(piece, "y", by) for by in range(1, n_y)]

time: 345 us -> 362 us (1.049)
  starting transfers between devices: 89.8 us -> 119 us
  blocking collectives: 37.8 us -> 30.1 us
  waiting for transfers between devices: 123 us -> 119 us
  other arithmetic: 14.4 us -> 10.5 us
    all_to_all x9, starting transfers between devices: 39.5 us -> 80 us  [exchange(): return lax.all_to_all(value, axes, 0, 0, tiled=True)]
    ppermute x24, waiting for transfers between devices: 61.7 us -> 50.4 us  [shift(): lax.ppermute(value, axis, [(i, (i + by) % size) for i in range(size)])]
    ppermute x24, starting transfers between devices: 47.9 us -> 36.9 us  [shift(): lax.ppermute(value, axis, [(i, (i + by) % size) for i in range(size)])]
    all_to_all x1, blocking collectives: 37.8 us -> 30.1 us  [exchange(): return lax.all_to_all(value, axes, 0, 0, tiled=True)]
    all_to_all x9, waiting for transfers between devices: 60.8 us -> 67.1 us  [exchange(): return lax.all_to_all(value, axes, 0, 0, tiled=True)]
  transfers between devices with their start and end apart: 42 -> 42, of which waited for: 21 -> 17; matrix products, arithmetic and copies ran while one was open for 11% -> 10% of each run, Pallas kernels for 10% -> 10%
where the time goes in v4:
time: 362 us; the launch traced here: 360 us
  starting transfers between devices  119 us (33%)
  waiting for transfers between devices  119 us (33%)
  Pallas kernels  34.3 us (9%)
  blocking collectives  30.1 us (8%)
  local copies, waits for them, and re-layouts  30 us (8%)
  between operations  14.5 us (4%)
  other arithmetic  10.5 us (3%)
    all_to_all x9, starting transfers between devices, exchange(): return lax.all_to_all(value, axes, 0, 0, tiled=True)  80 us
    all_to_all x9, waiting for transfers between devices, exchange(): return lax.all_to_all(value, axes, 0, 0, tiled=True)  67.1 us
    ppermute x24, waiting for transfers between devices, shift(): lax.ppermute(value, axis, [(i, (i + by) % size) for i in range(size)])  50.4 us
    ppermute x24, starting transfers between devices, shift(): lax.ppermute(value, axis, [(i, (i + by) % size) for i in range(size)])  36.9 us
    all_to_all x1, blocking collectives, exchange(): return lax.all_to_all(value, axes, 0, 0, tiled=True)  30.1 us
    pallas_call x2, Pallas kernels, apply_trail(): pl.pallas_call(functools.partial(trail_kernel, n_z, with_gram), grid=(blo...  17 us
    pallas_call x2, Pallas kernels, apply_matrix(): pl.pallas_call(functools.partial(product_kernel, pieces.shape[0]), grid=(...  7.77 us
  transfers between devices with their start and end apart: 42, of which 17 were waited for; matrix products, arithmetic and copies ran while one was open for 10% of the time, Pallas kernels for 10%

profile of v4, /device:TPU:0, one launch (start us, length us, event | category | flops | bytes accessed | tf_op | source)
XLA Modules:
  0.0 360.4 jit_solution(7061411061993427160)
XLA Ops:
  7.2 2.1 fusion.33
  10.7 1.6 fusion.3
  13.2 4.4 %all-to-all-start = ((f32[8,16,2,512]{3,1,2,0:T(8,128)}), f32[8,16,2,512]{3,1,2,0:T(8,128)S(1)}, u32[]{:S(2)}, u32[]{:S(2)}) async-start(f32[8,16,2,512]{3,1,2,0:T(8,128)} %copy.15), calls=%async_computation | async-start | bytes 1048576 | tf_op jit(solution)/shard_map/all_to_all | solution.py:30
  17.9 2.0 collective-permute-start
  19.9 3.6 collective-permute-start.1
  23.5 1.0 collective-permute-start.2
  24.5 4.5 %collective-permute-done = f32[2,128,256]{2,1,0:T(8,128)S(1)} collective-permute-done((f32[2,128,256]{2,1,0:T(8,128)S(1)}, f32[2,128,256]{2,1,0:T(8,128)S(1)}, u32[]{:S(2)}, u32[]{:S(2)}) %collective-permute-start) | collective-permute-done | bytes 262176 | tf_op jit(solution)/shard_map/ppermute | solution.py:26
  28.9 6.8 %collective-permute-done.1 = f32[2,128,256]{2,1,0:T(8,128)S(1)} collective-permute-done((f32[2,128,256]{2,1,0:T(8,128)S(1)}, f32[2,128,256]{2,1,0:T(8,128)S(1)}, u32[]{:S(2)}, u32[]{:S(2)}) %collective-permute-start.1) | collective-permute-done | bytes 262176 | tf_op jit(solution)/shard_map/ppermute | solution.py:26
  36.7 0.9 pad_maximum_fusion.6
  38.4 0.9 pad_maximum_fusion.7
  39.3 6.2 %all-to-all-start.1 = ((f32[16,16,512]{2,1,0:T(8,128)}), f32[16,16,512]{2,1,0:T(8,128)S(1)}, u32[]{:S(2)}, u32[]{:S(2)}) async-start(f32[16,16,512]{2,1,0:T(8,128)} %pad_maximum_fusion.7), calls=%async_computation.1 | async-start | bytes 1048576 | tf_op jit(solution)/shard_map/all_to_all | solution.py:30
  45.6 11.6 %all-to-all-done.1 = f32[16,16,512]{2,1,0:T(8,128)S(1)} async-done(((f32[16,16,512]{2,1,0:T(8,128)}), f32[16,16,512]{2,1,0:T(8,128)S(1)}, u32[]{:S(2)}, u32[]{:S(2)}) %all-to-all-start.1) | async-done | bytes 524320 | tf_op jit(solution)/shard_map/all_to_all | solution.py:30
  59.2 5.1 %shard_map.68 = f32[4,4,2,128,128]{4,3,2,1,0:T(8,128)} custom-call(f32[4096,256]{1,0:T(8,128)} %bitcast.106, f32[256,128]{1,0:T(8,128)} %slice.104.operand_ref), custom_call_target="tpu_custom_call" | custom-call | flops 805306368 | bytes 4194304 | tf_op jit(solution)/shard_map/pallas_call | solution.py:84
  64.3 3.7 %all-to-all-start.2 = ((f32[16,256,128]{2,1,0:T(8,128)}), f32[16,256,128]{2,1,0:T(8,128)S(1)}, u32[]{:S(2)}, u32[]{:S(2)}) async-start(f32[16,256,128]{2,1,0:T(8,128)} %bitcast.103), calls=%async_computation.2 | async-start | bytes 4194304 | tf_op jit(solution)/shard_map/all_to_all | solution.py:30
  68.1 28.5 %all-to-all-done.2 = f32[16,256,128]{2,1,0:T(8,128)S(1)} async-done(((f32[16,256,128]{2,1,0:T(8,128)}), f32[16,256,128]{2,1,0:T(8,128)S(1)}, u32[]{:S(2)}, u32[]{:S(2)}) %all-to-all-start.2) | async-done | bytes 2097184 | tf_op jit(solution)/shard_map/all_to_all | solution.py:30
  97.5 1.2 collective-permute-done.8
  99.4 2.3 slice.91
  101.7 4.0 %fusion.32 = (f32[4,1,512,256]{3,2,1,0:T(8,128)S(1)}, f32[4,1,512,256]{3,2,1,0:T(8,128)}) fusion(f32[4,2,512,256]{3,2,1,0:T(8,128)} %param.11), kind=kLoop, calls=%fused_computation.115 | loop fusion | bytes 8388608 | tf_op jit(solution)/shard_map/slice | solution.py:323
  106.6 3.5 all-to-all-start.3
  110.1 2.3 constant_dynamic-slice_fusion
  112.4 1.1 dynamic-slice_bitcast_fusion
  113.5 1.3 pad_maximum_fusion.2
  114.8 5.3 %all-to-all-done.3 = f32[4,256,128]{2,1,0:T(8,128)S(1)} async-done(((f32[4,256,128]{2,1,0:T(8,128)}), f32[4,256,128]{2,1,0:T(8,128)S(1)}, u32[]{:S(2)}, u32[]{:S(2)}) %all-to-all-start.3) | async-done | bytes 524320 | tf_op jit(solution)/shard_map/all_to_all | solution.py:30
  120.9 3.9 %shard_map.69 = f32[4,256,128]{2,1,0:T(8,128)} custom-call(s32[1]{0:T(128)} %bitcast.1.at_ref, f32[1024,1024]{1,0:T(8,128)} %all-gather.9.cloned.1.call-done.matrix_ref, f32[4,2,128,128]{3,2,1,0:T(8,128)} %bitcast.104), custom_call_target="tpu_custom_call" | custom-call | flops 805306368 | bytes 4194304 | tf_op jit(solution)/shard_map/pallas_call | solution.py:102
  124.7 1.2 collective-permute-start.4
  125.9 0.9 collective-permute-start.3
  126.8 15.6 %all-to-all-start.4 = ((f32[4,256,128]{2,1,0:T(8,128)}), f32[4,256,128]{2,1,0:T(8,128)S(1)}, u32[]{:S(2)}, u32[]{:S(2)}) async-start(f32[4,256,128]{2,1,0:T(8,128)} %shard_map.69), calls=%async_computation.4 | async-start | bytes 1048576 | tf_op jit(solution)/shard_map/all_to_all | solution.py:30
  142.4 1.4 dynamic-slice_bitcast_fusion.1
  144.4 2.6 collective-permute-start.6
  147.1 3.4 all-to-all-done.4
  150.5 0.9 slice_subtract_fusion
  151.4 13.2 %collective-permute-done.5.refs_1_ = f32[4,128,256]{2,1,0:T(8,128)S(1)} collective-permute-done((f32[4,128,256]{2,1,0:T(8,128)}, f32[4,128,256]{2,1,0:T(8,128)S(1)}, u32[]{:S(2)}, u32[]{:S(2)}) %collective-permute-start.5) | collective-permute-done | bytes 524320 | tf_op jit(solution)/shard_map/ppermute | solution.py:26
  164.6 0.9 broadcast_in_dim.42
  165.5 3.5 all-to-all-start.5
  169.0 0.9 pad_maximum_fusion.4
  170.0 7.1 %all-to-all-done.5 = f32[4,256,128]{2,1,0:T(8,128)S(1)} async-done(((f32[4,256,128]{2,1,0:T(8,128)}), f32[4,256,128]{2,1,0:T(8,128)S(1)}, u32[]{:S(2)}, u32[]{:S(2)}) %all-to-all-start.5) | async-done | bytes 524320 | tf_op jit(solution)/shard_map/all_to_all | solution.py:30
  177.9 3.9 %shard_map.70 = f32[4,256,128]{2,1,0:T(8,128)} custom-call(s32[1]{0:T(128)} %bitcast.1.at_ref, f32[1024,1024]{1,0:T(8,128)} %all-gather.7.cloned.1.call-done.matrix_ref, f32[4,2,128,128]{3,2,1,0:T(8,128)} %bitcast.110), custom_call_target="tpu_custom_call" | custom-call | flops 805306368 | bytes 4194304 | tf_op jit(solution)/shard_map/pallas_call | solution.py:102
  182.4 3.0 collective-permute-start.10
  185.4 16.0 %all-to-all-start.6 = ((f32[4,256,128]{2,1,0:T(8,128)}), f32[4,256,128]{2,1,0:T(8,128)S(1)}, u32[]{:S(2)}, u32[]{:S(2)}) async-start(f32[4,256,128]{2,1,0:T(8,128)} %shard_map.70), calls=%async_computation.6 | async-start | bytes 1048576 | tf_op jit(solution)/shard_map/all_to_all | solution.py:30
  201.4 1.0 pad_maximum_fusion.5.refs_0_.refs_8_
  203.2 6.3 %all-to-all-done.6 = f32[4,256,128]{2,1,0:T(8,128)S(1)} async-done(((f32[4,256,128]{2,1,0:T(8,128)}), f32[4,256,128]{2,1,0:T(8,128)S(1)}, u32[]{:S(2)}, u32[]{:S(2)}) %all-to-all-start.6) | async-done | bytes 524320 | tf_op jit(solution)/shard_map/all_to_all | solution.py:30
  209.5 1.5 broadcast_in_dim.45
  211.1 23.6 %all-to-all-start.7 = ((f32[16,256,128]{2,1,0:T(8,128)}), f32[16,256,128]{2,1,0:T(8,128)}, u32[]{:S(2)}, u32[]{:S(2)}) async-start(f32[16,256,128]{2,1,0:T(8,128)} %broadcast_in_dim.45), calls=%async_computation.7 | async-start | bytes 4194304 | tf_op jit(solution)/shard_map/all_to_all | solution.py:30
  234.8 2.3 gather_fusion
  237.1 2.3 gather_fusion.1
  242.2 1.9 collective-permute-start.13
  244.2 2.7 collective-permute-start.14
  246.9 14.8 %collective-permute-done.13 = f32[128,256]{1,0:T(8,128)S(1)} collective-permute-done((f32[128,256]{1,0:T(8,128)S(1)}, f32[128,256]{1,0:T(8,128)S(1)}, u32[]{:S(2)}, u32[]{:S(2)}) %collective-permute-start.13) | collective-permute-done | bytes 131104 | tf_op jit(solution)/shard_map/ppermute | solution.py:26
  261.7 0.9 and_convert_fusion.refs_16_
  262.6 2.9 collective-permute-done.14
  265.5 1.2 collective-permute-done.15
  266.7 7.5 %collective-permute-start.16 = (f32[4,128,256]{2,1,0:T(8,128)S(1)}, f32[4,128,256]{2,1,0:T(8,128)S(1)}, u32[]{:S(2)}, u32[]{:S(2)}) collective-permute-start(f32[4,128,256]{2,1,0:T(8,128)S(1)} %pad_maximum_fusion.9.refs_0_), channel_id=1, source_target_pairs={{0,4},{4,8},{8,12},{12,0},{1,5},{5,9},{9,13},{13,1},{2,6},{6,10},{... | collective-permute-start | bytes 1572872 | tf_op jit(solution)/shard_map/ppermute | solution.py:26
  274.3 7.6 %collective-permute-start.17 = (f32[4,128,256]{2,1,0:T(8,128)S(1)}, f32[4,128,256]{2,1,0:T(8,128)S(1)}, u32[]{:S(2)}, u32[]{:S(2)}) collective-permute-start(f32[4,128,256]{2,1,0:T(8,128)S(1)} %pad_maximum_fusion.9.refs_0_), channel_id=1, source_target_pairs={{0,8},{4,12},{8,0},{12,4},{1,9},{5,13},{9,1},{13,5},{2,10},{6,14},... | collective-permute-start | bytes 1572872 | tf_op jit(solution)/shard_map/ppermute | solution.py:26
  281.9 0.9 copy-done.7
  282.7 8.9 %shard_map.72.refs_8_ = f32[4,2,4,128,128]{4,3,2,1,0:T(8,128)} custom-call(s32[1]{0:T(128)} %bitcast.1.at_ref, f32[4,4,2,128,128]{4,3,2,1,0:T(8,128)} %all-gather.13.cloned.1.call-done.lists_ref, f32[4,128,384]{2,1,0:T(8,128)} %copy-done.1, f32[4,128,384]{2,1,0:T(8,128)} %collective-permute-done.3.refs_1_.refs_9_, f32[4,128,384]{2,1,0:T(8,128)} %copy-done.4, ...), custom_call_target="tpu_custom_call" | custom-call | flops 3221225472 | bytes 10485760 | tf_op jit(solution)/shard_map/pallas_call | solution.py:170
  291.7 8.1 %shard_map.73 = f32[4,2,4,128,128]{4,3,2,1,0:T(8,128)} custom-call(s32[1]{0:T(128)} %bitcast.1.at_ref, f32[4,4,2,128,128]{4,3,2,1,0:T(8,128)} %bitcast.43.lists_ref, f32[4,128,256]{2,1,0:T(8,128)} %get-tuple-element.53.refs_0_, f32[4,128,256]{2,1,0:T(8,128)} %copy-done.18, f32[4,128,256]{2,1,0:T(8,128)} %collective-permute-done.10.refs_2_, ...), custom_call_target="tpu_custom_call" | custom-call | flops 3221225472 | bytes 10485760 | tf_op jit(solution)/shard_map/pallas_call | solution.py:170
  299.8 5.6 %collective-permute-done.17.refs_2_ = f32[4,128,256]{2,1,0:T(8,128)S(1)} collective-permute-done((f32[4,128,256]{2,1,0:T(8,128)S(1)}, f32[4,128,256]{2,1,0:T(8,128)S(1)}, u32[]{:S(2)}, u32[]{:S(2)}) %collective-permute-start.17) | collective-permute-done | bytes 524320 | tf_op jit(solution)/shard_map/ppermute | solution.py:26
  306.2 30.1 %all_to_all.50 = f32[4,2,4,128,128]{4,3,2,1,0:T(8,128)S(1)} all-to-all(f32[4,2,4,128,128]{4,3,2,1,0:T(8,128)} %shard_map.73), channel_id=1, replica_groups=mesh['x'=4,'core'=2,'y'=4,'z'=4] {'y'}, dimensions={0} | all-to-all | bytes 4194304 | tf_op jit(solution)/shard_map/all_to_all | solution.py:30
  336.6 1.5 collective-permute-done.27
  338.4 1.1 copy.18
  339.5 3.5 all-to-all-start.9
  343.7 4.5 %shard_map.71 = f32[2,512,1024]{2,1,0:T(8,128)} custom-call(s32[2]{0:T(128)} %pad_add_fusion.at_ref, f32[4,4,128,256]{3,2,1,0:T(8,128)} %bitcast.109, f32[4,128,256]{2,1,0:T(8,128)} %copy-done.8, f32[4,128,256]{2,1,0:T(8,128)} %copy-done.14, f32[4,128,256]{2,1,0:T(8,128)} %copy-done.15, f32[4,128,256]{2,1,0:T(8,128)} %collective-permute-done.18.refs_3_), custom_call_target="tpu_custom_call" | custom-call | bytes 8388608 | tf_op jit(solution)/shard_map/pallas_call | solution.py:200
  348.2 4.9 %all-to-all-done.9 = f32[4,4,128,64]{2,3,1,0:T(8,128)S(1)} async-done(((f32[4,4,128,64]{2,3,1,0:T(8,128)}), f32[4,4,128,64]{2,3,1,0:T(8,128)S(1)}, u32[]{:S(2)}, u32[]{:S(2)}) %all-to-all-start.9) | async-done | bytes 524320 | tf_op jit(solution)/shard_map/all_to_all | solution.py:30
  353.0 0.9 copy_bitcast_fusion
  (144 shorter events, 17.4 us)
Async XLA Ops:
  7.2 2.2 copy-start.17
  7.2 52.1 %all-gather.15.cloned.1.call-start = ((), (), s32[]{:S(2)}) async-start(), calls=%async_computation.14 | async-start | bytes 4718592 | tf_op jit(solution)/shard_map/all_gather | solution.py:268
  9.3 8.3 %copy-start.16 = (f32[512,256]{1,0:T(8,128)S(1)}, f32[512,256]{1,0:T(8,128)}, u32[]{:S(2)}) copy-start(f32[512,256]{1,0:T(8,128)} %param.10) | copy-start | bytes 1572868
  13.2 22.5 %all-to-all-start = ((f32[8,16,2,512]{3,1,2,0:T(8,128)}), f32[8,16,2,512]{3,1,2,0:T(8,128)S(1)}, u32[]{:S(2)}, u32[]{:S(2)}) async-start(f32[8,16,2,512]{3,1,2,0:T(8,128)} %copy.15), calls=%async_computation | async-start | bytes 1048576 | tf_op jit(solution)/shard_map/all_to_all | solution.py:30
  17.6 97.2 %all-gather.9.cloned.1.call-start = ((), (), s32[]{:S(2)}) async-start(), calls=%async_computation.11 | async-start | bytes 4718592 | tf_op jit(solution)/shard_map/all_gather | solution.py:266
  17.9 11.0 %collective-permute-start = (f32[2,128,256]{2,1,0:T(8,128)S(1)}, f32[2,128,256]{2,1,0:T(8,128)S(1)}, u32[]{:S(2)}, u32[]{:S(2)}) collective-permute-start(f32[2,128,256]{2,1,0:T(8,128)S(1)} %get-tuple-element.65), channel_id=1, source_target_pairs={{0,1},{1,2},{2,3},{3,0},{4,5},{5,6},{6,7},{7,4},{8,9},{9,10},{10,1... | collective-permute-start | bytes 786440 | tf_op jit(solution)/shard_map/ppermute | solution.py:26
  19.9 15.8 %collective-permute-start.1 = (f32[2,128,256]{2,1,0:T(8,128)S(1)}, f32[2,128,256]{2,1,0:T(8,128)S(1)}, u32[]{:S(2)}, u32[]{:S(2)}) collective-permute-start(f32[2,128,256]{2,1,0:T(8,128)S(1)} %get-tuple-element.64), channel_id=1, source_target_pairs={{0,2},{1,3},{2,0},{3,1},{4,6},{5,7},{6,4},{7,5},{8,10},{9,11},{10,... | collective-permute-start | bytes 786440 | tf_op jit(solution)/shard_map/ppermute | solution.py:26
  23.5 12.3 %collective-permute-start.2 = (f32[2,128,256]{2,1,0:T(8,128)S(1)}, f32[2,128,256]{2,1,0:T(8,128)S(1)}, u32[]{:S(2)}, u32[]{:S(2)}) collective-permute-start(f32[2,128,256]{2,1,0:T(8,128)S(1)} %get-tuple-element.63), channel_id=1, source_target_pairs={{0,3},{1,0},{2,1},{3,2},{4,7},{5,4},{6,5},{7,6},{8,11},{9,8},{10,9... | collective-permute-start | bytes 786440 | tf_op jit(solution)/shard_map/ppermute | solution.py:26
  36.7 133.3 %all-gather.7.cloned.1.call-start = ((), (), s32[]{:S(2)}) async-start(), calls=%async_computation.10 | async-start | bytes 4718592 | tf_op jit(solution)/shard_map/all_gather | solution.py:266
  39.3 18.0 %all-to-all-start.1 = ((f32[16,16,512]{2,1,0:T(8,128)}), f32[16,16,512]{2,1,0:T(8,128)S(1)}, u32[]{:S(2)}, u32[]{:S(2)}) async-start(f32[16,16,512]{2,1,0:T(8,128)} %pad_maximum_fusion.7), calls=%async_computation.1 | async-start | bytes 1048576 | tf_op jit(solution)/shard_map/all_to_all | solution.py:30
  57.9 0.7 copy-start.13
  64.3 32.3 %all-to-all-start.2 = ((f32[16,256,128]{2,1,0:T(8,128)}), f32[16,256,128]{2,1,0:T(8,128)S(1)}, u32[]{:S(2)}, u32[]{:S(2)}) async-start(f32[16,256,128]{2,1,0:T(8,128)} %bitcast.103), calls=%async_computation.2 | async-start | bytes 4194304 | tf_op jit(solution)/shard_map/all_to_all | solution.py:30
  68.0 141.5 %all-gather.11.cloned.1.call-start = ((), (), s32[]{:S(2)}) async-start(), calls=%async_computation.12 | async-start | bytes 2228224 | tf_op jit(solution)/shard_map/all_gather | solution.py:333
  96.7 0.8 collective-permute-start.7
  97.4 1.3 collective-permute-start.8
  106.6 13.5 %all-to-all-start.3 = ((f32[4,256,128]{2,1,0:T(8,128)}), f32[4,256,128]{2,1,0:T(8,128)S(1)}, u32[]{:S(2)}, u32[]{:S(2)}) async-start(f32[4,256,128]{2,1,0:T(8,128)} %broadcast_in_dim.41), calls=%async_computation.3 | async-start | bytes 1048576 | tf_op jit(solution)/shard_map/all_to_all | solution.py:30
  110.1 2.3 copy-start
  120.1 0.8 copy-start.2
  124.7 39.9 %collective-permute-start.4 = (f32[4,128,384]{2,1,0:T(8,128)}, f32[4,128,384]{2,1,0:T(8,128)S(1)}, u32[]{:S(2)}, u32[]{:S(2)}) collective-permute-start(f32[4,128,384]{2,1,0:T(8,128)} %get-tuple-element.30), channel_id=1, source_target_pairs={{0,3},{1,0},{2,1},{3,2},{4,7},{5,4},{6,5},{7,6},{8,11},{9,8},{10,9... | collective-permute-start | bytes 2359304 | tf_op jit(solution)/shard_map/ppermute | solution.py:26
  125.9 38.7 %collective-permute-start.3 = (f32[4,128,384]{2,1,0:T(8,128)}, f32[4,128,384]{2,1,0:T(8,128)}, u32[]{:S(2)}, u32[]{:S(2)}) collective-permute-start(f32[4,128,384]{2,1,0:T(8,128)} %get-tuple-element.29), channel_id=1, source_target_pairs={{0,1},{1,2},{2,3},{3,0},{4,5},{5,6},{6,7},{7,4},{8,9},{9,10},{10,1... | collective-permute-start | bytes 2359304 | tf_op jit(solution)/shard_map/ppermute | solution.py:26
  126.8 23.7 %all-to-all-start.4 = ((f32[4,256,128]{2,1,0:T(8,128)}), f32[4,256,128]{2,1,0:T(8,128)S(1)}, u32[]{:S(2)}, u32[]{:S(2)}) async-start(f32[4,256,128]{2,1,0:T(8,128)} %shard_map.69), calls=%async_computation.4 | async-start | bytes 1048576 | tf_op jit(solution)/shard_map/all_to_all | solution.py:30
  142.4 140.4 %all-gather.13.cloned.1.call-start = ((), (), s32[]{:S(2)}) async-start(), calls=%async_computation.13 | async-start | bytes 2621440 | tf_op jit(solution)/shard_map/all_gather | solution.py:334
  143.8 25.2 %copy-start.10 = (f32[4,128,256]{2,1,0:T(8,128)S(1)}, f32[4,128,256]{2,1,0:T(8,128)}, u32[]{:S(2)}) copy-start(f32[4,128,256]{2,1,0:T(8,128)} %get-tuple-element.50) | copy-start | bytes 1572868
  143.8 25.2 %copy-start.12 = (f32[4,128,128]{2,1,0:T(8,128)S(1)}, f32[4,128,128]{2,1,0:T(8,128)}, u32[]{:S(2)}) copy-start(f32[4,128,128]{2,1,0:T(8,128)} %get-tuple-element.58) | copy-start | bytes 786436
  143.8 20.8 %collective-permute-start.5 = (f32[4,128,256]{2,1,0:T(8,128)}, f32[4,128,256]{2,1,0:T(8,128)S(1)}, u32[]{:S(2)}, u32[]{:S(2)}) collective-permute-start(f32[4,128,256]{2,1,0:T(8,128)} %get-tuple-element.31), channel_id=1, source_target_pairs={{0,1},{1,2},{2,3},{3,0},{4,5},{5,6},{6,7},{7,4},{8,9},{9,10},{10,1... | collective-permute-start | bytes 1572872 | tf_op jit(solution)/shard_map/ppermute | solution.py:26
  144.4 20.2 %collective-permute-start.6 = (f32[4,128,256]{2,1,0:T(8,128)}, f32[4,128,256]{2,1,0:T(8,128)}, u32[]{:S(2)}, u32[]{:S(2)}) collective-permute-start(f32[4,128,256]{2,1,0:T(8,128)} %get-tuple-element.32), channel_id=1, source_target_pairs={{0,3},{1,0},{2,1},{3,2},{4,7},{5,4},{6,5},{7,6},{8,11},{9,8},{10,9... | collective-permute-start | bytes 1572872 | tf_op jit(solution)/shard_map/ppermute | solution.py:26
  164.6 17.2 %copy-start.18 = (f32[4,128,256]{2,1,0:T(8,128)}, f32[4,128,256]{2,1,0:T(8,128)S(1)}, u32[]{:S(2)}) copy-start(f32[4,128,256]{2,1,0:T(8,128)S(1)} %collective-permute-done.5.refs_1_) | copy-start | bytes 1572868
  164.6 76.4 %copy-start.3 = (f32[4,128,384]{2,1,0:T(8,128)}, f32[4,128,384]{2,1,0:T(8,128)S(1)}, u32[]{:S(2)}) copy-start(f32[4,128,384]{2,1,0:T(8,128)S(1)} %collective-permute-done.4.refs_3_.refs_11_) | copy-start | bytes 2359300
  165.5 11.5 %all-to-all-start.5 = ((f32[4,256,128]{2,1,0:T(8,128)}), f32[4,256,128]{2,1,0:T(8,128)S(1)}, u32[]{:S(2)}, u32[]{:S(2)}) async-start(f32[4,256,128]{2,1,0:T(8,128)} %broadcast_in_dim.42), calls=%async_computation.5 | async-start | bytes 1048576 | tf_op jit(solution)/shard_map/all_to_all | solution.py:30
  177.1 0.8 copy-start.11
  177.9 23.5 %copy-start.9 = (f32[4,128,256]{2,1,0:T(8,128)S(1)}, f32[4,128,256]{2,1,0:T(8,128)}, u32[]{:S(2)}) copy-start(f32[4,128,256]{2,1,0:T(8,128)} %get-tuple-element.49) | copy-start | bytes 1572868
  181.8 27.7 %collective-permute-start.9 = (f32[4,128,384]{2,1,0:T(8,128)}, f32[4,128,384]{2,1,0:T(8,128)S(1)}, u32[]{:S(2)}, u32[]{:S(2)}) collective-permute-start(f32[4,128,384]{2,1,0:T(8,128)} %pad_maximum_fusion.4), channel_id=1, source_target_pairs={{0,2},{1,3},{2,0},{3,1},{4,6},{5,7},{6,4},{7,5},{8,10},{9,11},{10,... | collective-permute-start | bytes 2359304 | tf_op jit(solution)/shard_map/ppermute | solution.py:26
  182.4 27.1 %collective-permute-start.10 = (f32[4,128,256]{2,1,0:T(8,128)}, f32[4,128,256]{2,1,0:T(8,128)}, u32[]{:S(2)}, u32[]{:S(2)}) collective-permute-start(f32[4,128,256]{2,1,0:T(8,128)} %get-tuple-element.35), channel_id=1, source_target_pairs={{0,2},{1,3},{2,0},{3,1},{4,6},{5,7},{6,4},{7,5},{8,10},{9,11},{10,... | collective-permute-start | bytes 1572872 | tf_op jit(solution)/shard_map/ppermute | solution.py:26
  185.4 24.1 %all-to-all-start.6 = ((f32[4,256,128]{2,1,0:T(8,128)}), f32[4,256,128]{2,1,0:T(8,128)S(1)}, u32[]{:S(2)}, u32[]{:S(2)}) async-start(f32[4,256,128]{2,1,0:T(8,128)} %shard_map.70), calls=%async_computation.6 | async-start | bytes 1048576 | tf_op jit(solution)/shard_map/all_to_all | solution.py:30
  202.4 8.7 %copy-start.1 = (f32[4,128,384]{2,1,0:T(8,128)}, f32[4,128,384]{2,1,0:T(8,128)S(1)}, u32[]{:S(2)}) copy-start(f32[4,128,384]{2,1,0:T(8,128)S(1)} %pad_maximum_fusion.5.refs_0_.refs_8_) | copy-start | bytes 2359300
  202.4 39.8 %collective-permute-start.23 = (f32[4,128,384]{2,1,0:T(8,128)S(1)}, f32[4,128,384]{2,1,0:T(8,128)}, u32[]{:S(2)}, u32[]{:S(2)}) collective-permute-start(f32[4,128,384]{2,1,0:T(8,128)S(1)} %pad_maximum_fusion.5.refs_0_.refs_8_), channel_id=1, source_target_pairs={{0,16},{16,0},{1,17},{17,1},{2,18},{18,2},{3,19},{19,3},{4,20},{20... | collective-permute-start | bytes 2359304 | tf_op jit(solution)/shard_map/ppermute | solution.py:26
  202.7 38.2 %collective-permute-start.19 = (f32[4,128,256]{2,1,0:T(8,128)}, f32[4,128,256]{2,1,0:T(8,128)}, u32[]{:S(2)}, u32[]{:S(2)}) collective-permute-start(f32[4,128,256]{2,1,0:T(8,128)} %get-tuple-element.53.refs_0_), channel_id=1, source_target_pairs={{0,16},{16,0},{1,17},{17,1},{2,18},{18,2},{3,19},{19,3},{4,20},{20... | collective-permute-start | bytes 1572872 | tf_op jit(solution)/shard_map/ppermute | solution.py:26
  209.5 32.3 %copy-start.4 = (f32[4,128,384]{2,1,0:T(8,128)}, f32[4,128,384]{2,1,0:T(8,128)S(1)}, u32[]{:S(2)}) copy-start(f32[4,128,384]{2,1,0:T(8,128)S(1)} %collective-permute-done.9.refs_2_.refs_10_) | copy-start | bytes 2359300
  211.1 80.6 %all-to-all-start.7 = ((f32[16,256,128]{2,1,0:T(8,128)}), f32[16,256,128]{2,1,0:T(8,128)}, u32[]{:S(2)}, u32[]{:S(2)}) async-start(f32[16,256,128]{2,1,0:T(8,128)} %broadcast_in_dim.45), calls=%async_computation.7 | async-start | bytes 4194304 | tf_op jit(solution)/shard_map/all_to_all | solution.py:30
  234.8 4.7 %copy-start.19 = (f32[4,128,256]{2,1,0:T(8,128)S(1)}, f32[4,128,256]{2,1,0:T(8,128)}, u32[]{:S(2)}) copy-start(f32[4,128,256]{2,1,0:T(8,128)} %copy-done.18) | copy-start | bytes 1572868
  239.5 4.7 %collective-permute-start.20 = (f32[4,128,256]{2,1,0:T(8,128)S(1)}, f32[4,128,256]{2,1,0:T(8,128)S(1)}, u32[]{:S(2)}, u32[]{:S(2)}) collective-permute-start(f32[4,128,256]{2,1,0:T(8,128)S(1)} %copy-done.19), channel_id=1, source_target_pairs={{0,16},{16,0},{1,17},{17,1},{2,18},{18,2},{3,19},{19,3},{4,20},{20... | collective-permute-start | bytes 1572872 | tf_op jit(solution)/shard_map/ppermute | solution.py:26
  239.6 1.4 collective-permute-start.11
  240.3 1.5 collective-permute-start.12
  240.9 25.8 %collective-permute-start.24 = (f32[4,128,384]{2,1,0:T(8,128)}, f32[4,128,384]{2,1,0:T(8,128)S(1)}, u32[]{:S(2)}, u32[]{:S(2)}) collective-permute-start(f32[4,128,384]{2,1,0:T(8,128)} %collective-permute-done.3.refs_1_.refs_9_), channel_id=1, source_target_pairs={{0,16},{16,0},{1,17},{17,1},{2,18},{18,2},{3,19},{19,3},{4,20},{20... | collective-permute-start | bytes 2359304 | tf_op jit(solution)/shard_map/ppermute | solution.py:26
  241.0 33.3 %collective-permute-start.26 = (f32[4,128,384]{2,1,0:T(8,128)S(1)}, f32[4,128,384]{2,1,0:T(8,128)S(1)}, u32[]{:S(2)}, u32[]{:S(2)}) collective-permute-start(f32[4,128,384]{2,1,0:T(8,128)S(1)} %collective-permute-done.4.refs_3_.refs_11_), channel_id=1, source_target_pairs={{0,16},{16,0},{1,17},{17,1},{2,18},{18,2},{3,19},{19,3},{4,20},{20... | collective-permute-start | bytes 2359304 | tf_op jit(solution)/shard_map/ppermute | solution.py:26
  241.8 40.1 %collective-permute-start.25 = (f32[4,128,384]{2,1,0:T(8,128)S(1)}, f32[4,128,384]{2,1,0:T(8,128)S(1)}, u32[]{:S(2)}, u32[]{:S(2)}) collective-permute-start(f32[4,128,384]{2,1,0:T(8,128)S(1)} %collective-permute-done.9.refs_2_.refs_10_), channel_id=1, source_target_pairs={{0,16},{16,0},{1,17},{17,1},{2,18},{18,2},{3,19},{19,3},{4,20},{20... | collective-permute-start | bytes 2359304 | tf_op jit(solution)/shard_map/ppermute | solution.py:26
  242.2 19.5 %collective-permute-start.13 = (f32[128,256]{1,0:T(8,128)S(1)}, f32[128,256]{1,0:T(8,128)S(1)}, u32[]{:S(2)}, u32[]{:S(2)}) collective-permute-start(f32[128,256]{1,0:T(8,128)S(1)} %maximum_select_fusion.3), channel_id=1, source_target_pairs={{0,1},{1,2},{2,3},{3,0},{4,5},{5,6},{6,7},{7,4},{8,9},{9,10},{10,1... | collective-permute-start | bytes 393224 | tf_op jit(solution)/shard_map/ppermute | solution.py:26
  244.2 17.5 %copy-start.20 = (f32[4,128,256]{2,1,0:T(8,128)}, f32[4,128,256]{2,1,0:T(8,128)S(1)}, u32[]{:S(2)}) copy-start(f32[4,128,256]{2,1,0:T(8,128)S(1)} %collective-permute-done.20.refs_5_) | copy-start | bytes 1572868
  244.2 21.3 %collective-permute-start.14 = (f32[128,256]{1,0:T(8,128)S(1)}, f32[128,256]{1,0:T(8,128)S(1)}, u32[]{:S(2)}, u32[]{:S(2)}) collective-permute-start(f32[128,256]{1,0:T(8,128)S(1)} %maximum_select_fusion.3), channel_id=1, source_target_pairs={{0,2},{1,3},{2,0},{3,1},{4,6},{5,7},{6,4},{7,5},{8,10},{9,11},{10,... | collective-permute-start | bytes 393224 | tf_op jit(solution)/shard_map/ppermute | solution.py:26
  261.7 5.0 %collective-permute-start.15 = (f32[128,256]{1,0:T(8,128)S(1)}, f32[128,256]{1,0:T(8,128)S(1)}, u32[]{:S(2)}, u32[]{:S(2)}) collective-permute-start(f32[128,256]{1,0:T(8,128)S(1)} %maximum_select_fusion.3), channel_id=1, source_target_pairs={{0,3},{1,0},{2,1},{3,2},{4,7},{5,4},{6,5},{7,6},{8,11},{9,8},{10,9... | collective-permute-start | bytes 393224 | tf_op jit(solution)/shard_map/ppermute | solution.py:26
  265.5 26.2 %collective-permute-start.22 = (f32[4,128,256]{2,1,0:T(8,128)}, f32[4,128,256]{2,1,0:T(8,128)}, u32[]{:S(2)}, u32[]{:S(2)}) collective-permute-start(f32[4,128,256]{2,1,0:T(8,128)} %collective-permute-done.6.refs_3_), channel_id=1, source_target_pairs={{0,16},{16,0},{1,17},{17,1},{2,18},{18,2},{3,19},{19,3},{4,20},{20... | collective-permute-start | bytes 1572872 | tf_op jit(solution)/shard_map/ppermute | solution.py:26
  266.7 25.0 %collective-permute-start.21 = (f32[4,128,256]{2,1,0:T(8,128)}, f32[4,128,256]{2,1,0:T(8,128)}, u32[]{:S(2)}, u32[]{:S(2)}) collective-permute-start(f32[4,128,256]{2,1,0:T(8,128)} %collective-permute-done.10.refs_2_), channel_id=1, source_target_pairs={{0,16},{16,0},{1,17},{17,1},{2,18},{18,2},{3,19},{19,3},{4,20},{20... | collective-permute-start | bytes 1572872 | tf_op jit(solution)/shard_map/ppermute | solution.py:26
  266.7 24.9 %copy-start.8 = (f32[4,128,256]{2,1,0:T(8,128)}, f32[4,128,256]{2,1,0:T(8,128)S(1)}, u32[]{:S(2)}) copy-start(f32[4,128,256]{2,1,0:T(8,128)S(1)} %pad_maximum_fusion.9.refs_0_) | copy-start | bytes 1572868
  266.7 15.1 %copy-start.5 = (f32[4,128,384]{2,1,0:T(8,128)}, f32[4,128,384]{2,1,0:T(8,128)S(1)}, u32[]{:S(2)}) copy-start(f32[4,128,384]{2,1,0:T(8,128)S(1)} %collective-permute-done.24.refs_5_.refs_13_) | copy-start | bytes 2359300
  266.7 33.0 %collective-permute-start.16 = (f32[4,128,256]{2,1,0:T(8,128)S(1)}, f32[4,128,256]{2,1,0:T(8,128)S(1)}, u32[]{:S(2)}, u32[]{:S(2)}) collective-permute-start(f32[4,128,256]{2,1,0:T(8,128)S(1)} %pad_maximum_fusion.9.refs_0_), channel_id=1, source_target_pairs={{0,4},{4,8},{8,12},{12,0},{1,5},{5,9},{9,13},{13,1},{2,6},{6,10},{... | collective-permute-start | bytes 1572872 | tf_op jit(solution)/shard_map/ppermute | solution.py:26
  274.3 7.6 %copy-start.6 = (f32[4,128,384]{2,1,0:T(8,128)}, f32[4,128,384]{2,1,0:T(8,128)S(1)}, u32[]{:S(2)}) copy-start(f32[4,128,384]{2,1,0:T(8,128)S(1)} %collective-permute-done.26.refs_7_.refs_15_) | copy-start | bytes 2359300
  274.3 31.1 %collective-permute-start.17 = (f32[4,128,256]{2,1,0:T(8,128)S(1)}, f32[4,128,256]{2,1,0:T(8,128)S(1)}, u32[]{:S(2)}, u32[]{:S(2)}) collective-permute-start(f32[4,128,256]{2,1,0:T(8,128)S(1)} %pad_maximum_fusion.9.refs_0_), channel_id=1, source_target_pairs={{0,8},{4,12},{8,0},{12,4},{1,9},{5,13},{9,1},{13,5},{2,10},{6,14},... | collective-permute-start | bytes 1572872 | tf_op jit(solution)/shard_map/ppermute | solution.py:26
  281.9 0.9 copy-start.7
  282.7 22.6 %collective-permute-start.18 = (f32[4,128,256]{2,1,0:T(8,128)S(1)}, f32[4,128,256]{2,1,0:T(8,128)}, u32[]{:S(2)}, u32[]{:S(2)}) collective-permute-start(f32[4,128,256]{2,1,0:T(8,128)S(1)} %pad_maximum_fusion.9.refs_0_), channel_id=1, source_target_pairs={{0,12},{4,0},{8,4},{12,8},{1,13},{5,1},{9,5},{13,9},{2,14},{6,2},{... | collective-permute-start | bytes 1572872 | tf_op jit(solution)/shard_map/ppermute | solution.py:26
  299.8 36.5 %copy-start.14 = (f32[4,128,256]{2,1,0:T(8,128)}, f32[4,128,256]{2,1,0:T(8,128)S(1)}, u32[]{:S(2)}) copy-start(f32[4,128,256]{2,1,0:T(8,128)S(1)} %collective-permute-done.16.refs_1_) | copy-start | bytes 1572868
  305.4 0.8 copy-start.15
  336.5 1.6 collective-permute-start.27
  339.5 13.5 %all-to-all-start.9 = ((f32[4,4,128,64]{2,3,1,0:T(8,128)}), f32[4,4,128,64]{2,3,1,0:T(8,128)S(1)}, u32[]{:S(2)}, u32[]{:S(2)}) async-start(f32[4,4,128,64]{2,3,1,0:T(8,128)} %bitcast.50), calls=%async_computation.9 | async-start | bytes 1048576 | tf_op jit(solution)/shard_map/all_to_all | solution.py:30
Sparse Core Ops, SparseCore 0:
  10.3 36.1 all-gather.14
  48.2 32.5 all-gather.8
  82.5 37.6 all-gather.6
  122.2 50.2 all-gather.10
  174.5 30.5 all-gather.12

commit v5 on v3

--- a/solution.py
+++ b/solution.py
@@ -184,26 +184,23 @@
     )(*args, start)
 
 
-def rows_kernel(at_ref, first_ref, *refs):
-    seconds, out_ref = refs[:-1], refs[-1]
-    n_y, n_z, quarter, wide = first_ref.shape
+def rows_kernel(pieces_ref, out_ref):
+    n_y, _, n_panels, _, wide = pieces_ref.shape
     for y in range(n_y):
-        at_y = pl.multiple_of(lax.rem(at_ref[0] + n_y - y, n_y) * wide, wide)
-        for z in range(n_z):
-            out_ref[0, z * quarter : (z + 1) * quarter, y * wide : (y + 1) * wide] = first_ref[y, z]
-            at_z = pl.multiple_of(lax.rem(at_ref[1] + n_z - z, n_z) * quarter, quarter)
-            out_ref[1, pl.ds(at_z, quarter), pl.ds(at_y, wide)] = seconds[y][z]
-
-
-def as_rows(where, first, seconds):
-    n_y, n_z, quarter, wide = first.shape
+        for panel in range(n_panels):
+            out_ref[panel, :, y * wide : (y + 1) * wide] = pieces_ref[y, 0, panel]
+
+
+def as_rows(pieces):
+    n_y, n_z, n_panels, quarter, wide = pieces.shape
     return pl.pallas_call(
         rows_kernel,
-        in_specs=[SMEM] + [pl.BlockSpec(memory_space=pltpu.VMEM)] * (1 + n_y),
-        out_specs=pl.BlockSpec(memory_space=pltpu.VMEM),
-        out_shape=jax.ShapeDtypeStruct((2, n_z * quarter, n_y * wide), F32),
+        grid=(n_z,),
+        in_specs=[pl.BlockSpec((n_y, 1, n_panels, quarter, wide), lambda i: (0, i, 0, 0, 0))],
+        out_specs=pl.BlockSpec((n_panels, quarter, n_y * wide), lambda i: (0, i, 0)),
+        out_shape=jax.ShapeDtypeStruct((n_panels, n_z * quarter, n_y * wide), F32),
         cost_estimate=pl.CostEstimate(flops=0, bytes_accessed=8 * 2**20, transcendentals=0),
-    )(where, first, *seconds)
+    )(pieces)
 
 
 def after(value, *others):
@@ -216,7 +213,6 @@
     col = lax.axis_index(COLS)
     row = lax.axis_index(ROWS)
     core = lax.axis_index("core")
-    y_at = lax.axis_index("y")
     z_at = lax.axis_index("z")
     list_len = cells.shape[0]
     run_len = list_len // n_cols
@@ -332,7 +328,6 @@
     first_pieces = spread_z(first)
     first_all = lax.all_gather(first_pieces, "x", axis=0, tiled=False)
     first_piece = solution_piece(first)
-    first_out = lax.all_gather(first_piece, COLS, axis=0, tiled=False)
 
     terms = apply_matrix(where_z, below, first_pieces, n_y)
     own_0.update({by: moved(trail_0, by, terms) for by in near})
@@ -355,12 +350,9 @@
     base = apply_trail(where_z, own_0, other_0, width, first_all, to_lists, True)
 
     second = after(summed(terms, "y"), own_0[far])
-    piece = solution_piece(second)
-    piece = jnp.stack([piece] + [shift(piece, "z", by) for by in range(1, n_z)])
-    second_out = [piece] + [shift(piece, "y", by) for by in range(1, n_y)]
+    solved = lax.all_gather(jnp.stack([first_piece, solution_piece(second)]), COLS, axis=0, tiled=False)
     second_all = spread(second, ("x", "z")).reshape(n_x, n_z, n_core, quarter, slab)
     terms = apply_trail(where_z, own_1, other_1, width, second_all, base, False)
-    terms = after(terms, *second_out)
     total = summed(terms, "y").reshape(n_core, trail_blocks, quarter, slab)
     kept, given = total[0], total[1]
     got = shift(given, "core", 1)
@@ -368,8 +360,7 @@
     pair = pair.reshape(n_core, trail_blocks, quarter, n_z // n_core, run_len).transpose(0, 3, 1, 2, 4)
     out = exchange(pair.reshape(n_z, trail_blocks, quarter, run_len), "z")
     trail_out = out.transpose(1, 0, 2, 3).reshape(trail_blocks, block_rows, run_len)
-    first_out = first_out.reshape(n_y, n_z, quarter, n_core * slab)
-    return as_rows(jnp.stack([y_at, z_at]).astype(jnp.int32), first_out, second_out), trail_out
+    return as_rows(solved.reshape(n_y, n_z, 2, quarter, n_core * slab)), trail_out
 
 
 def solution(mesh):

time: 345 us -> 324 us (0.939)
  blocking collectives: 37.8 us -> 68.9 us
  starting transfers between devices: 89.8 us -> 63 us
  waiting for transfers between devices: 123 us -> 101 us
    all_to_all x1 -> x3, blocking collectives: 37.8 us -> 68.9 us  [exchange(): return lax.all_to_all(value, axes, 0, 0, tiled=True)]
    ppermute x24 -> x18, starting transfers between devices: 47.9 us -> 17.8 us  [shift(): lax.ppermute(value, axis, [(i, (i + by) % size) for i in range(size)])]
    ppermute x24 -> x18, waiting for transfers between devices: 61.7 us -> 43.9 us  [shift(): lax.ppermute(value, axis, [(i, (i + by) % size) for i in range(size)])]
    all_to_all x9 -> x7, waiting for transfers between devices: 60.8 us -> 55.8 us  [exchange(): return lax.all_to_all(value, axes, 0, 0, tiled=True)]
    all_to_all x9 -> x7, starting transfers between devices: 39.5 us -> 42.6 us  [exchange(): return lax.all_to_all(value, axes, 0, 0, tiled=True)]
  transfers between devices with their start and end apart: 42 -> 34, of which waited for: 21 -> 18; matrix products, arithmetic and copies ran while one was open for 11% -> 10% of each run, Pallas kernels for 10% -> 9%
where the time goes in v5:
time: 324 us; the launch traced here: 321 us
  waiting for transfers between devices  101 us (31%)
  blocking collectives  68.9 us (21%)
  starting transfers between devices  63 us (19%)
  Pallas kernels  34.5 us (11%)
  local copies, waits for them, and re-layouts  24.3 us (8%)
  between operations  14.4 us (4%)
  other arithmetic  12.7 us (4%)
    all_to_all x3, blocking collectives, exchange(): return lax.all_to_all(value, axes, 0, 0, tiled=True)  68.9 us
    all_to_all x7, waiting for transfers between devices, exchange(): return lax.all_to_all(value, axes, 0, 0, tiled=True)  55.8 us
    ppermute x18, waiting for transfers between devices, shift(): lax.ppermute(value, axis, [(i, (i + by) % size) for i in range(size)])  43.9 us
    all_to_all x7, starting transfers between devices, exchange(): return lax.all_to_all(value, axes, 0, 0, tiled=True)  42.6 us
    ppermute x18, starting transfers between devices, shift(): lax.ppermute(value, axis, [(i, (i + by) % size) for i in range(size)])  17.8 us
    pallas_call x2, Pallas kernels, apply_trail(): pl.pallas_call(functools.partial(trail_kernel, n_z, with_gram), grid=(blo...  17 us
    pallas_call x2, Pallas kernels, apply_matrix(): pl.pallas_call(functools.partial(product_kernel, pieces.shape[0]), grid=(...  7.72 us
  transfers between devices with their start and end apart: 34, of which 18 were waited for; matrix products, arithmetic and copies ran while one was open for 10% of the time, Pallas kernels for 9%

profile of v5, /device:TPU:0, one launch (start us, length us, event | category | flops | bytes accessed | tf_op | source)
XLA Modules:
  0.0 320.5 jit_solution(8640372333602883813)
XLA Ops:
  7.2 2.2 fusion.33
  11.5 0.8 copy.15
  12.3 4.4 %all-to-all-start = ((f32[8,16,2,512]{3,1,2,0:T(8,128)}), f32[8,16,2,512]{3,1,2,0:T(8,128)S(1)}, u32[]{:S(2)}, u32[]{:S(2)}) async-start(f32[8,16,2,512]{3,1,2,0:T(8,128)} %copy.15), calls=%async_computation | async-start | bytes 1048576 | tf_op jit(solution)/shard_map/all_to_all | solution.py:30
  17.0 2.0 collective-permute-start.5
  19.0 3.6 %collective-permute-start.6 = (f32[2,128,256]{2,1,0:T(8,128)S(1)}, f32[2,128,256]{2,1,0:T(8,128)S(1)}, u32[]{:S(2)}, u32[]{:S(2)}) collective-permute-start(f32[2,128,256]{2,1,0:T(8,128)S(1)} %get-tuple-element.50), channel_id=1, source_target_pairs={{0,2},{1,3},{2,0},{3,1},{4,6},{5,7},{6,4},{7,5},{8,10},{9,11},{10,... | collective-permute-start | bytes 786440 | tf_op jit(solution)/shard_map/ppermute | solution.py:26
  22.6 1.0 collective-permute-start.7
  23.6 4.5 %collective-permute-done.5 = f32[2,128,256]{2,1,0:T(8,128)S(1)} collective-permute-done((f32[2,128,256]{2,1,0:T(8,128)S(1)}, f32[2,128,256]{2,1,0:T(8,128)S(1)}, u32[]{:S(2)}, u32[]{:S(2)}) %collective-permute-start.5) | collective-permute-done | bytes 262176 | tf_op jit(solution)/shard_map/ppermute | solution.py:26
  28.0 6.8 %collective-permute-done.6 = f32[2,128,256]{2,1,0:T(8,128)S(1)} collective-permute-done((f32[2,128,256]{2,1,0:T(8,128)S(1)}, f32[2,128,256]{2,1,0:T(8,128)S(1)}, u32[]{:S(2)}, u32[]{:S(2)}) %collective-permute-start.6) | collective-permute-done | bytes 262176 | tf_op jit(solution)/shard_map/ppermute | solution.py:26
  34.9 0.8 pad_maximum_fusion.8
  35.8 0.9 pad_maximum_fusion.7
  37.5 0.9 pad_maximum_fusion.6
  38.4 6.2 %all-to-all-start.1 = ((f32[16,16,512]{2,1,0:T(8,128)}), f32[16,16,512]{2,1,0:T(8,128)S(1)}, u32[]{:S(2)}, u32[]{:S(2)}) async-start(f32[16,16,512]{2,1,0:T(8,128)} %pad_maximum_fusion.6), calls=%async_computation.1 | async-start | bytes 1048576 | tf_op jit(solution)/shard_map/all_to_all | solution.py:30
  44.7 11.6 %all-to-all-done.1 = f32[16,16,512]{2,1,0:T(8,128)S(1)} async-done(((f32[16,16,512]{2,1,0:T(8,128)}), f32[16,16,512]{2,1,0:T(8,128)S(1)}, u32[]{:S(2)}, u32[]{:S(2)}) %all-to-all-start.1) | async-done | bytes 524320 | tf_op jit(solution)/shard_map/all_to_all | solution.py:30
  58.3 5.1 %shard_map.68 = f32[4,4,2,128,128]{4,3,2,1,0:T(8,128)} custom-call(f32[4096,256]{1,0:T(8,128)} %bitcast.102, f32[256,128]{1,0:T(8,128)} %slice.103.operand_ref), custom_call_target="tpu_custom_call" | custom-call | flops 805306368 | bytes 4194304 | tf_op jit(solution)/shard_map/pallas_call | solution.py:84
  63.4 3.7 %all-to-all-start.2 = ((f32[16,256,128]{2,1,0:T(8,128)}), f32[16,256,128]{2,1,0:T(8,128)S(1)}, u32[]{:S(2)}, u32[]{:S(2)}) async-start(f32[16,256,128]{2,1,0:T(8,128)} %bitcast.99), calls=%async_computation.2 | async-start | bytes 4194304 | tf_op jit(solution)/shard_map/all_to_all | solution.py:30
  67.2 4.1 %fusion.32 = (f32[4,1,512,256]{3,2,1,0:T(8,128)}, f32[4,1,512,256]{3,2,1,0:T(8,128)S(1)}) fusion(f32[4,2,512,256]{3,2,1,0:T(8,128)} %param.11), kind=kLoop, calls=%fused_computation.113 | loop fusion | bytes 8388608 | tf_op jit(solution)/shard_map/slice | solution.py:316
  71.3 1.2 dynamic-slice_bitcast_fusion.4
  72.5 3.3 %collective-permute-start = (f32[4,128,256]{2,1,0:T(8,128)}, f32[4,128,256]{2,1,0:T(8,128)}, u32[]{:S(2)}, u32[]{:S(2)}) collective-permute-start(f32[4,128,256]{2,1,0:T(8,128)} %get-tuple-element.17), channel_id=1, source_target_pairs={{0,2},{1,3},{2,0},{3,1},{4,6},{5,7},{6,4},{7,5},{8,10},{9,11},{10,... | collective-permute-start | bytes 1572872 | tf_op jit(solution)/shard_map/ppermute | solution.py:26
  76.4 2.7 collective-permute-start.2
  79.0 16.7 %all-to-all-done.2 = f32[16,256,128]{2,1,0:T(8,128)S(1)} async-done(((f32[16,256,128]{2,1,0:T(8,128)}), f32[16,256,128]{2,1,0:T(8,128)S(1)}, u32[]{:S(2)}, u32[]{:S(2)}) %all-to-all-start.2) | async-done | bytes 2097184 | tf_op jit(solution)/shard_map/all_to_all | solution.py:30
  95.9 10.8 %collective-permute-done.refs_2_ = f32[4,128,256]{2,1,0:T(8,128)} collective-permute-done((f32[4,128,256]{2,1,0:T(8,128)}, f32[4,128,256]{2,1,0:T(8,128)}, u32[]{:S(2)}, u32[]{:S(2)}) %collective-permute-start) | collective-permute-done | bytes 524320 | tf_op jit(solution)/shard_map/ppermute | solution.py:26
  106.7 7.8 %collective-permute-done.1.refs_1_ = f32[4,128,256]{2,1,0:T(8,128)} collective-permute-done((f32[4,128,256]{2,1,0:T(8,128)S(1)}, f32[4,128,256]{2,1,0:T(8,128)}, u32[]{:S(2)}, u32[]{:S(2)}) %collective-permute-start.1) | collective-permute-done | bytes 524320 | tf_op jit(solution)/shard_map/ppermute | solution.py:26
  114.4 1.0 collective-permute-done.2.refs_3_
  115.5 12.6 %all_to_all.50 = f32[4,256,128]{2,1,0:T(8,128)} all-to-all(f32[4,256,128]{2,1,0:T(8,128)S(1)} %broadcast_in_dim.41), channel_id=1, replica_groups=mesh['x'=4,'core'=2,'y'=4,'z'=4] {'z'}, dimensions={0} | all-to-all | bytes 1048576 | tf_op jit(solution)/shard_map/all_to_all | solution.py:30
  128.2 0.9 constant_dynamic-slice_fusion
  129.1 0.9 copy-done
  129.9 0.9 dynamic-slice_bitcast_fusion
  130.8 1.3 pad_maximum_fusion.3
  132.1 3.9 %shard_map.69 = f32[4,256,128]{2,1,0:T(8,128)} custom-call(s32[1]{0:T(128)} %bitcast.19.at_ref, f32[1024,1024]{1,0:T(8,128)} %all-gather.10.cloned.1.call-done.matrix_ref, f32[4,2,128,128]{3,2,1,0:T(8,128)} %bitcast.101), custom_call_target="tpu_custom_call" | custom-call | flops 805306368 | bytes 4194304 | tf_op jit(solution)/shard_map/pallas_call | solution.py:102
  136.0 1.2 collective-permute-start.9
  137.2 0.9 collective-permute-start.8
  138.0 4.2 %all-to-all-start.4 = ((f32[4,256,128]{2,1,0:T(8,128)}), f32[4,256,128]{2,1,0:T(8,128)S(1)}, u32[]{:S(2)}, u32[]{:S(2)}) async-start(f32[4,256,128]{2,1,0:T(8,128)} %shard_map.69), calls=%async_computation.4 | async-start | bytes 1048576 | tf_op jit(solution)/shard_map/all_to_all | solution.py:30
  142.2 1.2 pad_maximum_fusion.2.refs_0_.refs_8_
  143.4 6.9 %all-to-all-done.4 = f32[4,256,128]{2,1,0:T(8,128)S(1)} async-done(((f32[4,256,128]{2,1,0:T(8,128)}), f32[4,256,128]{2,1,0:T(8,128)S(1)}, u32[]{:S(2)}, u32[]{:S(2)}) %all-to-all-start.4) | async-done | bytes 524320 | tf_op jit(solution)/shard_map/all_to_all | solution.py:30
  151.0 1.0 slice_subtract_fusion
  152.0 2.2 collective-permute-done.9.refs_3_.refs_11_
  154.1 2.1 collective-permute-done.8.refs_1_.refs_9_
  156.2 0.9 broadcast_in_dim.42
  157.1 3.5 %all-to-all-start.5 = ((f32[4,256,128]{2,1,0:T(8,128)}), f32[4,256,128]{2,1,0:T(8,128)S(1)}, u32[]{:S(2)}, u32[]{:S(2)}) async-start(f32[4,256,128]{2,1,0:T(8,128)} %broadcast_in_dim.42), calls=%async_computation.5 | async-start | bytes 1048576 | tf_op jit(solution)/shard_map/all_to_all | solution.py:30
  160.6 1.9 pad_maximum_fusion.5
  162.5 6.2 %all-to-all-done.5 = f32[4,256,128]{2,1,0:T(8,128)S(1)} async-done(((f32[4,256,128]{2,1,0:T(8,128)}), f32[4,256,128]{2,1,0:T(8,128)S(1)}, u32[]{:S(2)}, u32[]{:S(2)}) %all-to-all-start.5) | async-done | bytes 524320 | tf_op jit(solution)/shard_map/all_to_all | solution.py:30
  169.4 3.9 %shard_map.70 = f32[4,256,128]{2,1,0:T(8,128)} custom-call(s32[1]{0:T(128)} %bitcast.19.at_ref, f32[1024,1024]{1,0:T(8,128)} %all-gather.8.cloned.1.call-done.matrix_ref, f32[4,2,128,128]{3,2,1,0:T(8,128)} %bitcast.107), custom_call_target="tpu_custom_call" | custom-call | flops 805306368 | bytes 4194304 | tf_op jit(solution)/shard_map/pallas_call | solution.py:102
  173.8 4.4 %all-to-all-start.6 = ((f32[4,256,128]{2,1,0:T(8,128)}), f32[4,256,128]{2,1,0:T(8,128)}, u32[]{:S(2)}, u32[]{:S(2)}) async-start(f32[4,256,128]{2,1,0:T(8,128)} %shard_map.70), calls=%async_computation.6 | async-start | bytes 1048576 | tf_op jit(solution)/shard_map/all_to_all | solution.py:30
  178.9 1.5 collective-permute-start.3
  180.4 6.1 %all-to-all-done.6 = f32[4,256,128]{2,1,0:T(8,128)} async-done(((f32[4,256,128]{2,1,0:T(8,128)}), f32[4,256,128]{2,1,0:T(8,128)}, u32[]{:S(2)}, u32[]{:S(2)}) %all-to-all-start.6) | async-done | bytes 524320 | tf_op jit(solution)/shard_map/all_to_all | solution.py:30
  186.4 1.1 reduce_sum.78
  187.5 3.2 collective-permute-done.10.refs_2_.refs_10_
  191.7 1.2 collective-permute-done.12
  193.6 1.5 broadcast_in_dim.45
  195.1 16.1 %all-to-all-start.7 = ((f32[16,256,128]{2,1,0:T(8,128)}), f32[16,256,128]{2,1,0:T(8,128)}, u32[]{:S(2)}, u32[]{:S(2)}) async-start(f32[16,256,128]{2,1,0:T(8,128)} %broadcast_in_dim.45), calls=%async_computation.7 | async-start | bytes 4194304 | tf_op jit(solution)/shard_map/all_to_all | solution.py:30
  211.9 2.3 gather_fusion
  214.2 2.3 gather_fusion.1
  218.0 1.0 collective-permute-done.20.refs_7_.refs_15_
  219.1 3.2 %collective-permute-done.18.refs_5_.refs_13_ = f32[4,128,384]{2,1,0:T(8,128)S(1)} collective-permute-done((f32[4,128,384]{2,1,0:T(8,128)S(1)}, f32[4,128,384]{2,1,0:T(8,128)S(1)}, u32[]{:S(2)}, u32[]{:S(2)}) %collective-permute-start.18) | collective-permute-done | bytes 786464 | tf_op jit(solution)/shard_map/ppermute | solution.py:26
  222.3 0.9 copy-done.7
  223.3 0.9 and_convert_fusion.refs_16_
  224.2 8.9 %shard_map.72.refs_8_ = f32[4,2,4,128,128]{4,3,2,1,0:T(8,128)} custom-call(s32[1]{0:T(128)} %bitcast.19.at_ref, f32[4,4,2,128,128]{4,3,2,1,0:T(8,128)} %all-gather.12.cloned.1.call-done.lists_ref, f32[4,128,384]{2,1,0:T(8,128)} %copy-done.1, f32[4,128,384]{2,1,0:T(8,128)} %copy-done.4, f32[4,128,384]{2,1,0:T(8,128)} %copy-done.5, f32[4,128,384]{2,1,0:T(8,128)} %copy-done.3, ...), custom_call_target="tpu_custom_call" | custom-call | flops 3221225472 | bytes 10485760 | tf_op jit(solution)/shard_map/pallas_call | solution.py:170
  233.2 8.4 %all-to-all-done.7 = f32[16,256,128]{2,1,0:T(8,128)} async-done(((f32[16,256,128]{2,1,0:T(8,128)}), f32[16,256,128]{2,1,0:T(8,128)}, u32[]{:S(2)}, u32[]{:S(2)}) %all-to-all-start.7) | async-done | bytes 2097184 | tf_op jit(solution)/shard_map/all_to_all | solution.py:30
  241.6 8.1 %shard_map.73 = f32[4,2,4,128,128]{4,3,2,1,0:T(8,128)} custom-call(s32[1]{0:T(128)} %bitcast.19.at_ref, f32[4,4,2,128,128]{4,3,2,1,0:T(8,128)} %bitcast.41.lists_ref, f32[4,128,256]{2,1,0:T(8,128)} %get-tuple-element.42.refs_0_, f32[4,128,256]{2,1,0:T(8,128)} %collective-permute-done.1.refs_1_, f32[4,128,256]{2,1,0:T(8,128)} %collective-permute-done.refs_2_, ...), custom_call_target="tpu_custom_call" | custom-call | flops 3221225472 | bytes 10485760 | tf_op jit(solution)/shard_map/pallas_call | solution.py:170
  249.7 43.7 %all_to_all.51 = f32[4,2,4,128,128]{4,3,2,1,0:T(8,128)S(1)} all-to-all(f32[4,2,4,128,128]{4,3,2,1,0:T(8,128)} %shard_map.73), channel_id=1, replica_groups=mesh['x'=4,'core'=2,'y'=4,'z'=4] {'y'}, dimensions={0} | all-to-all | bytes 4194304 | tf_op jit(solution)/shard_map/all_to_all | solution.py:30
  293.7 1.5 collective-permute-done.21
  295.9 12.5 %all_to_all.52 = f32[4,4,128,64]{2,3,1,0:T(8,128)S(1)} all-to-all(f32[4,4,128,64]{2,3,1,0:T(8,128)S(1)} %bitcast.104), channel_id=1, replica_groups=mesh['x'=4,'core'=2,'y'=4,'z'=4] {'z'}, dimensions={0} | all-to-all | bytes 1048576 | tf_op jit(solution)/shard_map/all_to_all | solution.py:30
  308.4 0.9 copy_bitcast_fusion
  309.3 4.7 %shard_map.71 = f32[2,512,1024]{2,1,0:T(8,128)} custom-call(f32[4,4,2,128,256]{4,3,2,1,0:T(8,128)} %bitcast.103), custom_call_target="tpu_custom_call" | custom-call | bytes 8388608 | tf_op jit(solution)/shard_map/pallas_call | solution.py:196
  (117 shorter events, 13.6 us)
Async XLA Ops:
  7.2 2.3 copy-start.11
  7.2 3.7 %copy-start.2 = (f32[6,512,128]{2,1,0:T(8,128)S(1)}, f32[6,512,128]{2,1,0:T(8,128)}, u32[]{:S(2)}) copy-start(f32[6,512,128]{2,1,0:T(8,128)} %param.8) | copy-start | bytes 4718596
  7.2 51.1 %all-gather.14.cloned.1.call-start = ((), (), s32[]{:S(2)}) async-start(), calls=%async_computation.13 | async-start | bytes 4718592 | tf_op jit(solution)/shard_map/all_gather | solution.py:264
  9.4 7.3 %copy-start.10 = (f32[512,256]{1,0:T(8,128)S(1)}, f32[512,256]{1,0:T(8,128)}, u32[]{:S(2)}) copy-start(f32[512,256]{1,0:T(8,128)} %param.10) | copy-start | bytes 1572868
  12.3 22.5 %all-to-all-start = ((f32[8,16,2,512]{3,1,2,0:T(8,128)}), f32[8,16,2,512]{3,1,2,0:T(8,128)S(1)}, u32[]{:S(2)}, u32[]{:S(2)}) async-start(f32[8,16,2,512]{3,1,2,0:T(8,128)} %copy.15), calls=%async_computation | async-start | bytes 1048576 | tf_op jit(solution)/shard_map/all_to_all | solution.py:30
  16.7 115.4 %all-gather.10.cloned.1.call-start = ((), (), s32[]{:S(2)}) async-start(), calls=%async_computation.11 | async-start | bytes 4718592 | tf_op jit(solution)/shard_map/all_gather | solution.py:262
  17.0 11.0 %collective-permute-start.5 = (f32[2,128,256]{2,1,0:T(8,128)S(1)}, f32[2,128,256]{2,1,0:T(8,128)S(1)}, u32[]{:S(2)}, u32[]{:S(2)}) collective-permute-start(f32[2,128,256]{2,1,0:T(8,128)S(1)} %get-tuple-element.51), channel_id=1, source_target_pairs={{0,1},{1,2},{2,3},{3,0},{4,5},{5,6},{6,7},{7,4},{8,9},{9,10},{10,1... | collective-permute-start | bytes 786440 | tf_op jit(solution)/shard_map/ppermute | solution.py:26
  19.0 15.8 %collective-permute-start.6 = (f32[2,128,256]{2,1,0:T(8,128)S(1)}, f32[2,128,256]{2,1,0:T(8,128)S(1)}, u32[]{:S(2)}, u32[]{:S(2)}) collective-permute-start(f32[2,128,256]{2,1,0:T(8,128)S(1)} %get-tuple-element.50), channel_id=1, source_target_pairs={{0,2},{1,3},{2,0},{3,1},{4,6},{5,7},{6,4},{7,5},{8,10},{9,11},{10,... | collective-permute-start | bytes 786440 | tf_op jit(solution)/shard_map/ppermute | solution.py:26
  22.6 12.3 %collective-permute-start.7 = (f32[2,128,256]{2,1,0:T(8,128)S(1)}, f32[2,128,256]{2,1,0:T(8,128)S(1)}, u32[]{:S(2)}, u32[]{:S(2)}) collective-permute-start(f32[2,128,256]{2,1,0:T(8,128)S(1)} %get-tuple-element.49), channel_id=1, source_target_pairs={{0,3},{1,0},{2,1},{3,2},{4,7},{5,4},{6,5},{7,6},{8,11},{9,8},{10,9... | collective-permute-start | bytes 786440 | tf_op jit(solution)/shard_map/ppermute | solution.py:26
  35.8 126.7 %all-gather.8.cloned.1.call-start = ((), (), s32[]{:S(2)}) async-start(), calls=%async_computation.10 | async-start | bytes 4718592 | tf_op jit(solution)/shard_map/all_gather | solution.py:262
  38.4 18.0 %all-to-all-start.1 = ((f32[16,16,512]{2,1,0:T(8,128)}), f32[16,16,512]{2,1,0:T(8,128)S(1)}, u32[]{:S(2)}, u32[]{:S(2)}) async-start(f32[16,16,512]{2,1,0:T(8,128)} %pad_maximum_fusion.6), calls=%async_computation.1 | async-start | bytes 1048576 | tf_op jit(solution)/shard_map/all_to_all | solution.py:30
  57.0 0.7 copy-start.9
  63.4 32.4 %all-to-all-start.2 = ((f32[16,256,128]{2,1,0:T(8,128)}), f32[16,256,128]{2,1,0:T(8,128)S(1)}, u32[]{:S(2)}, u32[]{:S(2)}) async-start(f32[16,256,128]{2,1,0:T(8,128)} %bitcast.99), calls=%async_computation.2 | async-start | bytes 4194304 | tf_op jit(solution)/shard_map/all_to_all | solution.py:30
  67.1 157.1 %all-gather.12.cloned.1.call-start = ((), (), s32[]{:S(2)}) async-start(), calls=%async_computation.12 | async-start | bytes 2621440 | tf_op jit(solution)/shard_map/all_gather | solution.py:329
  72.5 34.2 %collective-permute-start = (f32[4,128,256]{2,1,0:T(8,128)}, f32[4,128,256]{2,1,0:T(8,128)}, u32[]{:S(2)}, u32[]{:S(2)}) collective-permute-start(f32[4,128,256]{2,1,0:T(8,128)} %get-tuple-element.17), channel_id=1, source_target_pairs={{0,2},{1,3},{2,0},{3,1},{4,6},{5,7},{6,4},{7,5},{8,10},{9,11},{10,... | collective-permute-start | bytes 1572872 | tf_op jit(solution)/shard_map/ppermute | solution.py:26
  75.8 38.6 %collective-permute-start.1 = (f32[4,128,256]{2,1,0:T(8,128)S(1)}, f32[4,128,256]{2,1,0:T(8,128)}, u32[]{:S(2)}, u32[]{:S(2)}) collective-permute-start(f32[4,128,256]{2,1,0:T(8,128)S(1)} %get-tuple-element.18), channel_id=1, source_target_pairs={{0,1},{1,2},{2,3},{3,0},{4,5},{5,6},{6,7},{7,4},{8,9},{9,10},{10,1... | collective-permute-start | bytes 1572872 | tf_op jit(solution)/shard_map/ppermute | solution.py:26
  76.4 39.1 %collective-permute-start.2 = (f32[4,128,256]{2,1,0:T(8,128)S(1)}, f32[4,128,256]{2,1,0:T(8,128)}, u32[]{:S(2)}, u32[]{:S(2)}) collective-permute-start(f32[4,128,256]{2,1,0:T(8,128)S(1)} %get-tuple-element.19), channel_id=1, source_target_pairs={{0,3},{1,0},{2,1},{3,2},{4,7},{5,4},{6,5},{7,6},{8,11},{9,8},{10,9... | collective-permute-start | bytes 1572872 | tf_op jit(solution)/shard_map/ppermute | solution.py:26
  115.4 12.7 %slice-start = ((f32[6,512,128]{2,1,0:T(8,128)}), f32[4,512,128]{2,1,0:T(8,128)S(1)}, s32[]{:S(2)}) async-start(f32[6,512,128]{2,1,0:T(8,128)} %param.8), calls=%async_computation.15 | async-start | bytes 2097152 | tf_op jit(solution)/shard_map/slice | solution.py:316
  128.1 1.8 copy-start
  136.0 18.1 %collective-permute-start.9 = (f32[4,128,384]{2,1,0:T(8,128)}, f32[4,128,384]{2,1,0:T(8,128)S(1)}, u32[]{:S(2)}, u32[]{:S(2)}) collective-permute-start(f32[4,128,384]{2,1,0:T(8,128)} %get-tuple-element.27), channel_id=1, source_target_pairs={{0,3},{1,0},{2,1},{3,2},{4,7},{5,4},{6,5},{7,6},{8,11},{9,8},{10,9... | collective-permute-start | bytes 2359304 | tf_op jit(solution)/shard_map/ppermute | solution.py:26
  137.2 19.1 %collective-permute-start.8 = (f32[4,128,384]{2,1,0:T(8,128)}, f32[4,128,384]{2,1,0:T(8,128)S(1)}, u32[]{:S(2)}, u32[]{:S(2)}) collective-permute-start(f32[4,128,384]{2,1,0:T(8,128)} %get-tuple-element.26), channel_id=1, source_target_pairs={{0,1},{1,2},{2,3},{3,0},{4,5},{5,6},{6,7},{7,4},{8,9},{9,10},{10,1... | collective-permute-start | bytes 2359304 | tf_op jit(solution)/shard_map/ppermute | solution.py:26
  138.0 12.3 %all-to-all-start.4 = ((f32[4,256,128]{2,1,0:T(8,128)}), f32[4,256,128]{2,1,0:T(8,128)S(1)}, u32[]{:S(2)}, u32[]{:S(2)}) async-start(f32[4,256,128]{2,1,0:T(8,128)} %shard_map.69), calls=%async_computation.4 | async-start | bytes 1048576 | tf_op jit(solution)/shard_map/all_to_all | solution.py:30
  143.4 67.9 %copy-start.1 = (f32[4,128,384]{2,1,0:T(8,128)}, f32[4,128,384]{2,1,0:T(8,128)S(1)}, u32[]{:S(2)}) copy-start(f32[4,128,384]{2,1,0:T(8,128)S(1)} %pad_maximum_fusion.2.refs_0_.refs_8_) | copy-start | bytes 2359300
  154.1 62.4 %copy-start.3 = (f32[4,128,384]{2,1,0:T(8,128)}, f32[4,128,384]{2,1,0:T(8,128)S(1)}, u32[]{:S(2)}) copy-start(f32[4,128,384]{2,1,0:T(8,128)S(1)} %collective-permute-done.9.refs_3_.refs_11_) | copy-start | bytes 2359300
  156.2 60.5 %copy-start.4 = (f32[4,128,384]{2,1,0:T(8,128)}, f32[4,128,384]{2,1,0:T(8,128)S(1)}, u32[]{:S(2)}) copy-start(f32[4,128,384]{2,1,0:T(8,128)S(1)} %collective-permute-done.8.refs_1_.refs_9_) | copy-start | bytes 2359300
  157.1 11.5 %all-to-all-start.5 = ((f32[4,256,128]{2,1,0:T(8,128)}), f32[4,256,128]{2,1,0:T(8,128)S(1)}, u32[]{:S(2)}, u32[]{:S(2)}) async-start(f32[4,256,128]{2,1,0:T(8,128)} %broadcast_in_dim.42), calls=%async_computation.5 | async-start | bytes 1048576 | tf_op jit(solution)/shard_map/all_to_all | solution.py:30
  168.6 0.8 copy-start.8
  173.3 17.4 %collective-permute-start.10 = (f32[4,128,384]{2,1,0:T(8,128)}, f32[4,128,384]{2,1,0:T(8,128)S(1)}, u32[]{:S(2)}, u32[]{:S(2)}) collective-permute-start(f32[4,128,384]{2,1,0:T(8,128)} %pad_maximum_fusion.5), channel_id=1, source_target_pairs={{0,2},{1,3},{2,0},{3,1},{4,6},{5,7},{6,4},{7,5},{8,10},{9,11},{10,... | collective-permute-start | bytes 2359304 | tf_op jit(solution)/shard_map/ppermute | solution.py:26
  173.8 12.6 %all-to-all-start.6 = ((f32[4,256,128]{2,1,0:T(8,128)}), f32[4,256,128]{2,1,0:T(8,128)}, u32[]{:S(2)}, u32[]{:S(2)}) async-start(f32[4,256,128]{2,1,0:T(8,128)} %shard_map.70), calls=%async_computation.6 | async-start | bytes 1048576 | tf_op jit(solution)/shard_map/all_to_all | solution.py:30
  178.2 131.0 %all-gather.16.cloned.1.call-start = ((), (), s32[]{:S(2)}) async-start(), calls=%async_computation.14 | async-start | bytes 4456448 | tf_op jit(solution)/shard_map/all_gather | solution.py:353
  178.9 12.7 %collective-permute-start.3 = (f32[128,128]{1,0:T(8,128)}, f32[128,128]{1,0:T(8,128)S(1)}, u32[]{:S(2)}, u32[]{:S(2)}) collective-permute-start(f32[128,128]{1,0:T(8,128)} %get-tuple-element.67), channel_id=1, source_target_pairs={{0,0},{1,1},{2,2},{3,3},{4,32},{5,33},{6,34},{7,35},{8,64},{9,65},... | collective-permute-start | bytes 196616 | tf_op jit(solution)/shard_map/ppermute | solution.py:312
  180.4 11.3 %collective-permute-start.4 = (f32[128,128]{1,0:T(8,128)S(1)}, f32[128,128]{1,0:T(8,128)S(1)}, u32[]{:S(2)}, u32[]{:S(2)}) collective-permute-start(f32[128,128]{1,0:T(8,128)S(1)} %get-tuple-element.68), channel_id=1, source_target_pairs={{0,16},{1,17},{2,18},{3,19},{4,48},{5,49},{6,50},{7,51},{8,80},{9,... | collective-permute-start | bytes 196616 | tf_op jit(solution)/shard_map/ppermute | solution.py:312
  190.7 26.6 %copy-start.5 = (f32[4,128,384]{2,1,0:T(8,128)}, f32[4,128,384]{2,1,0:T(8,128)S(1)}, u32[]{:S(2)}) copy-start(f32[4,128,384]{2,1,0:T(8,128)S(1)} %collective-permute-done.10.refs_2_.refs_10_) | copy-start | bytes 2359300
  190.7 1.0 collective-permute-start.11
  191.4 1.5 collective-permute-start.12
  195.1 46.5 %all-to-all-start.7 = ((f32[16,256,128]{2,1,0:T(8,128)}), f32[16,256,128]{2,1,0:T(8,128)}, u32[]{:S(2)}, u32[]{:S(2)}) async-start(f32[16,256,128]{2,1,0:T(8,128)} %broadcast_in_dim.45), calls=%async_computation.7 | async-start | bytes 4194304 | tf_op jit(solution)/shard_map/all_to_all | solution.py:30
  211.3 6.2 %collective-permute-start.17 = (f32[4,128,384]{2,1,0:T(8,128)S(1)}, f32[4,128,384]{2,1,0:T(8,128)}, u32[]{:S(2)}, u32[]{:S(2)}) collective-permute-start(f32[4,128,384]{2,1,0:T(8,128)S(1)} %pad_maximum_fusion.2.refs_0_.refs_8_), channel_id=1, source_target_pairs={{0,16},{16,0},{1,17},{17,1},{2,18},{18,2},{3,19},{19,3},{4,20},{20... | collective-permute-start | bytes 2359304 | tf_op jit(solution)/shard_map/ppermute | solution.py:26
  211.4 21.8 %collective-permute-start.13 = (f32[4,128,256]{2,1,0:T(8,128)}, f32[4,128,256]{2,1,0:T(8,128)}, u32[]{:S(2)}, u32[]{:S(2)}) collective-permute-start(f32[4,128,256]{2,1,0:T(8,128)} %get-tuple-element.42.refs_0_), channel_id=1, source_target_pairs={{0,16},{16,0},{1,17},{17,1},{2,18},{18,2},{3,19},{19,3},{4,20},{20... | collective-permute-start | bytes 1572872 | tf_op jit(solution)/shard_map/ppermute | solution.py:26
  216.6 2.4 collective-permute-start.20
  216.7 5.6 %collective-permute-start.18 = (f32[4,128,384]{2,1,0:T(8,128)S(1)}, f32[4,128,384]{2,1,0:T(8,128)S(1)}, u32[]{:S(2)}, u32[]{:S(2)}) collective-permute-start(f32[4,128,384]{2,1,0:T(8,128)S(1)} %collective-permute-done.8.refs_1_.refs_9_), channel_id=1, source_target_pairs={{0,16},{16,0},{1,17},{17,1},{2,18},{18,2},{3,19},{19,3},{4,20},{20... | collective-permute-start | bytes 2359304 | tf_op jit(solution)/shard_map/ppermute | solution.py:26
  217.2 7.0 %collective-permute-start.19 = (f32[4,128,384]{2,1,0:T(8,128)S(1)}, f32[4,128,384]{2,1,0:T(8,128)}, u32[]{:S(2)}, u32[]{:S(2)}) collective-permute-start(f32[4,128,384]{2,1,0:T(8,128)S(1)} %collective-permute-done.10.refs_2_.refs_10_), channel_id=1, source_target_pairs={{0,16},{16,0},{1,17},{17,1},{2,18},{18,2},{3,19},{19,3},{4,20},{20... | collective-permute-start | bytes 2359304 | tf_op jit(solution)/shard_map/ppermute | solution.py:26
  217.5 15.7 %collective-permute-start.15 = (f32[4,128,256]{2,1,0:T(8,128)}, f32[4,128,256]{2,1,0:T(8,128)S(1)}, u32[]{:S(2)}, u32[]{:S(2)}) collective-permute-start(f32[4,128,256]{2,1,0:T(8,128)} %collective-permute-done.refs_2_), channel_id=1, source_target_pairs={{0,16},{16,0},{1,17},{17,1},{2,18},{18,2},{3,19},{19,3},{4,20},{20... | collective-permute-start | bytes 1572872 | tf_op jit(solution)/shard_map/ppermute | solution.py:26
  218.9 3.4 %copy-start.6 = (f32[4,128,384]{2,1,0:T(8,128)}, f32[4,128,384]{2,1,0:T(8,128)S(1)}, u32[]{:S(2)}) copy-start(f32[4,128,384]{2,1,0:T(8,128)S(1)} %collective-permute-done.20.refs_7_.refs_15_) | copy-start | bytes 2359300
  218.9 14.3 %collective-permute-start.14 = (f32[4,128,256]{2,1,0:T(8,128)}, f32[4,128,256]{2,1,0:T(8,128)S(1)}, u32[]{:S(2)}, u32[]{:S(2)}) collective-permute-start(f32[4,128,256]{2,1,0:T(8,128)} %collective-permute-done.1.refs_1_), channel_id=1, source_target_pairs={{0,16},{16,0},{1,17},{17,1},{2,18},{18,2},{3,19},{19,3},{4,20},{20... | collective-permute-start | bytes 1572872 | tf_op jit(solution)/shard_map/ppermute | solution.py:26
  222.3 0.9 copy-start.7
  223.2 10.0 %collective-permute-start.16 = (f32[4,128,256]{2,1,0:T(8,128)}, f32[4,128,256]{2,1,0:T(8,128)S(1)}, u32[]{:S(2)}, u32[]{:S(2)}) collective-permute-start(f32[4,128,256]{2,1,0:T(8,128)} %collective-permute-done.2.refs_3_), channel_id=1, source_target_pairs={{0,16},{16,0},{1,17},{17,1},{2,18},{18,2},{3,19},{19,3},{4,20},{20... | collective-permute-start | bytes 1572872 | tf_op jit(solution)/shard_map/ppermute | solution.py:26
  233.2 8.4 %copy-start.12 = (f32[4,128,256]{2,1,0:T(8,128)}, f32[4,128,256]{2,1,0:T(8,128)S(1)}, u32[]{:S(2)}) copy-start(f32[4,128,256]{2,1,0:T(8,128)S(1)} %collective-permute-done.15.refs_6_) | copy-start | bytes 1572868
  233.2 8.4 %copy-start.13 = (f32[4,128,256]{2,1,0:T(8,128)}, f32[4,128,256]{2,1,0:T(8,128)S(1)}, u32[]{:S(2)}) copy-start(f32[4,128,256]{2,1,0:T(8,128)S(1)} %collective-permute-done.14.refs_5_) | copy-start | bytes 1572868
  233.2 8.4 %copy-start.14 = (f32[4,128,256]{2,1,0:T(8,128)}, f32[4,128,256]{2,1,0:T(8,128)S(1)}, u32[]{:S(2)}) copy-start(f32[4,128,256]{2,1,0:T(8,128)S(1)} %collective-permute-done.16.refs_7_) | copy-start | bytes 1572868
  293.6 1.6 collective-permute-start.21
Sparse Core Ops, SparseCore 0:
  10.3 35.2 all-gather.13
  47.3 32.5 all-gather.9
  81.6 32.0 all-gather.7
  128.3 29.9 all-gather.11
  193.7 99.4 all-gather.15

commit v6 on v5

--- a/solution.py
+++ b/solution.py
@@ -276,6 +276,8 @@
     by_sub = slab_gram[:, :, 1].reshape(n_y, n_core, slab_slots, n_z, quarter).transpose(0, 3, 2, 1, 4)
     by_sub = by_sub.reshape(n_cols, slab_slots, sub)
     sub_gram = exchange(jnp.concatenate([by_width, by_sub], axis=2), COLS)
+    far_piece = moved(lambda at: rows_at(trail_factor[:, 1], at), n_z // 2, slab_gram)
+    sub_gram, far_piece = lax.optimization_barrier((sub_gram, far_piece))
     slab_owner = lax.dynamic_slice_in_dim(owners, row * slab, slab)
     slab_rank = lax.dynamic_slice_in_dim(pair_rank, row * slab, slab)
     slab_slot = jnp.arange(slab, dtype=jnp.int32) // run_len * per_run + slab_rank
@@ -322,7 +324,7 @@
     near = [by for by in range(1, n_z) if by != far]
     own_0, own_1 = {0: trail_0(z_at)}, {0: trail_1(z_at)}
     terms = apply_first(inverse_0, rhs[:width], n_y, n_z, n_core)
-    own_1[far] = moved(trail_1, far, slab_gram)
+    own_1[far] = far_piece
     own_1.update({by: moved(trail_1, by, terms) for by in near})
     first = after(summed(terms.reshape(n_cols, sub, slab), COLS), *own_1.values())
     first_pieces = spread_z(first)

time: 324 us -> 322 us (level)
    ppermute x18, waiting for transfers between devices: 43.9 us -> 32 us  [shift(): lax.ppermute(value, axis, [(i, (i + by) % size) for i in range(size)])]
    all_to_all x7, waiting for transfers between devices: 55.8 us -> 65 us  [exchange(): return lax.all_to_all(value, axes, 0, 0, tiled=True)]
  transfers between devices with their start and end apart: 34 -> 34, of which waited for: 18 -> 17; matrix products, arithmetic and copies ran while one was open for 10% -> 10% of each run, Pallas kernels for 9% -> 9%
where the time goes in v6:
time: 322 us; the launch traced here: 319 us
  waiting for transfers between devices  98.2 us (30%)
  blocking collectives  69.3 us (22%)
  starting transfers between devices  63.6 us (20%)
  Pallas kernels  34.5 us (11%)
  local copies, waits for them, and re-layouts  24 us (7%)
  between operations  14.4 us (4%)
  other arithmetic  12.7 us (4%)
    all_to_all x3, blocking collectives, exchange(): return lax.all_to_all(value, axes, 0, 0, tiled=True)  69.3 us
    all_to_all x7, waiting for transfers between devices, exchange(): return lax.all_to_all(value, axes, 0, 0, tiled=True)  65 us
    all_to_all x7, starting transfers between devices, exchange(): return lax.all_to_all(value, axes, 0, 0, tiled=True)  44.3 us
    ppermute x18, waiting for transfers between devices, shift(): lax.ppermute(value, axis, [(i, (i + by) % size) for i in range(size)])  32 us
    pallas_call x2, Pallas kernels, apply_trail(): pl.pallas_call(functools.partial(trail_kernel, n_z, with_gram), grid=(blo...  17 us
    ppermute x18, starting transfers between devices, shift(): lax.ppermute(value, axis, [(i, (i + by) % size) for i in range(size)])  16.7 us
    pallas_call x2, Pallas kernels, apply_matrix(): pl.pallas_call(functools.partial(product_kernel, pieces.shape[0]), grid=(...  7.72 us
  transfers between devices with their start and end apart: 34, of which 17 were waited for; matrix products, arithmetic and copies ran while one was open for 10% of the time, Pallas kernels for 9%

profile of v6, /device:TPU:0, one launch (start us, length us, event | category | flops | bytes accessed | tf_op | source)
XLA Modules:
  0.0 318.6 jit_solution(3535673574301737531)
XLA Ops:
  7.2 2.2 fusion.33
  11.5 0.8 copy.15
  12.3 4.4 %all-to-all-start = ((f32[8,16,2,512]{3,1,2,0:T(8,128)}), f32[8,16,2,512]{3,1,2,0:T(8,128)S(1)}, u32[]{:S(2)}, u32[]{:S(2)}) async-start(f32[8,16,2,512]{3,1,2,0:T(8,128)} %copy.15), calls=%async_computation | async-start | bytes 1048576 | tf_op jit(solution)/shard_map/all_to_all | solution.py:30
  17.0 2.0 collective-permute-start.5
  19.0 3.6 %collective-permute-start.6 = (f32[2,128,256]{2,1,0:T(8,128)S(1)}, f32[2,128,256]{2,1,0:T(8,128)S(1)}, u32[]{:S(2)}, u32[]{:S(2)}) collective-permute-start(f32[2,128,256]{2,1,0:T(8,128)S(1)} %get-tuple-element.54), channel_id=1, source_target_pairs={{0,2},{1,3},{2,0},{3,1},{4,6},{5,7},{6,4},{7,5},{8,10},{9,11},{10,... | collective-permute-start | bytes 786440 | tf_op jit(solution)/shard_map/ppermute | solution.py:26
  22.6 1.0 collective-permute-start.7
  23.6 4.5 %collective-permute-done.5 = f32[2,128,256]{2,1,0:T(8,128)S(1)} collective-permute-done((f32[2,128,256]{2,1,0:T(8,128)S(1)}, f32[2,128,256]{2,1,0:T(8,128)S(1)}, u32[]{:S(2)}, u32[]{:S(2)}) %collective-permute-start.5) | collective-permute-done | bytes 262176 | tf_op jit(solution)/shard_map/ppermute | solution.py:26
  28.0 6.8 %collective-permute-done.6 = f32[2,128,256]{2,1,0:T(8,128)S(1)} collective-permute-done((f32[2,128,256]{2,1,0:T(8,128)S(1)}, f32[2,128,256]{2,1,0:T(8,128)S(1)}, u32[]{:S(2)}, u32[]{:S(2)}) %collective-permute-start.6) | collective-permute-done | bytes 262176 | tf_op jit(solution)/shard_map/ppermute | solution.py:26
  34.9 0.9 pad_maximum_fusion.8
  35.9 0.8 pad_maximum_fusion.7
  36.7 4.0 %fusion.32 = (f32[4,1,512,256]{3,2,1,0:T(8,128)}, f32[4,1,512,256]{3,2,1,0:T(8,128)S(1)}) fusion(f32[4,2,512,256]{3,2,1,0:T(8,128)} %param.11), kind=kLoop, calls=%fused_computation.113 | loop fusion | bytes 8388608 | tf_op jit(solution)/shard_map/slice | solution.py:318
  40.7 1.0 dynamic-slice_bitcast_fusion.4
  41.8 2.2 collective-permute-start
  44.8 0.9 pad_maximum_fusion.6
  45.6 5.7 %all-to-all-start.1 = ((f32[16,16,512]{2,1,0:T(8,128)}), f32[16,16,512]{2,1,0:T(8,128)S(1)}, u32[]{:S(2)}, u32[]{:S(2)}) async-start(f32[16,16,512]{2,1,0:T(8,128)} %pad_maximum_fusion.6), calls=%async_computation.1 | async-start | bytes 1048576 | tf_op jit(solution)/shard_map/all_to_all | solution.py:30
  51.4 11.1 %all-to-all-done.1 = f32[16,16,512]{2,1,0:T(8,128)S(1)} async-done(((f32[16,16,512]{2,1,0:T(8,128)}), f32[16,16,512]{2,1,0:T(8,128)S(1)}, u32[]{:S(2)}, u32[]{:S(2)}) %all-to-all-start.1) | async-done | bytes 524320 | tf_op jit(solution)/shard_map/all_to_all | solution.py:30
  64.5 5.1 %shard_map.68 = f32[4,4,2,128,128]{4,3,2,1,0:T(8,128)} custom-call(f32[4096,256]{1,0:T(8,128)} %bitcast.102, f32[256,128]{1,0:T(8,128)} %slice.103.operand_ref), custom_call_target="tpu_custom_call" | custom-call | flops 805306368 | bytes 4194304 | tf_op jit(solution)/shard_map/pallas_call | solution.py:84
  69.5 6.5 %all-to-all-start.2 = ((f32[16,256,128]{2,1,0:T(8,128)}), f32[16,256,128]{2,1,0:T(8,128)S(1)}, u32[]{:S(2)}, u32[]{:S(2)}) async-start(f32[16,256,128]{2,1,0:T(8,128)} %bitcast.99), calls=%async_computation.2 | async-start | bytes 4194304 | tf_op jit(solution)/shard_map/all_to_all | solution.py:30
  76.1 3.2 %collective-permute-start.2 = (f32[4,128,256]{2,1,0:T(8,128)S(1)}, f32[4,128,256]{2,1,0:T(8,128)}, u32[]{:S(2)}, u32[]{:S(2)}) collective-permute-start(f32[4,128,256]{2,1,0:T(8,128)S(1)} %get-tuple-element.23), channel_id=1, source_target_pairs={{0,3},{1,0},{2,1},{3,2},{4,7},{5,4},{6,5},{7,6},{8,11},{9,8},{10,9... | collective-permute-start | bytes 1572872 | tf_op jit(solution)/shard_map/ppermute | solution.py:26
  79.4 26.8 %all-to-all-done.2 = f32[16,256,128]{2,1,0:T(8,128)S(1)} async-done(((f32[16,256,128]{2,1,0:T(8,128)}), f32[16,256,128]{2,1,0:T(8,128)S(1)}, u32[]{:S(2)}, u32[]{:S(2)}) %all-to-all-start.2) | async-done | bytes 2097184 | tf_op jit(solution)/shard_map/all_to_all | solution.py:30
  106.2 5.8 %collective-permute-done.2.refs_3_ = f32[4,128,256]{2,1,0:T(8,128)} collective-permute-done((f32[4,128,256]{2,1,0:T(8,128)S(1)}, f32[4,128,256]{2,1,0:T(8,128)}, u32[]{:S(2)}, u32[]{:S(2)}) %collective-permute-start.2) | collective-permute-done | bytes 524320 | tf_op jit(solution)/shard_map/ppermute | solution.py:26
  112.0 1.2 collective-permute-done.1.refs_1_
  113.2 12.8 %all_to_all.50 = f32[4,256,128]{2,1,0:T(8,128)} all-to-all(f32[4,256,128]{2,1,0:T(8,128)S(1)} %broadcast_in_dim.41), channel_id=1, replica_groups=mesh['x'=4,'core'=2,'y'=4,'z'=4] {'z'}, dimensions={0} | all-to-all | bytes 1048576 | tf_op jit(solution)/shard_map/all_to_all | solution.py:30
  126.0 0.9 constant_dynamic-slice_fusion
  126.9 0.9 copy-done
  127.8 0.9 dynamic-slice_bitcast_fusion
  128.7 1.3 pad_maximum_fusion.3
  130.0 3.9 %shard_map.69 = f32[4,256,128]{2,1,0:T(8,128)} custom-call(s32[1]{0:T(128)} %bitcast.19.at_ref, f32[1024,1024]{1,0:T(8,128)} %all-gather.10.cloned.1.call-done.matrix_ref, f32[4,2,128,128]{3,2,1,0:T(8,128)} %bitcast.101), custom_call_target="tpu_custom_call" | custom-call | flops 805306368 | bytes 4194304 | tf_op jit(solution)/shard_map/pallas_call | solution.py:102
  133.9 1.2 collective-permute-start.9
  135.0 0.9 collective-permute-start.8
  135.9 4.2 %all-to-all-start.4 = ((f32[4,256,128]{2,1,0:T(8,128)}), f32[4,256,128]{2,1,0:T(8,128)S(1)}, u32[]{:S(2)}, u32[]{:S(2)}) async-start(f32[4,256,128]{2,1,0:T(8,128)} %shard_map.69), calls=%async_computation.4 | async-start | bytes 1048576 | tf_op jit(solution)/shard_map/all_to_all | solution.py:30
  140.1 1.2 pad_maximum_fusion.2.refs_0_.refs_8_
  141.3 6.9 %all-to-all-done.4 = f32[4,256,128]{2,1,0:T(8,128)S(1)} async-done(((f32[4,256,128]{2,1,0:T(8,128)}), f32[4,256,128]{2,1,0:T(8,128)S(1)}, u32[]{:S(2)}, u32[]{:S(2)}) %all-to-all-start.4) | async-done | bytes 524320 | tf_op jit(solution)/shard_map/all_to_all | solution.py:30
  148.9 1.0 slice_subtract_fusion
  149.9 2.3 collective-permute-done.9.refs_3_.refs_11_
  152.2 2.1 collective-permute-done.8.refs_1_.refs_9_
  154.3 0.9 broadcast_in_dim.42
  155.2 3.5 %all-to-all-start.5 = ((f32[4,256,128]{2,1,0:T(8,128)}), f32[4,256,128]{2,1,0:T(8,128)S(1)}, u32[]{:S(2)}, u32[]{:S(2)}) async-start(f32[4,256,128]{2,1,0:T(8,128)} %broadcast_in_dim.42), calls=%async_computation.5 | async-start | bytes 1048576 | tf_op jit(solution)/shard_map/all_to_all | solution.py:30
  158.7 1.9 pad_maximum_fusion.5
  160.6 6.2 %all-to-all-done.5 = f32[4,256,128]{2,1,0:T(8,128)S(1)} async-done(((f32[4,256,128]{2,1,0:T(8,128)}), f32[4,256,128]{2,1,0:T(8,128)S(1)}, u32[]{:S(2)}, u32[]{:S(2)}) %all-to-all-start.5) | async-done | bytes 524320 | tf_op jit(solution)/shard_map/all_to_all | solution.py:30
  166.7 0.8 copy-done.8
  167.5 3.9 %shard_map.70 = f32[4,256,128]{2,1,0:T(8,128)} custom-call(s32[1]{0:T(128)} %bitcast.19.at_ref, f32[1024,1024]{1,0:T(8,128)} %all-gather.8.cloned.1.call-done.matrix_ref, f32[4,2,128,128]{3,2,1,0:T(8,128)} %bitcast.107), custom_call_target="tpu_custom_call" | custom-call | flops 805306368 | bytes 4194304 | tf_op jit(solution)/shard_map/pallas_call | solution.py:102
  171.9 4.2 %all-to-all-start.6 = ((f32[4,256,128]{2,1,0:T(8,128)}), f32[4,256,128]{2,1,0:T(8,128)}, u32[]{:S(2)}, u32[]{:S(2)}) async-start(f32[4,256,128]{2,1,0:T(8,128)} %shard_map.70), calls=%async_computation.6 | async-start | bytes 1048576 | tf_op jit(solution)/shard_map/all_to_all | solution.py:30
  176.8 1.5 collective-permute-start.3
  178.3 6.0 %all-to-all-done.6 = f32[4,256,128]{2,1,0:T(8,128)} async-done(((f32[4,256,128]{2,1,0:T(8,128)}), f32[4,256,128]{2,1,0:T(8,128)}, u32[]{:S(2)}, u32[]{:S(2)}) %all-to-all-start.6) | async-done | bytes 524320 | tf_op jit(solution)/shard_map/all_to_all | solution.py:30
  184.3 1.1 reduce_sum.78
  185.4 3.6 %collective-permute-done.10.refs_2_.refs_10_ = f32[4,128,384]{2,1,0:T(8,128)S(1)} collective-permute-done((f32[4,128,384]{2,1,0:T(8,128)}, f32[4,128,384]{2,1,0:T(8,128)S(1)}, u32[]{:S(2)}, u32[]{:S(2)}) %collective-permute-start.10) | collective-permute-done | bytes 786464 | tf_op jit(solution)/shard_map/ppermute | solution.py:26
  190.0 1.2 collective-permute-done.12
  191.9 1.5 broadcast_in_dim.45
  193.5 15.8 %all-to-all-start.7 = ((f32[16,256,128]{2,1,0:T(8,128)}), f32[16,256,128]{2,1,0:T(8,128)}, u32[]{:S(2)}, u32[]{:S(2)}) async-start(f32[16,256,128]{2,1,0:T(8,128)} %broadcast_in_dim.45), calls=%async_computation.7 | async-start | bytes 4194304 | tf_op jit(solution)/shard_map/all_to_all | solution.py:30
  210.0 2.3 gather_fusion
  212.3 2.3 gather_fusion.1
  216.0 1.0 collective-permute-done.20.refs_7_.refs_15_
  217.1 3.2 %collective-permute-done.18.refs_5_.refs_13_ = f32[4,128,384]{2,1,0:T(8,128)S(1)} collective-permute-done((f32[4,128,384]{2,1,0:T(8,128)S(1)}, f32[4,128,384]{2,1,0:T(8,128)S(1)}, u32[]{:S(2)}, u32[]{:S(2)}) %collective-permute-start.18) | collective-permute-done | bytes 786464 | tf_op jit(solution)/shard_map/ppermute | solution.py:26
  220.4 0.9 copy-done.7
  221.4 0.9 and_convert_fusion.refs_16_
  222.3 8.9 %shard_map.72.refs_8_ = f32[4,2,4,128,128]{4,3,2,1,0:T(8,128)} custom-call(s32[1]{0:T(128)} %bitcast.19.at_ref, f32[4,4,2,128,128]{4,3,2,1,0:T(8,128)} %all-gather.12.cloned.1.call-done.lists_ref, f32[4,128,384]{2,1,0:T(8,128)} %copy-done.1, f32[4,128,384]{2,1,0:T(8,128)} %copy-done.4, f32[4,128,384]{2,1,0:T(8,128)} %copy-done.5, f32[4,128,384]{2,1,0:T(8,128)} %copy-done.3, ...), custom_call_target="tpu_custom_call" | custom-call | flops 3221225472 | bytes 10485760 | tf_op jit(solution)/shard_map/pallas_call | solution.py:170
  231.3 8.0 %all-to-all-done.7 = f32[16,256,128]{2,1,0:T(8,128)} async-done(((f32[16,256,128]{2,1,0:T(8,128)}), f32[16,256,128]{2,1,0:T(8,128)}, u32[]{:S(2)}, u32[]{:S(2)}) %all-to-all-start.7) | async-done | bytes 2097184 | tf_op jit(solution)/shard_map/all_to_all | solution.py:30
  239.3 8.1 %shard_map.73 = f32[4,2,4,128,128]{4,3,2,1,0:T(8,128)} custom-call(s32[1]{0:T(128)} %bitcast.19.at_ref, f32[4,4,2,128,128]{4,3,2,1,0:T(8,128)} %bitcast.41.lists_ref, f32[4,128,256]{2,1,0:T(8,128)} %get-tuple-element.45.refs_0_, f32[4,128,256]{2,1,0:T(8,128)} %collective-permute-done.1.refs_1_, f32[4,128,256]{2,1,0:T(8,128)} %collective-permute-done.refs_2_, ...), custom_call_target="tpu_custom_call" | custom-call | flops 3221225472 | bytes 10485760 | tf_op jit(solution)/shard_map/pallas_call | solution.py:170
  247.4 44.1 %all_to_all.51 = f32[4,2,4,128,128]{4,3,2,1,0:T(8,128)S(1)} all-to-all(f32[4,2,4,128,128]{4,3,2,1,0:T(8,128)} %shard_map.73), channel_id=1, replica_groups=mesh['x'=4,'core'=2,'y'=4,'z'=4] {'y'}, dimensions={0} | all-to-all | bytes 4194304 | tf_op jit(solution)/shard_map/all_to_all | solution.py:30
  291.8 1.5 collective-permute-done.21
  294.0 12.5 %all_to_all.52 = f32[4,4,128,64]{2,3,1,0:T(8,128)S(1)} all-to-all(f32[4,4,128,64]{2,3,1,0:T(8,128)S(1)} %bitcast.104), channel_id=1, replica_groups=mesh['x'=4,'core'=2,'y'=4,'z'=4] {'z'}, dimensions={0} | all-to-all | bytes 1048576 | tf_op jit(solution)/shard_map/all_to_all | solution.py:30
  306.4 0.9 copy_bitcast_fusion
  307.3 4.7 %shard_map.71 = f32[2,512,1024]{2,1,0:T(8,128)} custom-call(f32[4,4,2,128,256]{4,3,2,1,0:T(8,128)} %bitcast.103), custom_call_target="tpu_custom_call" | custom-call | bytes 8388608 | tf_op jit(solution)/shard_map/pallas_call | solution.py:196
  (117 shorter events, 12.3 us)
Async XLA Ops:
  7.2 2.3 copy-start.11
  7.2 3.7 %copy-start.2 = (f32[6,512,128]{2,1,0:T(8,128)S(1)}, f32[6,512,128]{2,1,0:T(8,128)}, u32[]{:S(2)}) copy-start(f32[6,512,128]{2,1,0:T(8,128)} %param.8) | copy-start | bytes 4718596
  7.2 57.3 %all-gather.14.cloned.1.call-start = ((), (), s32[]{:S(2)}) async-start(), calls=%async_computation.13 | async-start | bytes 4718592 | tf_op jit(solution)/shard_map/all_gather | solution.py:264
  9.4 7.3 %copy-start.10 = (f32[512,256]{1,0:T(8,128)S(1)}, f32[512,256]{1,0:T(8,128)}, u32[]{:S(2)}) copy-start(f32[512,256]{1,0:T(8,128)} %param.10) | copy-start | bytes 1572868
  12.3 22.5 %all-to-all-start = ((f32[8,16,2,512]{3,1,2,0:T(8,128)}), f32[8,16,2,512]{3,1,2,0:T(8,128)S(1)}, u32[]{:S(2)}, u32[]{:S(2)}) async-start(f32[8,16,2,512]{3,1,2,0:T(8,128)} %copy.15), calls=%async_computation | async-start | bytes 1048576 | tf_op jit(solution)/shard_map/all_to_all | solution.py:30
  16.7 113.3 %all-gather.10.cloned.1.call-start = ((), (), s32[]{:S(2)}) async-start(), calls=%async_computation.11 | async-start | bytes 4718592 | tf_op jit(solution)/shard_map/all_gather | solution.py:262
  17.0 11.0 %collective-permute-start.5 = (f32[2,128,256]{2,1,0:T(8,128)S(1)}, f32[2,128,256]{2,1,0:T(8,128)S(1)}, u32[]{:S(2)}, u32[]{:S(2)}) collective-permute-start(f32[2,128,256]{2,1,0:T(8,128)S(1)} %get-tuple-element.55), channel_id=1, source_target_pairs={{0,1},{1,2},{2,3},{3,0},{4,5},{5,6},{6,7},{7,4},{8,9},{9,10},{10,1... | collective-permute-start | bytes 786440 | tf_op jit(solution)/shard_map/ppermute | solution.py:26
  19.0 15.8 %collective-permute-start.6 = (f32[2,128,256]{2,1,0:T(8,128)S(1)}, f32[2,128,256]{2,1,0:T(8,128)S(1)}, u32[]{:S(2)}, u32[]{:S(2)}) collective-permute-start(f32[2,128,256]{2,1,0:T(8,128)S(1)} %get-tuple-element.54), channel_id=1, source_target_pairs={{0,2},{1,3},{2,0},{3,1},{4,6},{5,7},{6,4},{7,5},{8,10},{9,11},{10,... | collective-permute-start | bytes 786440 | tf_op jit(solution)/shard_map/ppermute | solution.py:26
  22.6 12.3 %collective-permute-start.7 = (f32[2,128,256]{2,1,0:T(8,128)S(1)}, f32[2,128,256]{2,1,0:T(8,128)S(1)}, u32[]{:S(2)}, u32[]{:S(2)}) collective-permute-start(f32[2,128,256]{2,1,0:T(8,128)S(1)} %get-tuple-element.53), channel_id=1, source_target_pairs={{0,3},{1,0},{2,1},{3,2},{4,7},{5,4},{6,5},{7,6},{8,11},{9,8},{10,9... | collective-permute-start | bytes 786440 | tf_op jit(solution)/shard_map/ppermute | solution.py:26
  35.8 124.8 %all-gather.8.cloned.1.call-start = ((), (), s32[]{:S(2)}) async-start(), calls=%async_computation.10 | async-start | bytes 4718592 | tf_op jit(solution)/shard_map/all_gather | solution.py:262
  41.8 20.8 %collective-permute-start = (f32[4,128,256]{2,1,0:T(8,128)S(1)}, f32[4,128,256]{2,1,0:T(8,128)}, u32[]{:S(2)}, u32[]{:S(2)}) collective-permute-start(f32[4,128,256]{2,1,0:T(8,128)S(1)} %get-tuple-element.19), channel_id=1, source_target_pairs={{0,2},{1,3},{2,0},{3,1},{4,6},{5,7},{6,4},{7,5},{8,10},{9,11},{10,... | collective-permute-start | bytes 1572872 | tf_op jit(solution)/shard_map/ppermute | solution.py:26
  45.6 16.9 %all-to-all-start.1 = ((f32[16,16,512]{2,1,0:T(8,128)}), f32[16,16,512]{2,1,0:T(8,128)S(1)}, u32[]{:S(2)}, u32[]{:S(2)}) async-start(f32[16,16,512]{2,1,0:T(8,128)} %pad_maximum_fusion.6), calls=%async_computation.1 | async-start | bytes 1048576 | tf_op jit(solution)/shard_map/all_to_all | solution.py:30
  63.1 0.7 copy-start.9
  69.5 36.6 %all-to-all-start.2 = ((f32[16,256,128]{2,1,0:T(8,128)}), f32[16,256,128]{2,1,0:T(8,128)S(1)}, u32[]{:S(2)}, u32[]{:S(2)}) async-start(f32[16,256,128]{2,1,0:T(8,128)} %bitcast.99), calls=%async_computation.2 | async-start | bytes 4194304 | tf_op jit(solution)/shard_map/all_to_all | solution.py:30
  76.1 146.2 %all-gather.12.cloned.1.call-start = ((), (), s32[]{:S(2)}) async-start(), calls=%async_computation.12 | async-start | bytes 2621440 | tf_op jit(solution)/shard_map/all_gather | solution.py:331
  76.1 35.9 %collective-permute-start.2 = (f32[4,128,256]{2,1,0:T(8,128)S(1)}, f32[4,128,256]{2,1,0:T(8,128)}, u32[]{:S(2)}, u32[]{:S(2)}) collective-permute-start(f32[4,128,256]{2,1,0:T(8,128)S(1)} %get-tuple-element.23), channel_id=1, source_target_pairs={{0,3},{1,0},{2,1},{3,2},{4,7},{5,4},{6,5},{7,6},{8,11},{9,8},{10,9... | collective-permute-start | bytes 1572872 | tf_op jit(solution)/shard_map/ppermute | solution.py:26
  79.3 33.8 %collective-permute-start.1 = (f32[4,128,256]{2,1,0:T(8,128)S(1)}, f32[4,128,256]{2,1,0:T(8,128)}, u32[]{:S(2)}, u32[]{:S(2)}) collective-permute-start(f32[4,128,256]{2,1,0:T(8,128)S(1)} %get-tuple-element.22), channel_id=1, source_target_pairs={{0,1},{1,2},{2,3},{3,0},{4,5},{5,6},{6,7},{7,4},{8,9},{9,10},{10,1... | collective-permute-start | bytes 1572872 | tf_op jit(solution)/shard_map/ppermute | solution.py:26
  113.2 12.9 %slice-start = ((f32[6,512,128]{2,1,0:T(8,128)}), f32[4,512,128]{2,1,0:T(8,128)S(1)}, s32[]{:S(2)}) async-start(f32[6,512,128]{2,1,0:T(8,128)} %param.8), calls=%async_computation.15 | async-start | bytes 2097152 | tf_op jit(solution)/shard_map/slice | solution.py:318
  126.0 1.8 copy-start
  133.9 18.4 %collective-permute-start.9 = (f32[4,128,384]{2,1,0:T(8,128)}, f32[4,128,384]{2,1,0:T(8,128)S(1)}, u32[]{:S(2)}, u32[]{:S(2)}) collective-permute-start(f32[4,128,384]{2,1,0:T(8,128)} %get-tuple-element.31), channel_id=1, source_target_pairs={{0,3},{1,0},{2,1},{3,2},{4,7},{5,4},{6,5},{7,6},{8,11},{9,8},{10,9... | collective-permute-start | bytes 2359304 | tf_op jit(solution)/shard_map/ppermute | solution.py:26
  135.0 19.3 %collective-permute-start.8 = (f32[4,128,384]{2,1,0:T(8,128)}, f32[4,128,384]{2,1,0:T(8,128)S(1)}, u32[]{:S(2)}, u32[]{:S(2)}) collective-permute-start(f32[4,128,384]{2,1,0:T(8,128)} %get-tuple-element.30), channel_id=1, source_target_pairs={{0,1},{1,2},{2,3},{3,0},{4,5},{5,6},{6,7},{7,4},{8,9},{9,10},{10,1... | collective-permute-start | bytes 2359304 | tf_op jit(solution)/shard_map/ppermute | solution.py:26
  135.9 12.3 %all-to-all-start.4 = ((f32[4,256,128]{2,1,0:T(8,128)}), f32[4,256,128]{2,1,0:T(8,128)S(1)}, u32[]{:S(2)}, u32[]{:S(2)}) async-start(f32[4,256,128]{2,1,0:T(8,128)} %shard_map.69), calls=%async_computation.4 | async-start | bytes 1048576 | tf_op jit(solution)/shard_map/all_to_all | solution.py:30
  141.3 68.0 %copy-start.1 = (f32[4,128,384]{2,1,0:T(8,128)}, f32[4,128,384]{2,1,0:T(8,128)S(1)}, u32[]{:S(2)}) copy-start(f32[4,128,384]{2,1,0:T(8,128)S(1)} %pad_maximum_fusion.2.refs_0_.refs_8_) | copy-start | bytes 2359300
  152.2 62.4 %copy-start.3 = (f32[4,128,384]{2,1,0:T(8,128)}, f32[4,128,384]{2,1,0:T(8,128)S(1)}, u32[]{:S(2)}) copy-start(f32[4,128,384]{2,1,0:T(8,128)S(1)} %collective-permute-done.9.refs_3_.refs_11_) | copy-start | bytes 2359300
  154.3 60.5 %copy-start.4 = (f32[4,128,384]{2,1,0:T(8,128)}, f32[4,128,384]{2,1,0:T(8,128)S(1)}, u32[]{:S(2)}) copy-start(f32[4,128,384]{2,1,0:T(8,128)S(1)} %collective-permute-done.8.refs_1_.refs_9_) | copy-start | bytes 2359300
  155.2 11.5 %all-to-all-start.5 = ((f32[4,256,128]{2,1,0:T(8,128)}), f32[4,256,128]{2,1,0:T(8,128)S(1)}, u32[]{:S(2)}, u32[]{:S(2)}) async-start(f32[4,256,128]{2,1,0:T(8,128)} %broadcast_in_dim.42), calls=%async_computation.5 | async-start | bytes 1048576 | tf_op jit(solution)/shard_map/all_to_all | solution.py:30
  166.7 0.8 copy-start.8
  171.4 17.6 %collective-permute-start.10 = (f32[4,128,384]{2,1,0:T(8,128)}, f32[4,128,384]{2,1,0:T(8,128)S(1)}, u32[]{:S(2)}, u32[]{:S(2)}) collective-permute-start(f32[4,128,384]{2,1,0:T(8,128)} %pad_maximum_fusion.5), channel_id=1, source_target_pairs={{0,2},{1,3},{2,0},{3,1},{4,6},{5,7},{6,4},{7,5},{8,10},{9,11},{10,... | collective-permute-start | bytes 2359304 | tf_op jit(solution)/shard_map/ppermute | solution.py:26
  171.9 12.4 %all-to-all-start.6 = ((f32[4,256,128]{2,1,0:T(8,128)}), f32[4,256,128]{2,1,0:T(8,128)}, u32[]{:S(2)}, u32[]{:S(2)}) async-start(f32[4,256,128]{2,1,0:T(8,128)} %shard_map.70), calls=%async_computation.6 | async-start | bytes 1048576 | tf_op jit(solution)/shard_map/all_to_all | solution.py:30
  176.1 131.2 %all-gather.16.cloned.1.call-start = ((), (), s32[]{:S(2)}) async-start(), calls=%async_computation.14 | async-start | bytes 4456448 | tf_op jit(solution)/shard_map/all_gather | solution.py:355
  176.8 13.2 %collective-permute-start.3 = (f32[128,128]{1,0:T(8,128)}, f32[128,128]{1,0:T(8,128)S(1)}, u32[]{:S(2)}, u32[]{:S(2)}) collective-permute-start(f32[128,128]{1,0:T(8,128)} %get-tuple-element.71), channel_id=1, source_target_pairs={{0,0},{1,1},{2,2},{3,3},{4,32},{5,33},{6,34},{7,35},{8,64},{9,65},... | collective-permute-start | bytes 196616 | tf_op jit(solution)/shard_map/ppermute | solution.py:314
  178.3 11.7 %collective-permute-start.4 = (f32[128,128]{1,0:T(8,128)S(1)}, f32[128,128]{1,0:T(8,128)S(1)}, u32[]{:S(2)}, u32[]{:S(2)}) collective-permute-start(f32[128,128]{1,0:T(8,128)S(1)} %get-tuple-element.72), channel_id=1, source_target_pairs={{0,16},{1,17},{2,18},{3,19},{4,48},{5,49},{6,50},{7,51},{8,80},{9,... | collective-permute-start | bytes 196616 | tf_op jit(solution)/shard_map/ppermute | solution.py:314
  189.0 26.3 %copy-start.5 = (f32[4,128,384]{2,1,0:T(8,128)}, f32[4,128,384]{2,1,0:T(8,128)S(1)}, u32[]{:S(2)}) copy-start(f32[4,128,384]{2,1,0:T(8,128)S(1)} %collective-permute-done.10.refs_2_.refs_10_) | copy-start | bytes 2359300
  189.0 1.0 collective-permute-start.11
  189.7 1.5 collective-permute-start.12
  193.5 45.8 %all-to-all-start.7 = ((f32[16,256,128]{2,1,0:T(8,128)}), f32[16,256,128]{2,1,0:T(8,128)}, u32[]{:S(2)}, u32[]{:S(2)}) async-start(f32[16,256,128]{2,1,0:T(8,128)} %broadcast_in_dim.45), calls=%async_computation.7 | async-start | bytes 4194304 | tf_op jit(solution)/shard_map/all_to_all | solution.py:30
  209.3 6.2 %collective-permute-start.17 = (f32[4,128,384]{2,1,0:T(8,128)S(1)}, f32[4,128,384]{2,1,0:T(8,128)}, u32[]{:S(2)}, u32[]{:S(2)}) collective-permute-start(f32[4,128,384]{2,1,0:T(8,128)S(1)} %pad_maximum_fusion.2.refs_0_.refs_8_), channel_id=1, source_target_pairs={{0,16},{16,0},{1,17},{17,1},{2,18},{18,2},{3,19},{19,3},{4,20},{20... | collective-permute-start | bytes 2359304 | tf_op jit(solution)/shard_map/ppermute | solution.py:26
  209.4 21.8 %collective-permute-start.13 = (f32[4,128,256]{2,1,0:T(8,128)}, f32[4,128,256]{2,1,0:T(8,128)}, u32[]{:S(2)}, u32[]{:S(2)}) collective-permute-start(f32[4,128,256]{2,1,0:T(8,128)} %get-tuple-element.45.refs_0_), channel_id=1, source_target_pairs={{0,16},{16,0},{1,17},{17,1},{2,18},{18,2},{3,19},{19,3},{4,20},{20... | collective-permute-start | bytes 1572872 | tf_op jit(solution)/shard_map/ppermute | solution.py:26
  214.6 2.4 collective-permute-start.20
  214.8 5.6 %collective-permute-start.18 = (f32[4,128,384]{2,1,0:T(8,128)S(1)}, f32[4,128,384]{2,1,0:T(8,128)S(1)}, u32[]{:S(2)}, u32[]{:S(2)}) collective-permute-start(f32[4,128,384]{2,1,0:T(8,128)S(1)} %collective-permute-done.8.refs_1_.refs_9_), channel_id=1, source_target_pairs={{0,16},{16,0},{1,17},{17,1},{2,18},{18,2},{3,19},{19,3},{4,20},{20... | collective-permute-start | bytes 2359304 | tf_op jit(solution)/shard_map/ppermute | solution.py:26
  215.3 7.0 %collective-permute-start.19 = (f32[4,128,384]{2,1,0:T(8,128)S(1)}, f32[4,128,384]{2,1,0:T(8,128)}, u32[]{:S(2)}, u32[]{:S(2)}) collective-permute-start(f32[4,128,384]{2,1,0:T(8,128)S(1)} %collective-permute-done.10.refs_2_.refs_10_), channel_id=1, source_target_pairs={{0,16},{16,0},{1,17},{17,1},{2,18},{18,2},{3,19},{19,3},{4,20},{20... | collective-permute-start | bytes 2359304 | tf_op jit(solution)/shard_map/ppermute | solution.py:26
  215.5 15.7 %collective-permute-start.15 = (f32[4,128,256]{2,1,0:T(8,128)}, f32[4,128,256]{2,1,0:T(8,128)S(1)}, u32[]{:S(2)}, u32[]{:S(2)}) collective-permute-start(f32[4,128,256]{2,1,0:T(8,128)} %collective-permute-done.refs_2_), channel_id=1, source_target_pairs={{0,16},{16,0},{1,17},{17,1},{2,18},{18,2},{3,19},{19,3},{4,20},{20... | collective-permute-start | bytes 1572872 | tf_op jit(solution)/shard_map/ppermute | solution.py:26
  217.0 3.4 %copy-start.6 = (f32[4,128,384]{2,1,0:T(8,128)}, f32[4,128,384]{2,1,0:T(8,128)S(1)}, u32[]{:S(2)}) copy-start(f32[4,128,384]{2,1,0:T(8,128)S(1)} %collective-permute-done.20.refs_7_.refs_15_) | copy-start | bytes 2359300
  217.0 14.3 %collective-permute-start.16 = (f32[4,128,256]{2,1,0:T(8,128)}, f32[4,128,256]{2,1,0:T(8,128)S(1)}, u32[]{:S(2)}, u32[]{:S(2)}) collective-permute-start(f32[4,128,256]{2,1,0:T(8,128)} %collective-permute-done.2.refs_3_), channel_id=1, source_target_pairs={{0,16},{16,0},{1,17},{17,1},{2,18},{18,2},{3,19},{19,3},{4,20},{20... | collective-permute-start | bytes 1572872 | tf_op jit(solution)/shard_map/ppermute | solution.py:26
  220.4 0.9 copy-start.7
  221.3 10.0 %collective-permute-start.14 = (f32[4,128,256]{2,1,0:T(8,128)}, f32[4,128,256]{2,1,0:T(8,128)S(1)}, u32[]{:S(2)}, u32[]{:S(2)}) collective-permute-start(f32[4,128,256]{2,1,0:T(8,128)} %collective-permute-done.1.refs_1_), channel_id=1, source_target_pairs={{0,16},{16,0},{1,17},{17,1},{2,18},{18,2},{3,19},{19,3},{4,20},{20... | collective-permute-start | bytes 1572872 | tf_op jit(solution)/shard_map/ppermute | solution.py:26
  231.2 8.1 %copy-start.12 = (f32[4,128,256]{2,1,0:T(8,128)}, f32[4,128,256]{2,1,0:T(8,128)S(1)}, u32[]{:S(2)}) copy-start(f32[4,128,256]{2,1,0:T(8,128)S(1)} %collective-permute-done.15.refs_6_) | copy-start | bytes 1572868
  231.2 8.1 %copy-start.13 = (f32[4,128,256]{2,1,0:T(8,128)}, f32[4,128,256]{2,1,0:T(8,128)S(1)}, u32[]{:S(2)}) copy-start(f32[4,128,256]{2,1,0:T(8,128)S(1)} %collective-permute-done.16.refs_7_) | copy-start | bytes 1572868
  231.3 8.0 %copy-start.14 = (f32[4,128,256]{2,1,0:T(8,128)}, f32[4,128,256]{2,1,0:T(8,128)S(1)}, u32[]{:S(2)}) copy-start(f32[4,128,256]{2,1,0:T(8,128)S(1)} %collective-permute-done.14.refs_5_) | copy-start | bytes 1572868
  291.7 1.6 collective-permute-start.21
Sparse Core Ops, SparseCore 0:
  10.3 35.2 all-gather.13
  47.3 32.5 all-gather.9
  81.6 32.0 all-gather.7
  126.1 30.1 all-gather.11
  192.1 99.2 all-gather.15
